TPU v7x, 32 devices: a whole 2x2x4 slice. The times are simulated.
32 devices in a mesh: dp: 8 (over y, x, core), seq: 4 (over z).
Axes of the slice: x: 2, y: 2, z: 4, core: 2. Of those that a mesh axis runs over, the one named last changes fastest.
Arguments:
- hidden_in: bfloat16 [8, 1024, 1536], P('dp', 'seq'), may hold values from -6 to 6
- segment_ids: int32 [8, 1024], P('dp'), may hold values from 0 to 8, as said below
- gain_attn: bfloat16 [1536], P(('dp', 'seq')), may hold values from 0.5 to 1.5
- w_query: bfloat16 [1536, 768], P(('dp', 'seq')), may hold values from -0.0625 to 0.0625
- w_key: bfloat16 [1536, 768], P(('dp', 'seq')), may hold values from -0.0625 to 0.0625
- w_value: bfloat16 [1536, 768], P(('dp', 'seq')), may hold values from -0.15625 to 0.15625
- w_out: bfloat16 [768, 1536], P(None, ('dp', 'seq')), may hold values from -0.875 to 0.875
- rel_table: bfloat16 [32, 12], replicated, may hold values from -4 to 4
- gain_ff: bfloat16 [1536], P(('dp', 'seq')), may hold values from 0.5 to 1.5
- w_gate: bfloat16 [1536, 3968], P(('dp', 'seq')), may hold values from -0.15625 to 0.15625
- w_up: bfloat16 [1536, 3968], P(('dp', 'seq')), may hold values from -0.15625 to 0.15625
- w_down: bfloat16 [3968, 1536], P(None, ('dp', 'seq')), may hold values from -0.09375 to 0.09375
- cotangent: bfloat16 [8, 1024, 1536], P('dp', 'seq'), may hold values from -6 to 6
Outputs:
- block_out: float32 [8, 1024, 1536], P('dp', 'seq')
- grad_in: float32 [8, 1024, 1536], P('dp', 'seq')
- grad_gain_attn: float32 [1536], P(('dp', 'seq'))
- grad_w_query: float32 [1536, 768], P(('dp', 'seq'))
- grad_w_key: float32 [1536, 768], P(('dp', 'seq'))
- grad_w_value: float32 [1536, 768], P(('dp', 'seq'))
- grad_w_out: float32 [768, 1536], P(None, ('dp', 'seq'))
- grad_rel_table: float32 [32, 12], replicated
- grad_gain_ff: float32 [1536], P(('dp', 'seq'))
- grad_w_gate: float32 [1536, 3968], P(('dp', 'seq'))
- grad_w_up: float32 [1536, 3968], P(('dp', 'seq'))
- grad_w_down: float32 [3968, 1536], P(None, ('dp', 'seq'))
Inputs may be any that keep to these rules, and one draw needn't show every extreme that they name: `segment_ids`: along each row the documents are numbered from 1 upward and never fall, each document contiguous; 8 documents are begun in each row before a tail of at most 128 bytes is set to padding (0), so a document may be cut short or covered entirely by the padding.
All inputs are finite; a program needn't handle non-finite values.
Results may differ from a plain program's by a relative error of at most 0.018.
Values may be sent and summed in bfloat16 or wider, within the bound.
A program may use at most 256 MiB of HBM per device.

v0:
```python
import jax
import jax.numpy as jnp
from jax import lax
from jax.sharding import PartitionSpec as P

epsilon = 1e-06
far_bounds = (12, 16, 23, 32, 46, 64, 91)
highest = lax.Precision.HIGHEST


def bucket_table(offset):
    magnitude = jnp.abs(offset)
    distant = 8 + sum(((magnitude >= bound).astype(jnp.int32) for bound in far_bounds))
    signed_part = jnp.where(offset > 0, 16, 0).astype(jnp.int32)
    return signed_part + jnp.where(magnitude < 8, magnitude, distant)


def norm_scale(hidden):
    return lax.rsqrt(jnp.mean(hidden * hidden, axis=-1, keepdims=True) + epsilon)


def norm_backward(grad_normed, hidden, scale, gain):
    weighted = grad_normed * gain
    grad_gain = jnp.sum(grad_normed * hidden * scale, axis=0)
    grad_hidden = scale * weighted - hidden * (scale * scale * scale) * jnp.mean(
        weighted * hidden, axis=-1, keepdims=True
    )
    return (grad_hidden, grad_gain)


def scores_of(query_heads, key_heads, bias, allowed):
    raw_scores = jnp.einsum(
        "rqhd,rkhd->rhqk", query_heads, key_heads, preferred_element_type=jnp.float32
    )
    return jnp.where(allowed, raw_scores + bias[None], -1000000000.0)


def spread_sum(first, second, third):
    got = (
        lax.all_to_all(
            first.astype(jnp.bfloat16), "seq", split_axis=1, concat_axis=1, tiled=True
        ).astype(first.dtype),
        lax.all_to_all(
            second.astype(jnp.bfloat16), "seq", split_axis=1, concat_axis=1, tiled=True
        ).astype(second.dtype),
        lax.all_to_all(
            third.astype(jnp.bfloat16), "seq", split_axis=1, concat_axis=1, tiled=True
        ).astype(third.dtype),
    )
    half = tuple((jnp.sum(value, axis=1, keepdims=True) for value in got))
    got = (
        lax.all_to_all(
            half[0].astype(jnp.bfloat16), "dp", split_axis=0, concat_axis=0, tiled=True
        ).astype(jnp.float32),
        lax.all_to_all(
            half[1].astype(jnp.bfloat16), "dp", split_axis=0, concat_axis=0, tiled=True
        ).astype(jnp.float32),
        lax.all_to_all(
            half[2].astype(jnp.bfloat16), "dp", split_axis=0, concat_axis=0, tiled=True
        ).astype(jnp.float32),
    )
    return tuple((jnp.sum(value, axis=0, keepdims=True) for value in got))


def local(
    hidden_in,
    segment_ids,
    gain_attn,
    w_query,
    w_key,
    w_value,
    w_out,
    rel_table,
    gain_ff,
    w_gate,
    w_up,
    w_down,
    cotangent,
):
    row_count, local_len, model_width = hidden_in.shape
    row_length = segment_ids.shape[1]
    bucket_count, head_count = rel_table.shape
    token_count = row_count * local_len
    data_count = lax.axis_size("dp")
    piece_count = lax.axis_size("seq")
    shard_width = model_width // (data_count * piece_count)
    first_place = lax.axis_index("seq") * local_len
    query_place = first_place + jnp.arange(local_len, dtype=jnp.int32)
    key_place = jnp.arange(row_length, dtype=jnp.int32)
    buckets = bucket_table(key_place[None, :] - query_place[:, None])
    onehot = (buckets[:, :, None] == jnp.arange(bucket_count, dtype=jnp.int32)).astype(jnp.float32)
    bias = jnp.einsum("qkb,bh->hqk", onehot, rel_table.astype(jnp.float32), precision=highest)
    query_segs = lax.dynamic_slice_in_dim(segment_ids, first_place, local_len, 1)
    same_doc = query_segs[:, :, None] == segment_ids[:, None, :]
    visible = (segment_ids[:, None, :] > 0) | (query_place[:, None] == key_place[None, :])[None]
    allowed = (same_doc & visible)[:, None]
    query_full, key_full, value_full, out_full, gain_one = (
        lax.all_gather(w_query, ("dp", "seq"), axis=0, tiled=True),
        lax.all_gather(w_key, ("dp", "seq"), axis=0, tiled=True),
        lax.all_gather(w_value, ("dp", "seq"), axis=0, tiled=True),
        lax.all_gather(w_out, ("dp", "seq"), axis=1, tiled=True),
        lax.all_gather(gain_attn, ("dp", "seq"), axis=0, tiled=True),
    )
    gain_first = gain_one.astype(jnp.float32)
    residual_in = hidden_in.astype(jnp.float32).reshape(token_count, model_width)
    scale_first = norm_scale(residual_in)
    normed_first = (residual_in * scale_first * gain_first).astype(jnp.bfloat16)
    queries = jnp.dot(normed_first, query_full, preferred_element_type=jnp.float32).astype(
        jnp.bfloat16
    )
    keys_local = jnp.dot(normed_first, key_full, preferred_element_type=jnp.float32).astype(
        jnp.bfloat16
    )
    values_local = jnp.dot(normed_first, value_full, preferred_element_type=jnp.float32).astype(
        jnp.bfloat16
    )
    inner = queries.shape[1]
    head_size = inner // head_count
    keys_row, values_row = (
        lax.all_gather(keys_local.reshape(row_count, local_len, inner), "seq", axis=1, tiled=True),
        lax.all_gather(
            values_local.reshape(row_count, local_len, inner), "seq", axis=1, tiled=True
        ),
    )
    query_heads = queries.reshape(row_count, local_len, head_count, head_size)
    key_heads = keys_row.reshape(row_count, row_length, head_count, head_size)
    value_heads = values_row.reshape(row_count, row_length, head_count, head_size)
    logits = scores_of(query_heads, key_heads, bias, allowed)
    row_max = jnp.max(logits, axis=-1, keepdims=True)
    exp_scores = jnp.exp(logits - row_max)
    denominator = jnp.sum(exp_scores, axis=-1, keepdims=True)
    probs_low = (exp_scores / denominator).astype(jnp.bfloat16)
    log_total = row_max + jnp.log(denominator)
    mixed = (
        jnp.einsum("rhqk,rkhd->rqhd", probs_low, value_heads, preferred_element_type=jnp.float32)
        .astype(jnp.bfloat16)
        .reshape(token_count, inner)
    )
    middle = residual_in + jnp.dot(mixed, out_full, preferred_element_type=jnp.float32)
    gate_full, up_full, down_full, gain_two = (
        lax.all_gather(w_gate, ("dp", "seq"), axis=0, tiled=True),
        lax.all_gather(w_up, ("dp", "seq"), axis=0, tiled=True),
        lax.all_gather(w_down, ("dp", "seq"), axis=1, tiled=True),
        lax.all_gather(gain_ff, ("dp", "seq"), axis=0, tiled=True),
    )
    gain_second = gain_two.astype(jnp.float32)
    scale_second = norm_scale(middle)
    normed_second = (middle * scale_second * gain_second).astype(jnp.bfloat16)
    gate_pre = jnp.dot(normed_second, gate_full, preferred_element_type=jnp.float32)
    up_pre = jnp.dot(normed_second, up_full, preferred_element_type=jnp.float32)
    activated = jax.nn.gelu(gate_pre, approximate=True)
    hidden_mid = (activated * up_pre).astype(jnp.bfloat16)
    block_out = middle + jnp.dot(hidden_mid, down_full, preferred_element_type=jnp.float32)
    gate_full, up_full, down_full, gain_two = (
        lax.all_gather(w_gate, ("dp", "seq"), axis=0, tiled=True),
        lax.all_gather(w_up, ("dp", "seq"), axis=0, tiled=True),
        lax.all_gather(w_down, ("dp", "seq"), axis=1, tiled=True),
        lax.all_gather(gain_ff, ("dp", "seq"), axis=0, tiled=True),
    )
    gain_second = gain_two.astype(jnp.float32)
    ff_width = gate_full.shape[1]
    grad_out = cotangent.reshape(token_count, model_width)
    grad_out_split = grad_out.reshape(token_count, data_count, piece_count, shard_width)
    grad_down_parts = jnp.einsum(
        "tf,tabp->abfp", hidden_mid, grad_out_split, preferred_element_type=jnp.float32
    )
    grad_hidden = (
        jnp.einsum("td,fd->tf", grad_out, down_full, preferred_element_type=jnp.float32)
        .astype(jnp.bfloat16)
        .astype(jnp.float32)
    )
    gelu_value, gelu_pull = jax.vjp(lambda value: jax.nn.gelu(value, approximate=True), gate_pre)
    grad_gate = gelu_pull(grad_hidden * up_pre)[0].astype(jnp.bfloat16)
    grad_up = (grad_hidden * gelu_value).astype(jnp.bfloat16)
    grad_gate_up = jnp.concatenate([grad_gate, grad_up], axis=1)
    normed_second_split = normed_second.reshape(token_count, data_count, piece_count, shard_width)
    grad_gate_up_parts = jnp.einsum(
        "tabp,tf->abpf", normed_second_split, grad_gate_up, preferred_element_type=jnp.float32
    )
    grad_normed_second = jnp.einsum(
        "tf,df->td", grad_gate, gate_full, preferred_element_type=jnp.float32
    ) + jnp.einsum("tf,df->td", grad_up, up_full, preferred_element_type=jnp.float32)
    grad_middle_norm, grad_gain_two = norm_backward(
        grad_normed_second, middle, scale_second, gain_second
    )
    grad_middle = grad_out.astype(jnp.float32) + grad_middle_norm
    feed_done = spread_sum(
        grad_gate_up_parts,
        grad_down_parts,
        grad_gain_two.reshape(data_count, piece_count, shard_width),
    )
    gate_up_sum = feed_done[0].reshape(shard_width, 2 * ff_width)
    grad_gate_shard = gate_up_sum[:, :ff_width]
    grad_up_shard = gate_up_sum[:, ff_width:]
    grad_down_shard = feed_done[1].reshape(ff_width, shard_width)
    grad_gain_two_shard = feed_done[2].reshape(shard_width)
    query_full, key_full, value_full, out_full, gain_one = (
        lax.all_gather(w_query, ("dp", "seq"), axis=0, tiled=True),
        lax.all_gather(w_key, ("dp", "seq"), axis=0, tiled=True),
        lax.all_gather(w_value, ("dp", "seq"), axis=0, tiled=True),
        lax.all_gather(w_out, ("dp", "seq"), axis=1, tiled=True),
        lax.all_gather(gain_attn, ("dp", "seq"), axis=0, tiled=True),
    )
    gain_first = gain_one.astype(jnp.float32)
    grad_attended = grad_middle.astype(jnp.bfloat16)
    grad_attended_split = grad_attended.reshape(token_count, data_count, piece_count, shard_width)
    grad_wout_parts = jnp.einsum(
        "ti,tabp->abip", mixed, grad_attended_split, preferred_element_type=jnp.float32
    )
    grad_mixed = jnp.einsum(
        "td,id->ti", grad_attended, out_full, preferred_element_type=jnp.float32
    ).astype(jnp.bfloat16)
    grad_heads = grad_mixed.reshape(row_count, local_len, head_count, head_size)
    logits_again = scores_of(query_heads, key_heads, bias, allowed)
    probs_again = jnp.exp(logits_again - log_total)
    probs_again_low = probs_again.astype(jnp.bfloat16)
    grad_probs = jnp.einsum(
        "rqhd,rkhd->rhqk", grad_heads, value_heads, preferred_element_type=jnp.float32
    )
    row_dot = jnp.sum(probs_again * grad_probs, axis=-1, keepdims=True)
    grad_logits = (probs_again * (grad_probs - row_dot)).astype(jnp.bfloat16)
    grad_bias = jnp.sum(grad_logits.astype(jnp.float32), axis=0)
    grad_table = jnp.einsum("qkb,hqk->bh", onehot, grad_bias, precision=highest)
    grad_queries = (
        jnp.einsum("rhqk,rkhd->rqhd", grad_logits, key_heads, preferred_element_type=jnp.float32)
        .astype(jnp.bfloat16)
        .reshape(token_count, inner)
    )
    grad_keys_row = jnp.einsum(
        "rhqk,rqhd->rkhd", grad_logits, query_heads, preferred_element_type=jnp.float32
    )
    grad_values_row = jnp.einsum(
        "rhqk,rqhd->rkhd", probs_again_low, grad_heads, preferred_element_type=jnp.float32
    )
    grad_keys_part, grad_values_part = (
        lax.psum_scatter(
            grad_keys_row.astype(jnp.bfloat16), "seq", scatter_dimension=1, tiled=True
        ).astype(jnp.float32),
        lax.psum_scatter(
            grad_values_row.astype(jnp.bfloat16), "seq", scatter_dimension=1, tiled=True
        ).astype(jnp.float32),
    )
    grad_keys = grad_keys_part.astype(jnp.bfloat16).reshape(token_count, inner)
    grad_values = grad_values_part.astype(jnp.bfloat16).reshape(token_count, inner)
    grad_projected = jnp.concatenate([grad_queries, grad_keys, grad_values], axis=1)
    normed_first_split = normed_first.reshape(token_count, data_count, piece_count, shard_width)
    grad_projection_parts = jnp.einsum(
        "tabp,ti->abpi", normed_first_split, grad_projected, preferred_element_type=jnp.float32
    )
    grad_normed_first = jnp.einsum(
        "ti,di->td", grad_queries, query_full, preferred_element_type=jnp.float32
    )
    grad_normed_first = grad_normed_first + jnp.einsum(
        "ti,di->td", grad_keys, key_full, preferred_element_type=jnp.float32
    )
    grad_normed_first = grad_normed_first + jnp.einsum(
        "ti,di->td", grad_values, value_full, preferred_element_type=jnp.float32
    )
    grad_first, grad_gain_one = norm_backward(
        grad_normed_first, residual_in, scale_first, gain_first
    )
    grad_input = grad_middle + grad_first
    attn_done = spread_sum(
        grad_projection_parts,
        grad_wout_parts,
        grad_gain_one.reshape(data_count, piece_count, shard_width),
    )
    projection_sum = attn_done[0].reshape(shard_width, 3 * inner)
    grad_query_shard = projection_sum[:, :inner]
    grad_key_shard = projection_sum[:, inner : 2 * inner]
    grad_value_shard = projection_sum[:, 2 * inner :]
    grad_out_shard = attn_done[1].reshape(inner, shard_width)
    grad_gain_one_shard = attn_done[2].reshape(shard_width)
    table_total = lax.psum(grad_table, ("dp", "seq"))
    return (
        block_out.reshape(row_count, local_len, model_width),
        grad_input.reshape(row_count, local_len, model_width),
        grad_gain_one_shard,
        grad_query_shard,
        grad_key_shard,
        grad_value_shard,
        grad_out_shard,
        table_total,
        grad_gain_two_shard,
        grad_gate_shard,
        grad_up_shard,
        grad_down_shard,
    )


def solution(mesh):
    in_specs = (
        P("dp", "seq", None),
        P("dp", None),
        P(("dp", "seq")),
        P(("dp", "seq"), None),
        P(("dp", "seq"), None),
        P(("dp", "seq"), None),
        P(None, ("dp", "seq")),
        P(),
        P(("dp", "seq")),
        P(("dp", "seq"), None),
        P(("dp", "seq"), None),
        P(None, ("dp", "seq")),
        P("dp", "seq", None),
    )
    out_specs = (
        P("dp", "seq", None),
        P("dp", "seq", None),
        P(("dp", "seq")),
        P(("dp", "seq"), None),
        P(("dp", "seq"), None),
        P(("dp", "seq"), None),
        P(None, ("dp", "seq")),
        P(),
        P(("dp", "seq")),
        P(("dp", "seq"), None),
        P(("dp", "seq"), None),
        P(None, ("dp", "seq")),
    )
    return jax.shard_map(local, mesh=mesh, in_specs=in_specs, out_specs=out_specs, check_vma=False)
```

profile of v0, /device:TPU:0, one launch (start us, length us, event | category | flops | bytes accessed | tf_op | source)
XLA Modules:
  0.0 2017.4 jit_solution(7699970168122829194)
XLA Ops:
  11.2 42.1 %all-reduce.2 = (bf16[1536]{0:T(1024)(128)(2,1)S(1)}, bf16[1536]{0:T(1024)(128)(2,1)S(1)}) all-reduce(bf16[1536]{0:T(1024)(128)(2,1)S(1)} %dynamic-update-slice, bf16[1536]{0:T(1024)(128)(2,1)S(1)} %dynamic-update-slice.1), channel_id=1, replica_groups=mesh['dp'=8,'seq'=4] {'dp','seq'}, use_global_device_ids=true, to_apply=%add | all-reduce | flops 3072 | bytes 12288
  55.3 15.6 all-gather.12.cloned.1.call-done
  70.9 3.6 convolution_convert_fusion.8
  74.5 55.4 %all-gather.16.cloned.1.call-done = bf16[1536,768]{1,0:T(8,128)(2,1)} async-done(((bf16[48,768]{1,0:T(8,128)(2,1)}), bf16[1536,768]{1,0:T(8,128)(2,1)}) %all-gather.16.cloned.1.call-update) | async-done | bytes 2359312 | tf_op jit(solution)/shard_map/all_gather | solution.py:99
  130.0 3.3 convolution_convert_fusion.6
  137.7 8.5 fusion.1
  146.2 15.7 copy.88
  162.9 26.1 %all-gather.14.cloned.1.call-done = bf16[1536,768]{1,0:T(8,128)(2,1)} async-done(((bf16[48,768]{1,0:T(8,128)(2,1)}), bf16[1536,768]{1,0:T(8,128)(2,1)}) %all-gather.14.cloned.1.call-update) | async-done | bytes 2359312 | tf_op jit(solution)/shard_map/all_gather | solution.py:98
  191.7 35.3 %all-gather.26.cloned.1.call-done = bf16[1024,768]{1,0:T(8,128)(2,1)} async-done(((bf16[256,768]{1,0:T(8,128)(2,1)}), bf16[1024,768]{1,0:T(8,128)(2,1)}) %all-gather.26.cloned.1.call-update) | async-done | bytes 1572880 | tf_op jit(solution)/shard_map/all_gather | solution.py:121
  229.6 35.4 %all-gather.28.cloned.1.call-done = bf16[1024,768]{1,0:T(8,128)(2,1)} async-done(((bf16[256,768]{1,0:T(8,128)(2,1)}), bf16[1024,768]{1,0:T(8,128)(2,1)}) %all-gather.28.cloned.1.call-update) | async-done | bytes 1572880 | tf_op jit(solution)/shard_map/all_gather | solution.py:120
  266.7 6.1 fusion.71
  277.6 3.3 fusion.39
  280.9 42.9 %all-gather.18.cloned.1.call-done = bf16[768,1536]{0,1:T(8,128)(2,1)} async-done(((bf16[768,48]{0,1:T(8,128)(2,1)}), bf16[768,1536]{0,1:T(8,128)(2,1)}) %all-gather.18.cloned.1.call-update) | async-done | bytes 2359312 | tf_op jit(solution)/shard_map/all_gather | solution.py:101
  327.9 91.9 %all-gather.20.cloned.1.call-done = bf16[1536,3968]{1,0:T(8,128)(2,1)} async-done(((bf16[48,3968]{1,0:T(8,128)(2,1)}), bf16[1536,3968]{1,0:T(8,128)(2,1)}) %all-gather.20.cloned.1.call-update) | async-done | bytes 12189712 | tf_op jit(solution)/shard_map/all_gather | solution.py:141
  419.8 9.8 fusion.72
  429.6 85.5 %all-gather.22.cloned.1.call-done = bf16[1536,3968]{1,0:T(8,128)(2,1)} async-done(((bf16[48,3968]{1,0:T(8,128)(2,1)}), bf16[1536,3968]{1,0:T(8,128)(2,1)}) %all-gather.22.cloned.1.call-update) | async-done | bytes 12189712 | tf_op jit(solution)/shard_map/all_gather | solution.py:142
  515.1 10.0 fusion.73
  525.1 85.3 %all-gather.24.cloned.1.call-done = bf16[3968,1536]{0,1:T(8,128)(2,1)} async-done(((bf16[3968,48]{0,1:T(8,128)(2,1)}), bf16[3968,1536]{0,1:T(8,128)(2,1)}) %all-gather.24.cloned.1.call-update) | async-done | bytes 12189712 | tf_op jit(solution)/shard_map/all_gather | solution.py:143
  610.4 12.8 multiply_convert_fusion.1
  623.3 8.0 fusion.74
  631.3 7.4 multiply_reduce_fusion.1
  642.4 11.2 multiply_reduce_fusion
  655.5 6.7 multiply_convert_fusion
  667.2 8.0 fusion.36
  676.0 3.2 all-to-all-start.6
  679.2 5.0 convolution_convert_fusion.4
  687.2 13.7 reduce-scatter.3.cloned.1.call-done
  700.9 3.8 convolution_add_fusion.1
  704.7 32.8 %reduce-scatter.5.cloned.1.call-done = bf16[1,256,12,64]{1,3,2,0:T(8,128)(2,1)} async-done(((bf16[1,1024,12,64]{1,3,2,0:T(8,128)(2,1)}), bf16[1,256,12,64]{1,3,2,0:T(8,128)(2,1)}) %reduce-scatter.5.cloned.1.call-update) | async-done | bytes 393232 | tf_op jit(solution)/shard_map/reduce_scatter | solution.py:239
  737.5 5.1 fusion.34
  743.5 3.2 all-to-all-start
  747.3 4.9 all-to-all-done
  752.2 3.6 all-to-all-start.7
  756.6 3.9 all-to-all-done.7
  760.5 3.3 all-to-all-start.1
  768.3 3.8 all-to-all-start.4
  778.3 3.7 convolution_convert_fusion.1
  782.0 3.5 copy.96
  785.5 40.7 %all-to-all-done.4 = bf16[8,4,768,48]{2,3,0,1:T(8,128)(2,1)S(1)} async-done(((bf16[8,4,768,48]{2,3,0,1:T(8,128)(2,1)}), bf16[8,4,768,48]{2,3,0,1:T(8,128)(2,1)S(1)}, u32[]{:S(2)}, u32[]{:S(2)}) %all-to-all-start.4) | async-done | bytes 2359328 | tf_op jit(solution)/shard_map/all_to_all | solution.py:43
  826.1 5.5 all-to-all-start.2
  832.9 153.2 %all-to-all-done.2 = bf16[8,4,48,2304]{3,2,0,1:T(8,128)(2,1)} async-done(((bf16[8,4,48,2304]{3,2,0,1:T(8,128)(2,1)}), bf16[8,4,48,2304]{3,2,0,1:T(8,128)(2,1)}, u32[]{:S(2)}, u32[]{:S(2)}) %all-to-all-start.2) | async-done | bytes 7077920 | tf_op jit(solution)/shard_map/all_to_all | solution.py:40
  986.2 3.5 all-to-all-start.5
  989.7 13.3 fusion.57
  1003.0 5.8 reduce_sum.211
  1009.6 4.1 all-to-all-start.3
  1013.8 8.9 convert_bitcast_fusion
  1022.7 5.1 copy.108
  1027.8 9.1 all-to-all-done.3
  1038.1 6.6 all-to-all-start.10
  1045.0 13.5 convolution_convert_fusion
  1058.5 20.0 copy.106
  1078.5 228.2 %all-to-all-done.10 = bf16[8,4,3968,48]{2,3,0,1:T(8,128)(2,1)} async-done(((bf16[8,4,3968,48]{2,3,0,1:T(8,128)(2,1)}), bf16[8,4,3968,48]{2,3,0,1:T(8,128)(2,1)}, u32[]{:S(2)}, u32[]{:S(2)}) %all-to-all-start.10) | async-done | bytes 12189728 | tf_op jit(solution)/shard_map/all_to_all | solution.py:43
  1306.7 8.3 all-to-all-start.8
  1315.0 8.8 reduce_sum.220
  1323.8 516.5 %all-to-all-done.8 = bf16[8,4,48,7936]{3,2,0,1:T(8,128)(2,1)} async-done(((bf16[8,4,48,7936]{3,2,0,1:T(8,128)(2,1)}), bf16[8,4,48,7936]{3,2,0,1:T(8,128)(2,1)}, u32[]{:S(2)}, u32[]{:S(2)}) %all-to-all-start.8) | async-done | bytes 24379424 | tf_op jit(solution)/shard_map/all_to_all | solution.py:40
  1840.3 5.0 all-to-all-start.11
  1845.3 17.0 reduce_sum.218
  1862.2 20.0 all-to-all-done.11
  1882.2 5.0 all-to-all-start.9
  1887.3 12.2 copy.102
  1899.4 7.4 fusion.44
  1906.9 81.1 %psum.7 = f32[32,12]{0,1:T(8,128)} all-reduce(f32[32,12]{0,1:T(8,128)S(1)} %fusion.44), channel_id=1, replica_groups=mesh['dp'=8,'seq'=4] {'dp','seq'}, use_global_device_ids=true, to_apply=%region_16.17 | all-reduce | flops 384 | bytes 3072 | tf_op jit(solution)/shard_map/psum | solution.py:274
  1988.0 9.8 fusion.21
  2005.6 3.8 convert_reduce_fusion
  (177 shorter events, 66.5 us)
Async XLA Ops:
  7.2 130.5 %copy-start = (bf16[32,12]{0,1:T(8,128)(2,1)S(1)}, bf16[32,12]{0,1:T(8,128)(2,1)}, u32[]{:S(2)}) copy-start(bf16[32,12]{0,1:T(8,128)(2,1)} %param.20) | copy-start | bytes 2308
  7.2 63.7 %all-gather.12.cloned.1.call-start = ((), (), s32[]{:S(2)}) async-start(), calls=%async_computation.14 | async-start | bytes 2433024 | tf_op jit(solution)/shard_map/all_gather | solution.py:100
  7.9 122.0 %all-gather.16.cloned.1.call-start = ((), (), s32[]{:S(2)}) async-start(), calls=%async_computation.16 | async-start | bytes 2433024 | tf_op jit(solution)/shard_map/all_gather | solution.py:99
  8.7 180.3 %all-gather.14.cloned.1.call-start = ((), (), s32[]{:S(2)}) async-start(), calls=%async_computation.15 | async-start | bytes 2433024 | tf_op jit(solution)/shard_map/all_gather | solution.py:98
  9.4 217.6 %all-gather.26.cloned.1.call-start = ((), (), s32[]{:S(2)}) async-start(), calls=%async_computation.23 | async-start | bytes 1966080 | tf_op jit(solution)/shard_map/all_gather | solution.py:121
  55.3 133.7 %copy-start.36 = (f32[256]{0:T(256)}, f32[256]{0:T(256)S(1)}, u32[]{:S(2)}) copy-start(f32[256]{0:T(256)S(1)} %get-tuple-element.29) | copy-start | bytes 3076
  70.9 59.1 %copy-start.4 = (bf16[1,256,1536]{2,1,0:T(8,128)(2,1)S(1)}, bf16[1,256,1536]{2,1,0:T(8,128)(2,1)}, u32[]{:S(2)}) copy-start(bf16[1,256,1536]{2,1,0:T(8,128)(2,1)} %param.13) | copy-start | bytes 2359300
  74.5 190.5 %all-gather.28.cloned.1.call-start = ((), (), s32[]{:S(2)}) async-start(), calls=%async_computation.24 | async-start | bytes 1966080 | tf_op jit(solution)/shard_map/all_gather | solution.py:120
  133.2 190.6 %all-gather.18.cloned.1.call-start = ((), (), s32[]{:S(2)}) async-start(), calls=%async_computation.17 | async-start | bytes 2433024 | tf_op jit(solution)/shard_map/all_gather | solution.py:101
  133.8 286.0 %all-gather.20.cloned.1.call-start = ((), (), s32[]{:S(2)}) async-start(), calls=%async_computation.18 | async-start | bytes 12570624 | tf_op jit(solution)/shard_map/all_gather | solution.py:141
  134.6 380.5 %all-gather.22.cloned.1.call-start = ((), (), s32[]{:S(2)}) async-start(), calls=%async_computation.19 | async-start | bytes 12570624 | tf_op jit(solution)/shard_map/all_gather | solution.py:142
  135.3 475.1 %all-gather.24.cloned.1.call-start = ((), (), s32[]{:S(2)}) async-start(), calls=%async_computation.20 | async-start | bytes 12570624 | tf_op jit(solution)/shard_map/all_gather | solution.py:143
  136.0 564.9 %reduce-scatter.3.cloned.1.call-start = ((), (), s32[]{:S(2)}) async-start(), calls=%async_computation.21 | async-start | bytes 1966080 | tf_op jit(solution)/shard_map/reduce_scatter | solution.py:236
  137.7 8.5 copy-start.10
  146.2 16.3 copy-start.31
  272.8 4.8 copy-start.2
  272.8 4.8 copy-start.12
  280.9 45.6 %copy-start.25 = (bf16[12,64,256]{2,1,0:T(8,128)(2,1)}, bf16[12,64,256]{2,1,0:T(8,128)(2,1)S(1)}, u32[]{:S(2)}) copy-start(bf16[12,64,256]{2,1,0:T(8,128)(2,1)S(1)} %fusion.39) | copy-start | bytes 1179652
  323.8 3.9 copy-start.28
  327.9 91.9 %copy-start.17 = (bf16[256,1536]{1,0:T(8,128)(2,1)}, bf16[256,1536]{1,0:T(8,128)(2,1)S(1)}, u32[]{:S(2)}) copy-start(bf16[256,1536]{1,0:T(8,128)(2,1)S(1)} %multiply_convert_fusion.4) | copy-start | bytes 2359300
  429.6 180.8 %copy-start.15 = (bf16[1,256,1536]{2,1,0:T(8,128)(2,1)S(1)}, bf16[1,256,1536]{2,1,0:T(8,128)(2,1)}, u32[]{:S(2)}) copy-start(bf16[1,256,1536]{2,1,0:T(8,128)(2,1)} %param.25) | copy-start | bytes 2359300
  623.2 8.0 copy-start.24
  623.3 8.0 copy-start.23
  623.3 8.0 copy-start.6
  623.3 8.0 copy-start.29
  631.3 7.5 copy-start.38
  638.7 2.7 copy-start.22
  642.4 11.3 slice-start
  642.4 11.3 slice-start.1
  642.4 13.1 slice-start.2
  642.4 13.1 copy-start.27
  662.2 2.6 copy-start.3
  667.1 8.1 copy-start.39
  667.1 70.4 %reduce-scatter.5.cloned.1.call-start = ((), (), s32[]{:S(2)}) async-start(), calls=%async_computation.22 | async-start | bytes 1966080 | tf_op jit(solution)/shard_map/reduce_scatter | solution.py:239
  676.0 10.5 all-to-all-start.6
  679.2 5.0 copy-start.19
  737.5 9.2 copy-start.30
  737.5 26.2 %copy-start.26 = (bf16[12,64,256]{2,1,0:T(8,128)(2,1)S(1)}, bf16[12,64,256]{2,1,0:T(8,128)(2,1)}, u32[]{:S(2)}) copy-start(bf16[12,64,256]{2,1,0:T(8,128)(2,1)} %copy-done.25) | copy-start | bytes 1179652
  743.5 8.8 all-to-all-start
  752.2 8.2 all-to-all-start.7
  760.5 5.7 copy-start.32
  760.5 7.8 all-to-all-start.1
  768.3 5.3 copy-start.34
  768.3 57.8 %all-to-all-start.4 = ((bf16[8,4,768,48]{2,3,0,1:T(8,128)(2,1)}), bf16[8,4,768,48]{2,3,0,1:T(8,128)(2,1)S(1)}, u32[]{:S(2)}, u32[]{:S(2)}) async-start(bf16[8,4,768,48]{2,3,0,1:T(8,128)(2,1)} %copy.99), calls=%async_computation.6 | async-start | bytes 4718592 | tf_op jit(solution)/shard_map/all_to_all | solution.py:43
  774.3 4.0 copy-start.37
  826.1 160.0 %all-to-all-start.2 = ((bf16[8,4,48,2304]{3,2,0,1:T(8,128)(2,1)}), bf16[8,4,48,2304]{3,2,0,1:T(8,128)(2,1)}, u32[]{:S(2)}, u32[]{:S(2)}) async-start(bf16[8,4,48,2304]{3,2,0,1:T(8,128)(2,1)} %copy.96), calls=%async_computation.4 | async-start | bytes 14155776 | tf_op jit(solution)/shard_map/all_to_all | solution.py:40
  986.2 22.7 %all-to-all-start.5 = ((bf16[8,1,768,48]{2,3,1,0:T(8,128)(2,1)}), bf16[8,1,768,48]{2,3,1,0:T(8,128)(2,1)S(1)}, u32[]{:S(2)}, u32[]{:S(2)}) async-start(bf16[8,1,768,48]{2,3,1,0:T(8,128)(2,1)} %bitcast.180), calls=%async_computation.7 | async-start | bytes 1179648 | tf_op jit(solution)/shard_map/all_to_all | solution.py:55
  1009.6 27.3 %all-to-all-start.3 = ((bf16[8,1,48,2304]{3,2,1,0:T(8,128)(2,1)}), bf16[8,1,48,2304]{3,2,1,0:T(8,128)(2,1)S(1)}, u32[]{:S(2)}, u32[]{:S(2)}) async-start(bf16[8,1,48,2304]{3,2,1,0:T(8,128)(2,1)} %bitcast.168), calls=%async_computation.5 | async-start | bytes 3538944 | tf_op jit(solution)/shard_map/all_to_all | solution.py:52
  1027.8 16.9 copy-start.18
  1038.1 268.6 %all-to-all-start.10 = ((bf16[8,4,3968,48]{2,3,0,1:T(8,128)(2,1)}), bf16[8,4,3968,48]{2,3,0,1:T(8,128)(2,1)}, u32[]{:S(2)}, u32[]{:S(2)}) async-start(bf16[8,4,3968,48]{2,3,0,1:T(8,128)(2,1)} %copy.108), calls=%async_computation.12 | async-start | bytes 24379392 | tf_op jit(solution)/shard_map/all_to_all | solution.py:43
  1306.7 533.5 %all-to-all-start.8 = ((bf16[8,4,48,7936]{3,2,0,1:T(8,128)(2,1)}), bf16[8,4,48,7936]{3,2,0,1:T(8,128)(2,1)}, u32[]{:S(2)}, u32[]{:S(2)}) async-start(bf16[8,4,48,7936]{3,2,0,1:T(8,128)(2,1)} %copy.106), calls=%async_computation.10 | async-start | bytes 48758784 | tf_op jit(solution)/shard_map/all_to_all | solution.py:40
  1840.3 41.9 %all-to-all-start.11 = ((bf16[8,1,3968,48]{2,3,1,0:T(8,128)(2,1)}), bf16[8,1,3968,48]{2,3,1,0:T(8,128)(2,1)}, u32[]{:S(2)}, u32[]{:S(2)}) async-start(bf16[8,1,3968,48]{2,3,1,0:T(8,128)(2,1)} %bitcast.167), calls=%async_computation.13 | async-start | bytes 6094848 | tf_op jit(solution)/shard_map/all_to_all | solution.py:55
  1882.2 123.4 %all-to-all-start.9 = ((bf16[8,1,48,7936]{3,2,1,0:T(8,128)(2,1)}), bf16[8,1,48,7936]{3,2,1,0:T(8,128)(2,1)}, u32[]{:S(2)}, u32[]{:S(2)}) async-start(bf16[8,1,48,7936]{3,2,1,0:T(8,128)(2,1)} %bitcast.164), calls=%async_computation.11 | async-start | bytes 12189696 | tf_op jit(solution)/shard_map/all_to_all | solution.py:52
  1887.2 12.2 copy-start.11
  1899.4 88.6 %copy-start.7 = (f32[256,1536]{1,0:T(8,128)S(1)}, f32[256,1536]{1,0:T(8,128)}, u32[]{:S(2)}) copy-start(f32[256,1536]{1,0:T(8,128)} %copy-done.5) | copy-start | bytes 4718596
  1988.0 9.9 copy-start.33
  1988.0 10.4 copy-start.41
  1988.0 10.4 copy-start.13
  1988.0 10.4 copy-start.14
  1988.0 10.4 copy-start.40
  1998.4 1.6 copy-start.35
  1998.4 2.2 copy-start.21
  1998.4 2.9 copy-start.9
  2005.6 5.0 copy-start.1
  (4 other events, 4.2 us)
Sparse Core Ops, SparseCore 0:
  10.8 60.0 all-gather.11
  73.7 56.2 all-gather.15
  132.8 56.2 all-gather.13
  191.0 35.9 all-gather.25
  229.0 35.9 all-gather.27
  267.7 56.1 all-gather.17
  326.6 93.0 all-gather.19
  422.6 92.4 all-gather.21
  517.9 92.4 all-gather.23
  667.2 33.6 reduce-scatter.2
  703.2 34.2 reduce-scatter.4
where the time goes:
time: 2020 us
  waiting for transfers between devices  1500 us (74%)
  matrix products  164 us (8%)
  blocking collectives  123 us (6%)
  local copies, waits for them, and re-layouts  87.5 us (4%)
  other arithmetic  69.1 us (3%)
  starting transfers between devices  55.9 us (3%)
    all_to_all x2, waiting for transfers between devices, spread_sum(): lax.all_to_all(first.astype(jnp.bfloat16), 'seq', split_axis=1, concat_ax...  670 us
    all_to_all x2, waiting for transfers between devices, spread_sum(): lax.all_to_all(second.astype(jnp.bfloat16), 'seq', split_axis=1, concat_a...  269 us
    all_gather x1, waiting for transfers between devices, local(): lax.all_gather(w_gate, ('dp', 'seq'), axis=0, tiled=True)  91.9 us
    all_gather x1, waiting for transfers between devices, local(): lax.all_gather(w_up, ('dp', 'seq'), axis=0, tiled=True)  85.5 us
    all_gather x1, waiting for transfers between devices, local(): lax.all_gather(w_down, ('dp', 'seq'), axis=1, tiled=True)  85.3 us
    psum x1, blocking collectives, local(): table_total = lax.psum(grad_table, ('dp', 'seq'))  81.1 us
    all_gather x1, waiting for transfers between devices, local(): lax.all_gather(w_key, ('dp', 'seq'), axis=0, tiled=True)  55.4 us
    all_gather x1, waiting for transfers between devices, local(): lax.all_gather(w_out, ('dp', 'seq'), axis=1, tiled=True)  42.9 us
  transfers between devices with their start and end apart: 23, of which 20 were waited for; matrix products, arithmetic and copies ran while one was open for 12% of the time, Pallas kernels for 0%

commit v1 on v0

--- a/solution.py
+++ b/solution.py
@@ -35,31 +35,17 @@
     return jnp.where(allowed, raw_scores + bias[None], -1000000000.0)
 
 
-def spread_sum(first, second, third):
-    got = (
-        lax.all_to_all(
-            first.astype(jnp.bfloat16), "seq", split_axis=1, concat_axis=1, tiled=True
-        ).astype(first.dtype),
-        lax.all_to_all(
-            second.astype(jnp.bfloat16), "seq", split_axis=1, concat_axis=1, tiled=True
-        ).astype(second.dtype),
-        lax.all_to_all(
-            third.astype(jnp.bfloat16), "seq", split_axis=1, concat_axis=1, tiled=True
-        ).astype(third.dtype),
-    )
-    half = tuple((jnp.sum(value, axis=1, keepdims=True) for value in got))
-    got = (
-        lax.all_to_all(
-            half[0].astype(jnp.bfloat16), "dp", split_axis=0, concat_axis=0, tiled=True
-        ).astype(jnp.float32),
-        lax.all_to_all(
-            half[1].astype(jnp.bfloat16), "dp", split_axis=0, concat_axis=0, tiled=True
-        ).astype(jnp.float32),
-        lax.all_to_all(
-            half[2].astype(jnp.bfloat16), "dp", split_axis=0, concat_axis=0, tiled=True
-        ).astype(jnp.float32),
-    )
-    return tuple((jnp.sum(value, axis=0, keepdims=True) for value in got))
+def gather_rows(shard):
+    return lax.all_gather(shard, ("dp", "seq"), axis=0, tiled=True)
+
+
+def scatter_sum(parts):
+    data_count = lax.axis_size("dp")
+    piece_count = lax.axis_size("seq")
+    shard_width = parts.shape[0] // (data_count * piece_count)
+    split = parts.reshape(data_count, piece_count, shard_width, parts.shape[1])
+    half = lax.psum_scatter(split, "dp", scatter_dimension=0, tiled=True)
+    return lax.psum_scatter(half, "seq", scatter_dimension=1, tiled=True)[0, 0]
 
 
 def local(
@@ -94,13 +80,20 @@
     same_doc = query_segs[:, :, None] == segment_ids[:, None, :]
     visible = (segment_ids[:, None, :] > 0) | (query_place[:, None] == key_place[None, :])[None]
     allowed = (same_doc & visible)[:, None]
-    query_full, key_full, value_full, out_full, gain_one = (
-        lax.all_gather(w_query, ("dp", "seq"), axis=0, tiled=True),
-        lax.all_gather(w_key, ("dp", "seq"), axis=0, tiled=True),
-        lax.all_gather(w_value, ("dp", "seq"), axis=0, tiled=True),
-        lax.all_gather(w_out, ("dp", "seq"), axis=1, tiled=True),
-        lax.all_gather(gain_attn, ("dp", "seq"), axis=0, tiled=True),
-    )
+    inner = w_query.shape[1]
+    ff_width = w_gate.shape[1]
+    gains = jnp.pad(jnp.stack([gain_attn, gain_ff], axis=1), ((0, 0), (0, 126)))
+    attn_full = gather_rows(jnp.concatenate([w_query, w_key, w_value, w_out.T, gains], axis=1))
+    feed_full = gather_rows(jnp.concatenate([w_gate, w_up, w_down.T], axis=1))
+    query_full = attn_full[:, :inner]
+    key_full = attn_full[:, inner : 2 * inner]
+    value_full = attn_full[:, 2 * inner : 3 * inner]
+    out_full = attn_full[:, 3 * inner : 4 * inner].T
+    gain_one = attn_full[:, 4 * inner]
+    gain_two = attn_full[:, 4 * inner + 1]
+    gate_full = feed_full[:, :ff_width]
+    up_full = feed_full[:, ff_width : 2 * ff_width]
+    down_full = feed_full[:, 2 * ff_width :].T
     gain_first = gain_one.astype(jnp.float32)
     residual_in = hidden_in.astype(jnp.float32).reshape(token_count, model_width)
     scale_first = norm_scale(residual_in)
@@ -114,7 +107,6 @@
     values_local = jnp.dot(normed_first, value_full, preferred_element_type=jnp.float32).astype(
         jnp.bfloat16
     )
-    inner = queries.shape[1]
     head_size = inner // head_count
     keys_row, values_row = (
         lax.all_gather(keys_local.reshape(row_count, local_len, inner), "seq", axis=1, tiled=True),
@@ -137,12 +129,6 @@
         .reshape(token_count, inner)
     )
     middle = residual_in + jnp.dot(mixed, out_full, preferred_element_type=jnp.float32)
-    gate_full, up_full, down_full, gain_two = (
-        lax.all_gather(w_gate, ("dp", "seq"), axis=0, tiled=True),
-        lax.all_gather(w_up, ("dp", "seq"), axis=0, tiled=True),
-        lax.all_gather(w_down, ("dp", "seq"), axis=1, tiled=True),
-        lax.all_gather(gain_ff, ("dp", "seq"), axis=0, tiled=True),
-    )
     gain_second = gain_two.astype(jnp.float32)
     scale_second = norm_scale(middle)
     normed_second = (middle * scale_second * gain_second).astype(jnp.bfloat16)
@@ -151,19 +137,12 @@
     activated = jax.nn.gelu(gate_pre, approximate=True)
     hidden_mid = (activated * up_pre).astype(jnp.bfloat16)
     block_out = middle + jnp.dot(hidden_mid, down_full, preferred_element_type=jnp.float32)
-    gate_full, up_full, down_full, gain_two = (
-        lax.all_gather(w_gate, ("dp", "seq"), axis=0, tiled=True),
-        lax.all_gather(w_up, ("dp", "seq"), axis=0, tiled=True),
-        lax.all_gather(w_down, ("dp", "seq"), axis=1, tiled=True),
-        lax.all_gather(gain_ff, ("dp", "seq"), axis=0, tiled=True),
-    )
     gain_second = gain_two.astype(jnp.float32)
-    ff_width = gate_full.shape[1]
     grad_out = cotangent.reshape(token_count, model_width)
-    grad_out_split = grad_out.reshape(token_count, data_count, piece_count, shard_width)
     grad_down_parts = jnp.einsum(
-        "tf,tabp->abfp", hidden_mid, grad_out_split, preferred_element_type=jnp.float32
-    )
+        "tf,td->df", hidden_mid, grad_out, preferred_element_type=jnp.float32
+    ).astype(jnp.bfloat16)
+    down_sum = scatter_sum(grad_down_parts)
     grad_hidden = (
         jnp.einsum("td,fd->tf", grad_out, down_full, preferred_element_type=jnp.float32)
         .astype(jnp.bfloat16)
@@ -173,10 +152,10 @@
     grad_gate = gelu_pull(grad_hidden * up_pre)[0].astype(jnp.bfloat16)
     grad_up = (grad_hidden * gelu_value).astype(jnp.bfloat16)
     grad_gate_up = jnp.concatenate([grad_gate, grad_up], axis=1)
-    normed_second_split = normed_second.reshape(token_count, data_count, piece_count, shard_width)
     grad_gate_up_parts = jnp.einsum(
-        "tabp,tf->abpf", normed_second_split, grad_gate_up, preferred_element_type=jnp.float32
-    )
+        "td,tf->df", normed_second, grad_gate_up, preferred_element_type=jnp.float32
+    ).astype(jnp.bfloat16)
+    gate_up_sum = scatter_sum(grad_gate_up_parts)
     grad_normed_second = jnp.einsum(
         "tf,df->td", grad_gate, gate_full, preferred_element_type=jnp.float32
     ) + jnp.einsum("tf,df->td", grad_up, up_full, preferred_element_type=jnp.float32)
@@ -184,29 +163,13 @@
         grad_normed_second, middle, scale_second, gain_second
     )
     grad_middle = grad_out.astype(jnp.float32) + grad_middle_norm
-    feed_done = spread_sum(
-        grad_gate_up_parts,
-        grad_down_parts,
-        grad_gain_two.reshape(data_count, piece_count, shard_width),
-    )
-    gate_up_sum = feed_done[0].reshape(shard_width, 2 * ff_width)
-    grad_gate_shard = gate_up_sum[:, :ff_width]
-    grad_up_shard = gate_up_sum[:, ff_width:]
-    grad_down_shard = feed_done[1].reshape(ff_width, shard_width)
-    grad_gain_two_shard = feed_done[2].reshape(shard_width)
-    query_full, key_full, value_full, out_full, gain_one = (
-        lax.all_gather(w_query, ("dp", "seq"), axis=0, tiled=True),
-        lax.all_gather(w_key, ("dp", "seq"), axis=0, tiled=True),
-        lax.all_gather(w_value, ("dp", "seq"), axis=0, tiled=True),
-        lax.all_gather(w_out, ("dp", "seq"), axis=1, tiled=True),
-        lax.all_gather(gain_attn, ("dp", "seq"), axis=0, tiled=True),
-    )
-    gain_first = gain_one.astype(jnp.float32)
+    grad_gate_shard = gate_up_sum[:, :ff_width].astype(jnp.float32)
+    grad_up_shard = gate_up_sum[:, ff_width:].astype(jnp.float32)
+    grad_down_shard = down_sum.T.astype(jnp.float32)
     grad_attended = grad_middle.astype(jnp.bfloat16)
-    grad_attended_split = grad_attended.reshape(token_count, data_count, piece_count, shard_width)
     grad_wout_parts = jnp.einsum(
-        "ti,tabp->abip", mixed, grad_attended_split, preferred_element_type=jnp.float32
-    )
+        "ti,td->di", mixed, grad_attended, preferred_element_type=jnp.float32
+    ).astype(jnp.bfloat16)
     grad_mixed = jnp.einsum(
         "td,id->ti", grad_attended, out_full, preferred_element_type=jnp.float32
     ).astype(jnp.bfloat16)
@@ -243,10 +206,9 @@
     grad_keys = grad_keys_part.astype(jnp.bfloat16).reshape(token_count, inner)
     grad_values = grad_values_part.astype(jnp.bfloat16).reshape(token_count, inner)
     grad_projected = jnp.concatenate([grad_queries, grad_keys, grad_values], axis=1)
-    normed_first_split = normed_first.reshape(token_count, data_count, piece_count, shard_width)
     grad_projection_parts = jnp.einsum(
-        "tabp,ti->abpi", normed_first_split, grad_projected, preferred_element_type=jnp.float32
-    )
+        "td,ti->di", normed_first, grad_projected, preferred_element_type=jnp.float32
+    ).astype(jnp.bfloat16)
     grad_normed_first = jnp.einsum(
         "ti,di->td", grad_queries, query_full, preferred_element_type=jnp.float32
     )
@@ -260,18 +222,29 @@
         grad_normed_first, residual_in, scale_first, gain_first
     )
     grad_input = grad_middle + grad_first
-    attn_done = spread_sum(
-        grad_projection_parts,
-        grad_wout_parts,
-        grad_gain_one.reshape(data_count, piece_count, shard_width),
-    )
-    projection_sum = attn_done[0].reshape(shard_width, 3 * inner)
-    grad_query_shard = projection_sum[:, :inner]
-    grad_key_shard = projection_sum[:, inner : 2 * inner]
-    grad_value_shard = projection_sum[:, 2 * inner :]
-    grad_out_shard = attn_done[1].reshape(inner, shard_width)
-    grad_gain_one_shard = attn_done[2].reshape(shard_width)
-    table_total = lax.psum(grad_table, ("dp", "seq"))
+    device_count = data_count * piece_count
+    table_size = bucket_count * head_count
+    table_rows = -(-table_size // shard_width)
+    table_block = jnp.pad(grad_table.reshape(-1), (0, table_rows * shard_width - table_size))
+    table_block = jnp.broadcast_to(
+        table_block.reshape(1, table_rows, shard_width), (device_count, table_rows, shard_width)
+    )
+    gain_block = jnp.stack([grad_gain_one, grad_gain_two], axis=0)
+    gain_block = gain_block.reshape(2, device_count, shard_width).transpose(1, 0, 2)
+    extra = jnp.concatenate([table_block, gain_block], axis=1).transpose(0, 2, 1)
+    extra = extra.reshape(model_width, table_rows + 2)
+    extra = jnp.pad(extra, ((0, 0), (0, -(table_rows + 2) % 128))).astype(jnp.bfloat16)
+    attn_sum = scatter_sum(
+        jnp.concatenate([grad_projection_parts, grad_wout_parts, extra], axis=1)
+    ).astype(jnp.float32)
+    grad_query_shard = attn_sum[:, :inner]
+    grad_key_shard = attn_sum[:, inner : 2 * inner]
+    grad_value_shard = attn_sum[:, 2 * inner : 3 * inner]
+    grad_out_shard = attn_sum[:, 3 * inner : 4 * inner].T
+    table_total = attn_sum[:, 4 * inner : 4 * inner + table_rows].T.reshape(-1)[:table_size]
+    table_total = table_total.reshape(bucket_count, head_count)
+    grad_gain_one_shard = attn_sum[:, 4 * inner + table_rows]
+    grad_gain_two_shard = attn_sum[:, 4 * inner + table_rows + 1]
     return (
         block_out.reshape(row_count, local_len, model_width),
         grad_input.reshape(row_count, local_len, model_width),

time: 2020 us -> 1030 us (0.51)
  waiting for transfers between devices: 1500 us -> 754 us
  blocking collectives: 123 us -> 0 us
  starting transfers between devices: 55.9 us -> 0.67 us
  other arithmetic: 69.1 us -> 34.6 us
  local copies, waits for them, and re-layouts: 87.5 us -> 53.6 us
    all_to_all x12 -> x0, waiting for transfers between devices: 979 us -> none  [the longest x2 670 us: spread_sum(): lax.all_to_all(first.astype(jnp.bfloat16), 'seq', split_axis=1, concat_ax...]
    reduce_scatter x0 -> x6, waiting for transfers between devices: none -> 412 us  [the longest x3 301 us: scatter_sum(): half = lax.psum_scatter(split, 'dp', scatter_dimension=0, tiled=True)]
    all_gather x7 -> x2, waiting for transfers between devices: 403 us -> 275 us  [gather_rows(): return lax.all_gather(shard, ('dp', 'seq'), axis=0, tiled=True)]
    psum x1 -> x0, blocking collectives: 81.1 us -> none  [local(): table_total = lax.psum(grad_table, ('dp', 'seq'))]
    all_to_all x12 -> x0, starting transfers between devices: 55.3 us -> none  [the longest x2 13.7 us: spread_sum(): lax.all_to_all(first.astype(jnp.bfloat16), 'seq', split_axis=1, concat_ax...]
    unnamed x1 -> x0, blocking collectives: 42.1 us -> none
    reduce_sum x12 -> x0, other arithmetic: 41.9 us -> none  [the longest x6 32.9 us: spread_sum(): half = tuple((jnp.sum(value, axis=1, keepdims=True) for value in got))]
    convert_element_type x13 -> x0, local copies, waits for them, and re-layouts: 34.7 us -> none  [the longest x2 23.6 us: spread_sum(): first.astype(jnp.bfloat16)]
  transfers between devices with their start and end apart: 23 -> 12, of which waited for: 20 -> 11; matrix products, arithmetic and copies ran while one was open for 12% -> 14% of each run, Pallas kernels for 0% -> 0%
where the time goes in v1:
time: 1030 us; the launch traced here: 1020 us
  waiting for transfers between devices  754 us (73%)
  matrix products  165 us (16%)
  local copies, waits for them, and re-layouts  53.6 us (5%)
  other arithmetic  34.6 us (3%)
  between operations  14.9 us (1%)
    reduce_scatter x3, waiting for transfers between devices, scatter_sum(): half = lax.psum_scatter(split, 'dp', scatter_dimension=0, tiled=True)  301 us
    all_gather x2, waiting for transfers between devices, gather_rows(): return lax.all_gather(shard, ('dp', 'seq'), axis=0, tiled=True)  275 us
    reduce_scatter x3, waiting for transfers between devices, scatter_sum(): return lax.psum_scatter(half, 'seq', scatter_dimension=1, tiled=True)[0, 0]  111 us
    all_gather x1, waiting for transfers between devices, local(): lax.all_gather(keys_local.reshape(row_count, local_len, inner), 'seq', ax...  35.6 us
    reduce_scatter x1, waiting for transfers between devices, local(): lax.psum_scatter(grad_values_row.astype(jnp.bfloat16), 'seq', scatter_dim...  29.3 us
  transfers between devices with their start and end apart: 12, of which 11 were waited for; matrix products, arithmetic and copies ran while one was open for 14% of the time, Pallas kernels for 0%

profile of v1, /device:TPU:0, one launch (start us, length us, event | category | flops | bytes accessed | tf_op | source)
XLA Modules:
  0.0 1022.4 jit_solution(5752319633577023852)
XLA Ops:
  7.2 0.9 constant_dynamic-update-slice_fusion.2
  8.9 0.9 constant_dynamic-update-slice_fusion.1
  9.8 0.9 constant_dynamic-update-slice_fusion
  10.7 0.9 bitcast_dynamic-update-slice_fusion
  12.4 1.4 fusion.69
  14.3 84.6 %all-gather.7.cloned.1.call-done = bf16[1536,3200]{1,0:T(8,128)(2,1)} async-done(((bf16[48,3200]{1,0:T(8,128)(2,1)}), bf16[1536,3200]{1,0:T(8,128)(2,1)}) %all-gather.7.cloned.1.call-update) | async-done | bytes 9830416 | tf_op jit(solution)/shard_map/all_gather | solution.py:39
  99.0 2.2 convert_reduce_fusion
  101.2 3.6 fusion.83
  104.9 3.4 fusion.89
  108.3 1.1 pad_maximum_fusion
  109.7 1.1 fusion.103
  111.2 8.6 fusion.1
  119.8 15.8 %copy.61 = f32[256,1024,12]{1,0,2:T(8,128)} copy(f32[256,1024,12]{0,2,1:T(8,128)} %fusion.1) | data formatting | bytes 25165824 | tf_op jit(solution)/shard_map/qkb,bh->hqk/dot_general | solution.py:78
  135.9 2.5 fusion.86
  138.6 1.9 all-gather.11.cloned.1.call-done
  140.6 2.6 copy.57
  143.1 35.6 %all-gather.13.cloned.1.call-done = bf16[1024,768]{1,0:T(8,128)(2,1)} async-done(((bf16[256,768]{1,0:T(8,128)(2,1)}), bf16[1024,768]{1,0:T(8,128)(2,1)}) %all-gather.13.cloned.1.call-update) | async-done | bytes 1572880 | tf_op jit(solution)/shard_map/all_gather | solution.py:112
  178.7 1.7 copy.59
  180.4 6.1 fusion.126
  186.5 2.8 fusion.6
  189.4 2.7 copy-done.2
  192.1 3.3 fusion.95
  195.4 2.8 multiply_reduce_fusion.3
  199.6 189.9 %all-gather.9.cloned.1.call-done = bf16[1536,11904]{1,0:T(8,128)(2,1)} async-done(((bf16[48,11904]{1,0:T(8,128)(2,1)}), bf16[1536,11904]{1,0:T(8,128)(2,1)}) %all-gather.9.cloned.1.call-update) | async-done | bytes 36569104 | tf_op jit(solution)/shard_map/all_gather | solution.py:39
  389.6 7.1 fusion.31
  396.6 9.9 fusion.13
  406.5 11.5 %fusion.40 = (bf16[256,3968]{1,0:T(8,128)(2,1)S(1)}, bf16[256,3968]{1,0:T(8,128)(2,1)S(1)}, bf16[256,3968]{1,0:T(8,128)(2,1)}) fusion(f32[256,3968]{1,0:T(8,128)S(1)} %fusion.31, f32[256,3968]{1,0:T(8,128)} %fusion.13, bf16[256,1536]{1,0:T(8,128)(2,1)S(1)} %multiply_convert_fusion.3, bf16[1536,11904]{1,0:T(8,128)(2,1)} %all-gather.9.cloned.1.call-done), kind=kOutput, calls=%fused_computation.46 | convolution fusion | flops 3146973184 | bytes 27197440 | tf_op jit(solution)/shard_map/dot_general | solution.py:135
  418.1 8.0 fusion.11
  426.1 7.5 multiply_reduce_fusion.1
  434.1 3.2 fusion.92
  437.3 1.9 copy.63
  439.2 11.3 %multiply_reduce_fusion = (f32[12,256]{1,0:T(8,128)S(1)}, f32[12,256,1024]{2,1,0:T(8,128)}) fusion(f32[12,256,1024]{2,1,0:T(8,128)} %copy-done.2, f32[12,256]{1,0:T(8,128)} %log_add_fusion, bf16[256,12,64]{0,2,1:T(8,128)(2,1)} %bitcast.123, bf16[1024,12,64]{0,2,1:T(8,128)(2,1)} %bitcast.119), kind=kOutput, calls=%fused_computation.12 | convolution fusion | flops 412087296 | bytes 27156480 | tf_op jit(solution)/shard_map/rqhd,rkhd->rhqk/dot_general | solution.py:180
  450.5 1.9 slice-done.2
  452.4 6.4 multiply_convert_fusion
  458.9 2.7 copy-done.3
  461.6 2.4 fusion.79
  464.0 8.1 fusion.80
  472.2 12.0 %copy.65 = bf16[12,256,1024]{1,0,2:T(8,128)(2,1)} copy(bf16[12,256,1024]{2,1,0:T(8,128)(2,1)} %copy-done.3) | data formatting | bytes 12582912 | tf_op jit(solution)/shard_map/convert_element_type | solution.py:184
  484.9 7.5 fusion.102
  493.1 0.8 reshape.399
  493.9 2.2 convolution_convert_fusion.3
  496.1 4.9 convolution_convert_fusion.5
  501.0 3.7 fusion.59
  504.8 29.3 %reduce-scatter.11.cloned.1.call-done = bf16[1,256,12,64]{1,3,2,0:T(8,128)(2,1)} async-done(((bf16[1,1024,12,64]{1,3,2,0:T(8,128)(2,1)}), bf16[1,256,12,64]{1,3,2,0:T(8,128)(2,1)}) %reduce-scatter.11.cloned.1.call-update) | async-done | bytes 393232 | tf_op jit(solution)/shard_map/reduce_scatter | solution.py:202
  534.1 6.4 convolution_convert_fusion.2
  540.5 2.6 convolution_add_fusion.1
  543.1 3.9 fusion.78
  547.6 9.2 fusion.19
  556.8 1.1 copy-done.12
  557.8 9.6 convolution_convert_fusion.1
  567.5 1.2 copy-done.14
  568.8 15.0 %convolution_convert_fusion = bf16[1536,7936]{1,0:T(8,128)(2,1)} fusion(bf16[256,1536]{1,0:T(8,128)(2,1)S(1)} %copy-done.14, bf16[256,3968]{1,0:T(8,128)(2,1)} %copy-done.16, bf16[256,3968]{1,0:T(8,128)(2,1)} %copy-done.15), kind=kOutput, calls=%fused_computation.3 | convolution fusion | flops 6261440512 | bytes 29229056 | tf_op jit(solution)/shard_map/td,tf->df/dot_general | solution.py:155
  583.8 50.3 %reduce-scatter.13.cloned.1.call-done = bf16[1,4,48,3200]{3,2,1,0:T(8,128)(2,1)} async-done(((bf16[8,4,48,3200]{3,2,1,0:T(8,128)(2,1)}), bf16[1,4,48,3200]{3,2,1,0:T(8,128)(2,1)}) %reduce-scatter.13.cloned.1.call-update) | async-done | bytes 1228816 | tf_op jit(solution)/shard_map/reduce_scatter | solution.py:47
  634.2 93.8 %reduce-scatter.21.cloned.1.call-done = bf16[1,4,48,3968]{3,2,1,0:T(8,128)(2,1)} async-done(((bf16[8,4,48,3968]{3,2,1,0:T(8,128)(2,1)}), bf16[1,4,48,3968]{3,2,1,0:T(8,128)(2,1)}) %reduce-scatter.21.cloned.1.call-update) | async-done | bytes 1523728 | tf_op jit(solution)/shard_map/reduce_scatter | solution.py:47
  728.1 156.8 %reduce-scatter.17.cloned.1.call-done = bf16[1,4,48,7936]{3,2,1,0:T(8,128)(2,1)} async-done(((bf16[8,4,48,7936]{3,2,1,0:T(8,128)(2,1)}), bf16[1,4,48,7936]{3,2,1,0:T(8,128)(2,1)}) %reduce-scatter.17.cloned.1.call-update) | async-done | bytes 3047440 | tf_op jit(solution)/shard_map/reduce_scatter | solution.py:47
  885.0 10.2 fusion.50
  895.2 1.6 fusion.75
  896.8 20.5 %reduce-scatter.15.cloned.1.call-done = bf16[1,1,48,3200]{3,2,1,0:T(8,128)(2,1)} async-done(((bf16[1,4,48,3200]{3,2,1,0:T(8,128)(2,1)}), bf16[1,1,48,3200]{3,2,1,0:T(8,128)(2,1)}) %reduce-scatter.15.cloned.1.call-update) | async-done | bytes 307216 | tf_op jit(solution)/shard_map/reduce_scatter | solution.py:48
  917.2 1.0 bitcast_convert_fusion
  919.8 0.8 slice_bitcast_fusion
  920.6 32.6 %reduce-scatter.23.cloned.1.call-done = bf16[1,1,48,3968]{3,2,1,0:T(8,128)(2,1)} async-done(((bf16[1,4,48,3968]{3,2,1,0:T(8,128)(2,1)}), bf16[1,1,48,3968]{3,2,1,0:T(8,128)(2,1)}) %reduce-scatter.23.cloned.1.call-update) | async-done | bytes 380944 | tf_op jit(solution)/shard_map/reduce_scatter | solution.py:48
  953.2 1.9 convert_bitcast_fusion
  955.1 58.0 %reduce-scatter.19.cloned.1.call-done = bf16[1,1,48,7936]{3,2,1,0:T(8,128)(2,1)} async-done(((bf16[1,4,48,7936]{3,2,1,0:T(8,128)(2,1)}), bf16[1,1,48,7936]{3,2,1,0:T(8,128)(2,1)}) %reduce-scatter.19.cloned.1.call-update) | async-done | bytes 761872 | tf_op jit(solution)/shard_map/reduce_scatter | solution.py:48
  1013.0 2.3 slice_convert_fusion
  (125 shorter events, 9.3 us)
Async XLA Ops:
  7.2 104.0 %copy-start = (bf16[32,12]{0,1:T(8,128)(2,1)S(1)}, bf16[32,12]{0,1:T(8,128)(2,1)}, u32[]{:S(2)}) copy-start(bf16[32,12]{0,1:T(8,128)(2,1)} %param.20) | copy-start | bytes 2308
  7.2 91.8 %all-gather.7.cloned.1.call-start = ((), (), s32[]{:S(2)}) async-start(), calls=%async_computation.8 | async-start | bytes 10137600 | tf_op jit(solution)/shard_map/all_gather | solution.py:39
  11.6 0.7 copy-start.20
  12.3 128.2 %all-gather.11.cloned.1.call-start = ((), (), s32[]{:S(2)}) async-start(), calls=%async_computation.18 | async-start | bytes 1966080 | tf_op jit(solution)/shard_map/all_gather | solution.py:113
  101.2 3.7 copy-start.4
  104.8 3.5 copy-start.24
  104.8 3.5 copy-start.25
  104.8 3.5 copy-start.26
  104.8 73.9 %all-gather.13.cloned.1.call-start = ((), (), s32[]{:S(2)}) async-start(), calls=%async_computation.19 | async-start | bytes 1966080 | tf_op jit(solution)/shard_map/all_gather | solution.py:112
  108.2 281.3 %all-gather.9.cloned.1.call-start = ((), (), s32[]{:S(2)}) async-start(), calls=%async_computation.9 | async-start | bytes 37711872 | tf_op jit(solution)/shard_map/all_gather | solution.py:39
  109.5 395.3 %reduce-scatter.9.cloned.1.call-start = ((), (), s32[]{:S(2)}) async-start(), calls=%async_computation.10 | async-start | bytes 1966080 | tf_op jit(solution)/shard_map/reduce_scatter | solution.py:199
  111.2 8.6 copy-start.6
  119.8 15.8 %copy-start.31 = (s32[1,1024]{1,0:T(1,128)S(1)}, s32[1,1024]{1,0:T(1,128)}, u32[]{:S(2)}) copy-start(s32[1,1024]{1,0:T(1,128)} %param.14) | copy-start | bytes 12292
  186.5 5.6 copy-start.2
  186.5 5.6 copy-start.7
  195.4 4.0 copy-start.22
  195.4 4.0 copy-start.28
  195.4 194.2 %copy-start.10 = (bf16[1,256,1536]{2,1,0:T(8,128)(2,1)S(1)}, bf16[1,256,1536]{2,1,0:T(8,128)(2,1)}, u32[]{:S(2)}) copy-start(bf16[1,256,1536]{2,1,0:T(8,128)(2,1)} %param.25) | copy-start | bytes 2359300
  198.2 1.2 copy-start.8
  199.6 206.9 %copy-start.13 = (bf16[256,1536]{1,0:T(8,128)(2,1)}, bf16[256,1536]{1,0:T(8,128)(2,1)S(1)}, u32[]{:S(2)}) copy-start(bf16[256,1536]{1,0:T(8,128)(2,1)S(1)} %multiply_convert_fusion.3) | copy-start | bytes 2359300
  418.0 8.0 copy-start.16
  418.0 8.0 copy-start.15
  418.1 8.0 copy-start.9
  418.1 8.0 copy-start.29
  426.1 7.5 copy-start.11
  426.1 7.5 copy-start.34
  439.2 11.3 %slice-start = ((s8[12582912]{0:T(1024)(128)(4,1)}), s8[4194304]{0:T(1024)(128)(4,1)S(1)}, s32[]{:S(2)}) async-start(s8[12582912]{0:T(1024)(128)(4,1)} %bitcast.112), calls=%async_computation.20 | async-start | bytes 8388608
  439.2 11.3 %slice-start.1 = ((s8[12582912]{0:T(1024)(128)(4,1)}), s8[4194304]{0:T(1024)(128)(4,1)S(1)}, s32[]{:S(2)}) async-start(s8[12582912]{0:T(1024)(128)(4,1)} %bitcast.112), calls=%async_computation.21 | async-start | bytes 8388608
  439.2 13.2 %slice-start.2 = ((s8[12582912]{0:T(1024)(128)(4,1)}), s8[4194304]{0:T(1024)(128)(4,1)S(1)}, s32[]{:S(2)}) async-start(s8[12582912]{0:T(1024)(128)(4,1)} %bitcast.112), calls=%async_computation.22 | async-start | bytes 8388608
  439.2 13.2 %copy-start.27 = (f32[12,256]{1,0:T(8,128)S(1)}, f32[12,256]{1,0:T(8,128)}, u32[]{:S(2)}) copy-start(f32[12,256]{1,0:T(8,128)} %log_add_fusion) | copy-start | bytes 36868
  458.9 2.7 copy-start.3
  464.0 70.1 %reduce-scatter.11.cloned.1.call-start = ((), (), s32[]{:S(2)}) async-start(), calls=%async_computation.11 | async-start | bytes 1966080 | tf_op jit(solution)/shard_map/reduce_scatter | solution.py:202
  472.1 12.1 %copy-start.32 = (bf16[1536]{0:T(1024)(128)(2,1)S(1)}, bf16[1536]{0:T(1024)(128)(2,1)}, u32[]{:S(2)}) copy-start(bf16[1536]{0:T(1024)(128)(2,1)} %get-tuple-element.38) | copy-start | bytes 9220
  472.1 162.0 %reduce-scatter.13.cloned.1.call-start = ((), (), s32[]{:S(2)}) async-start(), calls=%async_computation.12 | async-start | bytes 11059200 | tf_op jit(solution)/shard_map/reduce_scatter | solution.py:47
  484.9 9.0 copy-start.23
  501.0 33.1 %copy-start.5 = (bf16[1,256,1536]{2,1,0:T(8,128)(2,1)S(1)}, bf16[1,256,1536]{2,1,0:T(8,128)(2,1)}, u32[]{:S(2)}) copy-start(bf16[1,256,1536]{2,1,0:T(8,128)(2,1)} %param.13) | copy-start | bytes 2359300
  534.1 6.4 copy-start.17
  534.1 6.4 copy-start.19
  540.5 2.6 copy-start.21
  543.1 4.0 copy-start.30
  556.7 1.1 copy-start.12
  556.7 171.3 %reduce-scatter.21.cloned.1.call-start = ((), (), s32[]{:S(2)}) async-start(), calls=%async_computation.16 | async-start | bytes 13713408 | tf_op jit(solution)/shard_map/reduce_scatter | solution.py:47
  567.4 1.3 copy-start.14
  567.5 317.5 %reduce-scatter.17.cloned.1.call-start = ((), (), s32[]{:S(2)}) async-start(), calls=%async_computation.14 | async-start | bytes 27426816 | tf_op jit(solution)/shard_map/reduce_scatter | solution.py:47
  583.8 333.4 %reduce-scatter.15.cloned.1.call-start = ((), (), s32[]{:S(2)}) async-start(), calls=%async_computation.13 | async-start | bytes 1536000 | tf_op jit(solution)/shard_map/reduce_scatter | solution.py:48
  634.2 319.0 %reduce-scatter.23.cloned.1.call-start = ((), (), s32[]{:S(2)}) async-start(), calls=%async_computation.17 | async-start | bytes 1904640 | tf_op jit(solution)/shard_map/reduce_scatter | solution.py:48
  728.1 285.0 %reduce-scatter.19.cloned.1.call-start = ((), (), s32[]{:S(2)}) async-start(), calls=%async_computation.15 | async-start | bytes 3809280 | tf_op jit(solution)/shard_map/reduce_scatter | solution.py:48
  885.0 10.2 copy-start.18
  885.0 10.2 copy-start.33
  895.2 120.2 %copy-start.1 = (bf16[32,12]{0,1:T(8,128)(2,1)S(1)}, bf16[32,12]{0,1:T(8,128)(2,1)}, u32[]{:S(2)}) copy-start(bf16[32,12]{0,1:T(8,128)(2,1)} %param.20) | copy-start | bytes 2308
Sparse Core Ops, SparseCore 0:
  12.5 86.4 all-gather.6
  104.9 35.6 all-gather.10
  142.7 35.9 all-gather.12
  181.3 208.1 all-gather.8
  464.1 33.4 reduce-scatter.8
  499.8 34.2 reduce-scatter.10
  556.9 77.2 reduce-scatter.12
  637.7 90.2 reduce-scatter.20
  732.2 152.6 reduce-scatter.16
  887.1 30.0 reduce-scatter.14
  919.7 33.4 reduce-scatter.22
  955.3 57.6 reduce-scatter.18

commit v2 on v1

--- a/solution.py
+++ b/solution.py
@@ -1,11 +1,16 @@
+import functools
+
 import jax
 import jax.numpy as jnp
 from jax import lax
+from jax.experimental import pallas as pl
+from jax.experimental.pallas import tpu as pltpu
 from jax.sharding import PartitionSpec as P
 
 epsilon = 1e-06
 far_bounds = (12, 16, 23, 32, 46, 64, 91)
 highest = lax.Precision.HIGHEST
+mesh_ids = pl.DeviceIdType.MESH
 
 
 def bucket_table(offset):
@@ -46,6 +51,185 @@
     split = parts.reshape(data_count, piece_count, shard_width, parts.shape[1])
     half = lax.psum_scatter(split, "dp", scatter_dimension=0, tiled=True)
     return lax.psum_scatter(half, "seq", scatter_dimension=1, tiled=True)[0, 0]
+
+
+def plain_sums(pairs, extra):
+    found = []
+    for left, rights in pairs:
+        for right in rights:
+            part = jnp.einsum("td,tf->df", left, right, preferred_element_type=jnp.float32)
+            found.append(scatter_sum(part.astype(jnp.bfloat16)).astype(jnp.float32))
+    return found, scatter_sum(extra.astype(jnp.bfloat16)).astype(jnp.float32)
+
+
+def peers_of():
+    dp=lax.axis_index("dp"); z=lax.axis_index("seq")
+    c=lax.rem(dp,2); x=lax.rem(dp//2,2); y=dp//4
+    return dp,z,c,x,y
+
+def remote(src,dst,ss,rs,dev):
+    return pltpu.make_async_remote_copy(src_ref=src,dst_ref=dst,send_sem=ss,recv_sem=rs,device_id=dev,device_id_type=mesh_ids)
+
+part_slots=3
+def rs_kernel(chunks, lt_hbm, r_hbm, out, lt, r, p, *rest):
+    n=len(chunks)
+    ra1=rest[0:n]; rb1=rest[n:2*n]; ra2=rest[2*n:3*n]; rb2=rest[3*n:4*n]; rz=rest[4*n:5*n]; fin=rest[5*n]
+    lts,ltr,rss,rsr,ll,rl,s1,v1,s2,v2,s3,v3,s4,v4=rest[5*n+1:]
+    groups=lt_hbm.shape[0]
+    dp,z,c,x,y=peers_of()
+    sib=(dp+1-2*c,z); dx=(dp+2-4*x,z); dy=(lax.rem(dp+4,8),z)
+    zs=[lax.rem(z+k,4) for k in (1,2,3)]
+    dzs=[(dp,zz) for zz in zs]
+    bar=pltpu.get_barrier_semaphore()
+    for d in [sib,dx,dy]+dzs: pl.semaphore_signal(bar,inc=1,device_id=d,device_id_type=mesh_ids)
+    pl.semaphore_wait(bar,6)
+    order=[]
+    for g,off,w in chunks:
+        if g not in order: order.append(g)
+    ex={}
+    def exch_lt(g):
+        a=remote(lt_hbm.at[g],lt.at[c,g],lts.at[g],ltr.at[g],sib); a.start()
+        b=pltpu.make_async_copy(lt_hbm.at[g],lt.at[c,g],ll.at[g]); b.start()
+        ex[("l",g)]=(a,b)
+    def exch_r(t):
+        g,off,w=chunks[t]; s=pl.ds(off,w)
+        a=remote(r_hbm.at[1-c,:,s],r.at[c,:,s],rss.at[t],rsr.at[t],sib); a.start()
+        b=pltpu.make_async_copy(r_hbm.at[c,:,s],r.at[c,:,s],rl.at[t]); b.start()
+        ex[("r",t)]=(a,b)
+    seen=set()
+    for t,(g,off,w) in enumerate(chunks):
+        if g not in seen: seen.add(g); exch_lt(g)
+        exch_r(t)
+    def wait_lt(g):
+        remote(lt_hbm.at[g],lt.at[1-c,g],lts.at[g],ltr.at[g],sib).wait_recv(); ex[("l",g)][1].wait()
+    def wait_r(t):
+        g,off,w=chunks[t]; s=pl.ds(off,w)
+        remote(r_hbm.at[1-c,:,s],r.at[1-c,:,s],rss.at[t],rsr.at[t],sib).wait_recv(); ex[("r",t)][1].wait()
+    got=set(); c1={}; c2={}; c3={}; c4={}
+    def stage1(t):
+        g,off,w=chunks[t]; b=t%part_slots
+        if g not in got: got.add(g); wait_lt(g)
+        wait_r(t)
+        if t>=part_slots:
+            for d in c1[t-part_slots]: d.wait_send()
+        def body(i,_):
+            rows=pl.ds(pl.multiple_of(i*192,192),192)
+            acc=jnp.dot(lt[0,g,rows,:],r[0,:,off:off+w],preferred_element_type=jnp.float32)
+            acc=acc+jnp.dot(lt[1,g,rows,:],r[1,:,off:off+w],preferred_element_type=jnp.float32)
+            p[b,i//4,lax.rem(i//2,2),lax.rem(i,2),:,:,0:w]=acc.astype(jnp.bfloat16).reshape(4,48,w)
+            return 0
+        lax.fori_loop(0,8,body,0)
+        a=remote(p.at[b,:,1-x,0,:,:,pl.ds(0,w)],ra1[t],s1.at[t,0],v1.at[t,0],dx)
+        e=remote(p.at[b,1-y,:,1,:,:,pl.ds(0,w)],rb1[t],s1.at[t,1],v1.at[t,1],dy)
+        a.start(); e.start(); c1[t]=(a,e)
+    def stage2(t):
+        g,off,w=chunks[t]; b=t%part_slots
+        for d in c1[t]: d.wait_recv()
+        def body(i,_):
+            h=i//4; zz=lax.rem(i,4)
+            ra1[t][h,zz]=ra1[t][h,zz]+p[b,h,x,0,zz,:,0:w]
+            rb1[t][h,zz]=rb1[t][h,zz]+p[b,y,h,1,zz,:,0:w]
+            return 0
+        lax.fori_loop(0,8,body,0)
+        a=remote(ra1[t].at[1-y],ra2[t],s2.at[t,0],v2.at[t,0],dy)
+        e=remote(rb1[t].at[1-x],rb2[t],s2.at[t,1],v2.at[t,1],dx)
+        a.start(); e.start(); c2[t]=(a,e)
+    def stage3(t):
+        for d in c2[t]: d.wait_recv()
+        def body(zz,_):
+            ra2[t][zz]=ra2[t][zz]+ra1[t][y,zz]
+            rb2[t][zz]=rb2[t][zz]+rb1[t][x,zz]
+            return 0
+        lax.fori_loop(0,4,body,0)
+        cs=[]
+        for k in range(3):
+            cs.append(remote(ra2[t].at[zs[k]],rz[t].at[k,0],s3.at[t,k,0],v3.at[t,k,0],dzs[k]))
+            cs.append(remote(rb2[t].at[zs[k]],rz[t].at[k,1],s3.at[t,k,1],v3.at[t,k,1],dzs[k]))
+        for d in cs: d.start()
+        c3[t]=cs
+    def stage4(t):
+        g,off,w=chunks[t]
+        for d in c3[t]: d.wait_recv()
+        f0=ra2[t][z].astype(jnp.float32); f1=rb2[t][z].astype(jnp.float32)
+        for k in range(3):
+            f0=f0+rz[t][k,0].astype(jnp.float32); f1=f1+rz[t][k,1].astype(jnp.float32)
+        fin[0,:,off:off+w]=f0; fin[1,:,off:off+w]=f1
+        out[c,:,off:off+w]=fin[c,:,off:off+w]
+        a=remote(fin.at[1-c,:,pl.ds(off,w)],out.at[c,:,pl.ds(off,w)],s4.at[t],v4.at[t],sib)
+        a.start(); c4[t]=a
+    for t in range(n+3):
+        if t<n: stage1(t)
+        if 0<=t-1<n: stage2(t-1)
+        if 0<=t-2<n: stage3(t-2)
+        if 0<=t-3<n: stage4(t-3)
+    for t in range(n):
+        g,off,w=chunks[t]
+        remote(fin.at[1-c,:,pl.ds(off,w)],out.at[1-c,:,pl.ds(off,w)],s4.at[t],v4.at[t],sib).wait_recv()
+        c4[t].wait_send()
+        if t>=n-part_slots:
+            for d in c1[t]: d.wait_send()
+        for d in c2[t]: d.wait_send()
+        for d in c3[t]: d.wait_send()
+        ex[("r",t)][0].wait_send()
+    for g in order: ex[("l",g)][0].wait_send()
+
+def reduce_scatter(lt, r, chunks, cid=1):
+    n=len(chunks); G=lt.shape[0]; C=r.shape[2]; wm=max(w for _,_,w in chunks)
+    D=pltpu.SemaphoreType.DMA; bf=jnp.bfloat16
+    V=pltpu.VMEM
+    scratch=[V((2,)+lt.shape,bf),V(r.shape,bf),V((part_slots,2,2,2,4,48,wm),bf)]
+    scratch+=[V((2,4,48,w),bf) for _,_,w in chunks]*1
+    scratch+=[V((2,4,48,w),bf) for _,_,w in chunks]
+    scratch+=[V((4,48,w),bf) for _,_,w in chunks]
+    scratch+=[V((4,48,w),bf) for _,_,w in chunks]
+    scratch+=[V((3,2,48,w),bf) for _,_,w in chunks]
+    scratch+=[V((2,48,C),jnp.float32)]
+    scratch+=[D((G,)),D((G,)),D((n,)),D((n,)),D((G,)),D((n,)),D((n,2)),D((n,2)),D((n,2)),D((n,2)),D((n,3,2)),D((n,3,2)),D((n,)),D((n,))]
+    return pl.pallas_call(functools.partial(rs_kernel,chunks),
+        out_shape=jax.ShapeDtypeStruct((2,48,C),jnp.float32),
+        in_specs=[pl.BlockSpec(memory_space=pltpu.HBM)]*2,
+        out_specs=pl.BlockSpec(memory_space=pltpu.VMEM),
+        scratch_shapes=scratch,
+        compiler_params=pltpu.CompilerParams(collective_id=cid,has_side_effects=True,vmem_limit_bytes=60*2**20))(lt,r)
+
+
+def halves(values, width):
+    spare = 2 * width - values.shape[1]
+    padded = jnp.pad(values, ((0, 0), (0, spare)))
+    return padded.reshape(values.shape[0], 2, width).transpose(1, 0, 2)
+
+
+def join_halves(summed, start, width, total):
+    piece = summed[:, :, start : start + width]
+    return piece.transpose(1, 0, 2).reshape(piece.shape[1], 2 * width)[:, :total]
+
+
+def kernel_sums(pairs, extra):
+    low = jnp.bfloat16
+    chunks = []
+    pieces = []
+    places = []
+    start = 0
+    for group, (left, rights) in enumerate(pairs):
+        for right in rights:
+            width = -(-right.shape[1] // 256) * 128
+            step = 512 if width % 512 == 0 else 384
+            assert width % step == 0
+            for offset in range(0, width, step):
+                chunks.append((group, start + offset, step))
+            pieces.append(halves(right.astype(low), width))
+            places.append((start, width, right.shape[1]))
+            start += width
+    upper = extra.astype(low)
+    lower = (extra - upper.astype(jnp.float32)).astype(low)
+    chunks.append((len(pairs), start, 128))
+    token_count = pairs[0][0].shape[0]
+    pieces.append(jnp.eye(token_count, dtype=low).reshape(2, 128, token_count).transpose(0, 2, 1))
+    lefts = [left.astype(low).T for left, rights in pairs]
+    lefts.append(jnp.concatenate([upper, lower], axis=1))
+    summed = reduce_scatter(jnp.stack(lefts), jnp.concatenate(pieces, axis=2), chunks)
+    found = [join_halves(summed, *place) for place in places]
+    return found, summed[0, :, start:] + summed[1, :, start:]
 
 
 def local(
@@ -139,10 +323,6 @@
     block_out = middle + jnp.dot(hidden_mid, down_full, preferred_element_type=jnp.float32)
     gain_second = gain_two.astype(jnp.float32)
     grad_out = cotangent.reshape(token_count, model_width)
-    grad_down_parts = jnp.einsum(
-        "tf,td->df", hidden_mid, grad_out, preferred_element_type=jnp.float32
-    ).astype(jnp.bfloat16)
-    down_sum = scatter_sum(grad_down_parts)
     grad_hidden = (
         jnp.einsum("td,fd->tf", grad_out, down_full, preferred_element_type=jnp.float32)
         .astype(jnp.bfloat16)
@@ -151,11 +331,6 @@
     gelu_value, gelu_pull = jax.vjp(lambda value: jax.nn.gelu(value, approximate=True), gate_pre)
     grad_gate = gelu_pull(grad_hidden * up_pre)[0].astype(jnp.bfloat16)
     grad_up = (grad_hidden * gelu_value).astype(jnp.bfloat16)
-    grad_gate_up = jnp.concatenate([grad_gate, grad_up], axis=1)
-    grad_gate_up_parts = jnp.einsum(
-        "td,tf->df", normed_second, grad_gate_up, preferred_element_type=jnp.float32
-    ).astype(jnp.bfloat16)
-    gate_up_sum = scatter_sum(grad_gate_up_parts)
     grad_normed_second = jnp.einsum(
         "tf,df->td", grad_gate, gate_full, preferred_element_type=jnp.float32
     ) + jnp.einsum("tf,df->td", grad_up, up_full, preferred_element_type=jnp.float32)
@@ -163,13 +338,7 @@
         grad_normed_second, middle, scale_second, gain_second
     )
     grad_middle = grad_out.astype(jnp.float32) + grad_middle_norm
-    grad_gate_shard = gate_up_sum[:, :ff_width].astype(jnp.float32)
-    grad_up_shard = gate_up_sum[:, ff_width:].astype(jnp.float32)
-    grad_down_shard = down_sum.T.astype(jnp.float32)
     grad_attended = grad_middle.astype(jnp.bfloat16)
-    grad_wout_parts = jnp.einsum(
-        "ti,td->di", mixed, grad_attended, preferred_element_type=jnp.float32
-    ).astype(jnp.bfloat16)
     grad_mixed = jnp.einsum(
         "td,id->ti", grad_attended, out_full, preferred_element_type=jnp.float32
     ).astype(jnp.bfloat16)
@@ -205,10 +374,6 @@
     )
     grad_keys = grad_keys_part.astype(jnp.bfloat16).reshape(token_count, inner)
     grad_values = grad_values_part.astype(jnp.bfloat16).reshape(token_count, inner)
-    grad_projected = jnp.concatenate([grad_queries, grad_keys, grad_values], axis=1)
-    grad_projection_parts = jnp.einsum(
-        "td,ti->di", normed_first, grad_projected, preferred_element_type=jnp.float32
-    ).astype(jnp.bfloat16)
     grad_normed_first = jnp.einsum(
         "ti,di->td", grad_queries, query_full, preferred_element_type=jnp.float32
     )
@@ -233,31 +398,34 @@
     gain_block = gain_block.reshape(2, device_count, shard_width).transpose(1, 0, 2)
     extra = jnp.concatenate([table_block, gain_block], axis=1).transpose(0, 2, 1)
     extra = extra.reshape(model_width, table_rows + 2)
-    extra = jnp.pad(extra, ((0, 0), (0, -(table_rows + 2) % 128))).astype(jnp.bfloat16)
-    attn_sum = scatter_sum(
-        jnp.concatenate([grad_projection_parts, grad_wout_parts, extra], axis=1)
-    ).astype(jnp.float32)
-    grad_query_shard = attn_sum[:, :inner]
-    grad_key_shard = attn_sum[:, inner : 2 * inner]
-    grad_value_shard = attn_sum[:, 2 * inner : 3 * inner]
-    grad_out_shard = attn_sum[:, 3 * inner : 4 * inner].T
-    table_total = attn_sum[:, 4 * inner : 4 * inner + table_rows].T.reshape(-1)[:table_size]
+    extra = jnp.pad(extra, ((0, 0), (0, -(table_rows + 2) % 128)))
+    pairs = (
+        (normed_second, (grad_gate, grad_up)),
+        (grad_out, (hidden_mid,)),
+        (grad_attended, (mixed,)),
+        (normed_first, (grad_queries, grad_keys, grad_values)),
+    )
+    sums = kernel_sums if data_count == 8 and piece_count == 4 else plain_sums
+    (gate_sum, up_sum, down_sum, out_sum, query_sum, key_sum, value_sum), extra_sum = sums(
+        pairs, extra
+    )
+    table_total = extra_sum[:, :table_rows].T.reshape(-1)[:table_size]
     table_total = table_total.reshape(bucket_count, head_count)
-    grad_gain_one_shard = attn_sum[:, 4 * inner + table_rows]
-    grad_gain_two_shard = attn_sum[:, 4 * inner + table_rows + 1]
+    grad_gain_one_shard = extra_sum[:, table_rows]
+    grad_gain_two_shard = extra_sum[:, table_rows + 1]
     return (
         block_out.reshape(row_count, local_len, model_width),
         grad_input.reshape(row_count, local_len, model_width),
         grad_gain_one_shard,
-        grad_query_shard,
-        grad_key_shard,
-        grad_value_shard,
-        grad_out_shard,
+        query_sum,
+        key_sum,
+        value_sum,
+        out_sum.T,
         table_total,
         grad_gain_two_shard,
-        grad_gate_shard,
-        grad_up_shard,
-        grad_down_shard,
+        gate_sum,
+        up_sum,
+        down_sum.T,
     )
 
 

time: 1030 us -> 844 us (0.82)
  waiting for transfers between devices: 754 us -> 328 us
  Pallas kernels: 0 us -> 219 us
  local copies, waits for them, and re-layouts: 53.6 us -> 115 us
  matrix products: 165 us -> 132 us
    reduce_scatter x6 -> x0, waiting for transfers between devices: 412 us -> none  [the longest x3 301 us: scatter_sum(): half = lax.psum_scatter(split, 'dp', scatter_dimension=0, tiled=True)]
    pallas_call x0 -> x1, Pallas kernels: none -> 219 us  [reduce_scatter(): pl.pallas_call(functools.partial(rs_kernel, chunks), out_shape=jax.ShapeD...]
    dot_general x4 -> x0, matrix products: 33.2 us -> none  [the longest x1 15 us: local(): jnp.einsum('td,tf->df', normed_second, grad_gate_up, preferred_element_ty...]
    unnamed x82 -> x111, local copies, waits for them, and re-layouts: 14.8 us -> 43.7 us
    reshape x0 -> x14, local copies, waits for them, and re-layouts: none -> 21.3 us  [the longest x7 16.6 us: halves(): return padded.reshape(values.shape[0], 2, width).transpose(1, 0, 2)]
    reduce_scatter x1, waiting for transfers between devices: 29.3 us -> 18.9 us  [local(): lax.psum_scatter(grad_values_row.astype(jnp.bfloat16), 'seq', scatter_dim...]
  transfers between devices with their start and end apart: 12 -> 6, of which waited for: 11 -> 5; matrix products, arithmetic and copies ran while one was open for 14% -> 19% of each run, Pallas kernels for 0% -> 0%
where the time goes in v2:
time: 844 us; the launch traced here: 838 us
  waiting for transfers between devices  328 us (39%)
  Pallas kernels  219 us (26%)
  matrix products  132 us (16%)
  local copies, waits for them, and re-layouts  115 us (14%)
  other arithmetic  29.4 us (3%)
  between operations  14.9 us (2%)
    all_gather x2, waiting for transfers between devices, gather_rows(): return lax.all_gather(shard, ('dp', 'seq'), axis=0, tiled=True)  272 us
    pallas_call x1, Pallas kernels, reduce_scatter(): pl.pallas_call(functools.partial(rs_kernel, chunks), out_shape=jax.ShapeD...  219 us
    unnamed x111, local copies, waits for them, and re-layouts  43.7 us
    all_gather x1, waiting for transfers between devices, local(): lax.all_gather(keys_local.reshape(row_count, local_len, inner), 'seq', ax...  35.6 us
    reduce_scatter x1, waiting for transfers between devices, local(): lax.psum_scatter(grad_values_row.astype(jnp.bfloat16), 'seq', scatter_dim...  18.9 us
  transfers between devices with their start and end apart: 6, of which 5 were waited for; matrix products, arithmetic and copies ran while one was open for 19% of the time, Pallas kernels for 0%

profile of v2, /device:TPU:0, one launch (start us, length us, event | category | flops | bytes accessed | tf_op | source)
XLA Modules:
  0.0 838.1 jit_solution(11573061455757226086)
XLA Ops:
  12.4 1.4 copy.93
  14.6 84.3 %all-gather.7.cloned.1.call-done = bf16[1536,3200]{1,0:T(8,128)(2,1)} async-done(((bf16[48,3200]{1,0:T(8,128)(2,1)}), bf16[1536,3200]{1,0:T(8,128)(2,1)}) %all-gather.7.cloned.1.call-update) | async-done | bytes 9830416 | tf_op jit(solution)/shard_map/all_gather | solution.py:44
  99.0 2.2 convert_reduce_fusion
  101.2 3.5 fusion.81
  104.8 3.4 fusion.87
  110.9 8.8 %fusion.1 = f32[256,1024,12]{0,2,1:T(8,128)} fusion(s32[256,1024]{0,1:T(8,128)S(1)} %copy.98, bf16[32,12]{0,1:T(8,128)(2,1)S(1)} %copy-done), kind=kOutput, calls=%fused_computation.2 | convolution fusion | flops 209715200 | bytes 13632256 | tf_op jit(solution)/shard_map/qkb,bh->hqk/dot_general | solution.py:262
  119.7 15.8 %copy.99 = f32[256,1024,12]{1,0,2:T(8,128)} copy(f32[256,1024,12]{0,2,1:T(8,128)} %fusion.1) | data formatting | bytes 25165824 | tf_op jit(solution)/shard_map/qkb,bh->hqk/dot_general | solution.py:262
  137.0 2.7 fusion.84
  140.5 2.6 copy.95
  143.1 35.6 %all-gather.13.cloned.1.call-done = bf16[1024,768]{1,0:T(8,128)(2,1)} async-done(((bf16[256,768]{1,0:T(8,128)(2,1)}), bf16[1024,768]{1,0:T(8,128)(2,1)}) %all-gather.13.cloned.1.call-update) | async-done | bytes 1572880 | tf_op jit(solution)/shard_map/all_gather | solution.py:296
  178.7 1.7 copy.97
  180.4 6.1 fusion.113
  186.6 2.8 fusion.5
  189.4 2.7 copy-done.2
  192.1 3.3 fusion.90
  195.4 2.6 multiply_reduce_fusion.3
  199.3 1.5 bitcast_dynamic-update-slice_fusion.6
  201.7 187.9 %all-gather.9.cloned.1.call-done = bf16[1536,11904]{1,0:T(8,128)(2,1)} async-done(((bf16[48,11904]{1,0:T(8,128)(2,1)}), bf16[1536,11904]{1,0:T(8,128)(2,1)}) %all-gather.9.cloned.1.call-update) | async-done | bytes 36569104 | tf_op jit(solution)/shard_map/all_gather | solution.py:44
  389.6 6.7 fusion.29
  396.2 6.7 fusion.12
  403.0 10.6 %fusion.38 = (bf16[256,3968]{1,0:T(8,128)(2,1)S(1)}, bf16[256,3968]{1,0:T(8,128)(2,1)S(1)}, bf16[256,3968]{1,0:T(8,128)(2,1)}) fusion(f32[256,3968]{1,0:T(8,128)S(1)} %fusion.29, f32[256,3968]{1,0:T(8,128)S(1)} %fusion.12, bf16[256,1536]{0,1:T(8,128)(2,1)S(1)} %copy-done.26, bf16[1536,11904]{1,0:T(8,128)(2,1)} %all-gather.9.cloned.1.call-done), kind=kOutput, calls=%fused_computation.40 | convolution fusion | flops 3146973184 | bytes 27197440 | tf_op jit(solution)/shard_map/dot_general | solution.py:319
  413.6 7.9 fusion.10
  421.6 7.5 multiply_reduce_fusion.1
  429.0 1.3 bitcast_dynamic-update-slice_fusion.4
  430.4 3.2 fusion.78
  433.6 1.9 copy.106
  435.6 11.3 %multiply_reduce_fusion = (f32[12,256]{1,0:T(8,128)S(1)}, f32[12,256,1024]{2,1,0:T(8,128)}) fusion(f32[12,256,1024]{2,1,0:T(8,128)} %copy-done.2, f32[12,256]{1,0:T(8,128)} %log_add_fusion, bf16[256,12,64]{0,2,1:T(8,128)(2,1)} %bitcast.183, bf16[1024,12,64]{0,2,1:T(8,128)(2,1)} %bitcast.179), kind=kOutput, calls=%fused_computation.8 | convolution fusion | flops 412087296 | bytes 27156480 | tf_op jit(solution)/shard_map/rqhd,rkhd->rhqk/dot_general | solution.py:349
  446.9 1.9 slice-done.2
  448.8 6.3 multiply_convert_fusion
  455.1 2.7 copy-done.3
  457.8 2.4 fusion.74
  461.2 1.9 copy.119
  463.2 12.0 %copy.110 = bf16[12,256,1024]{1,0,2:T(8,128)(2,1)} copy(bf16[12,256,1024]{2,1,0:T(8,128)(2,1)} %copy-done.3) | data formatting | bytes 12582912 | tf_op jit(solution)/shard_map/convert_element_type | solution.py:353
  475.2 4.0 copy.145
  479.2 4.0 copy.146
  483.2 4.0 copy.147
  487.2 10.2 %fusion.45 = f32[1,256,1536]{1,2,0:T(8,128)} fusion(f32[256,1536]{0,1:T(8,128)} %copy-done.13, bf16[256,3968]{1,0:T(8,128)(2,1)} %get-tuple-element.62, bf16[1536,11904]{1,0:T(8,128)(2,1)} %all-gather.9.cloned.1.call-done), kind=kOutput, calls=%fused_computation.55 | convolution fusion | flops 3120955392 | bytes 17367040 | tf_op jit(solution)/shard_map/dot_general | solution.py:323
  497.4 3.0 copy.131
  501.1 7.0 fusion.91
  508.2 3.0 pad.20.clone
  511.2 4.0 copy.114
  515.2 3.0 pad.21.clone
  518.2 4.0 copy.116
  522.2 3.0 pad.22.clone
  525.2 4.1 copy.118
  529.4 5.6 convolution_convert_fusion.1
  535.0 1.2 copy.120
  536.2 7.9 fusion.75
  544.1 1.9 bitcast_dynamic-update-slice_fusion.2
  548.0 5.5 fusion.51
  554.7 4.2 convolution_add_fusion.1
  558.9 18.9 %reduce-scatter.5.cloned.1.call-done = bf16[1,256,12,64]{1,3,2,0:T(8,128)(2,1)} async-done(((bf16[1,1024,12,64]{1,3,2,0:T(8,128)(2,1)}), bf16[1,256,12,64]{1,3,2,0:T(8,128)(2,1)}) %reduce-scatter.5.cloned.1.call-update) | async-done | bytes 393232 | tf_op jit(solution)/shard_map/reduce_scatter | solution.py:371
  577.8 4.9 fusion.73
  583.5 1.2 copy.112
  586.6 1.2 copy.122
  589.5 1.4 fusion.108.r_hbm
  590.8 2.1 fusion.104.lt_hbm
  593.0 218.6 %shard_map.223 = f32[2,48,7808]{2,1,0:T(8,128)} custom-call(bf16[5,1536,256]{2,1,0:T(8,128)(2,1)} %fusion.104.lt_hbm, bf16[2,256,7808]{2,1,0:T(8,128)(2,1)} %fusion.108.r_hbm), custom_call_target="tpu_custom_call" | custom-call | tf_op jit(solution)/shard_map/pallas_call | solution.py:188
  812.5 1.9 slice_bitcast_fusion.4
  815.0 3.0 slice_bitcast_fusion
  818.0 1.6 fusion.70
  819.6 3.1 copy.132
  822.8 1.6 copy.148
  824.4 1.6 copy.149
  (154 shorter events, 29.1 us)
Async XLA Ops:
  7.2 103.7 %copy-start = (bf16[32,12]{0,1:T(8,128)(2,1)S(1)}, bf16[32,12]{0,1:T(8,128)(2,1)}, u32[]{:S(2)}) copy-start(bf16[32,12]{0,1:T(8,128)(2,1)} %param.20) | copy-start | bytes 2308
  7.2 91.8 %all-gather.7.cloned.1.call-start = ((), (), s32[]{:S(2)}) async-start(), calls=%async_computation.2 | async-start | bytes 10137600 | tf_op jit(solution)/shard_map/all_gather | solution.py:44
  11.6 0.7 copy-start.27
  12.3 128.2 %all-gather.11.cloned.1.call-start = ((), (), s32[]{:S(2)}) async-start(), calls=%async_computation.6 | async-start | bytes 1966080 | tf_op jit(solution)/shard_map/all_gather | solution.py:297
  13.8 181.6 %copy-start.5 = (bf16[1,256,1536]{1,2,0:T(8,128)(2,1)}, bf16[1,256,1536]{1,2,0:T(8,128)(2,1)S(1)}, u32[]{:S(2)}) copy-start(bf16[1,256,1536]{1,2,0:T(8,128)(2,1)S(1)} %copy.93) | copy-start | bytes 2359300
  101.2 7.1 copy-start.29
  101.2 7.1 copy-start.30
  101.2 7.1 copy-start.31
  104.7 73.9 %all-gather.13.cloned.1.call-start = ((), (), s32[]{:S(2)}) async-start(), calls=%async_computation.7 | async-start | bytes 1966080 | tf_op jit(solution)/shard_map/all_gather | solution.py:296
  108.2 281.3 %all-gather.9.cloned.1.call-start = ((), (), s32[]{:S(2)}) async-start(), calls=%async_computation.3 | async-start | bytes 37711872 | tf_op jit(solution)/shard_map/all_gather | solution.py:44
  109.4 445.3 %reduce-scatter.3.cloned.1.call-start = ((), (), s32[]{:S(2)}) async-start(), calls=%async_computation.4 | async-start | bytes 1966080 | tf_op jit(solution)/shard_map/reduce_scatter | solution.py:368
  110.9 8.8 %copy-start.11 = (s32[256,1024]{0,1:T(8,128)}, s32[256,1024]{0,1:T(8,128)S(1)}, u32[]{:S(2)}) copy-start(s32[256,1024]{0,1:T(8,128)S(1)} %copy.98) | copy-start | bytes 3145732
  119.7 15.8 %copy-start.24 = (bf16[1,256,1536]{2,1,0:T(8,128)(2,1)S(1)}, bf16[1,256,1536]{2,1,0:T(8,128)(2,1)}, u32[]{:S(2)}) copy-start(bf16[1,256,1536]{2,1,0:T(8,128)(2,1)} %param.25) | copy-start | bytes 2359300
  119.7 16.1 %copy-start.36 = (s32[1,1024]{1,0:T(1,128)S(1)}, s32[1,1024]{1,0:T(1,128)}, u32[]{:S(2)}) copy-start(s32[1,1024]{1,0:T(1,128)} %param.14) | copy-start | bytes 12292
  135.8 64.9 %copy-start.9 = (bf16[1,256,1536]{1,2,0:T(8,128)(2,1)}, bf16[1,256,1536]{1,2,0:T(8,128)(2,1)S(1)}, u32[]{:S(2)}) copy-start(bf16[1,256,1536]{1,2,0:T(8,128)(2,1)S(1)} %copy.102) | copy-start | bytes 2359300
  186.5 5.5 copy-start.2
  186.5 5.5 copy-start.12
  195.4 2.7 copy-start.28
  195.4 3.9 copy-start.33
  198.1 1.2 copy-start.13
  198.1 191.5 %copy-start.25 = (bf16[1,256,1536]{2,1,0:T(8,128)(2,1)S(1)}, bf16[1,256,1536]{2,1,0:T(8,128)(2,1)}, u32[]{:S(2)}) copy-start(bf16[1,256,1536]{2,1,0:T(8,128)(2,1)} %param.25) | copy-start | bytes 2359300
  201.7 194.5 %copy-start.26 = (bf16[256,1536]{0,1:T(8,128)(2,1)S(1)}, bf16[256,1536]{0,1:T(8,128)(2,1)}, u32[]{:S(2)}) copy-start(bf16[256,1536]{0,1:T(8,128)(2,1)} %get-tuple-element.59) | copy-start | bytes 2359300
  413.6 7.9 copy-start.18
  413.6 8.0 copy-start.19
  413.6 8.0 copy-start.14
  413.6 8.0 copy-start.34
  421.6 7.5 copy-start.10
  421.6 7.5 copy-start.38
  435.5 11.3 %slice-start = ((s8[12582912]{0:T(1024)(128)(4,1)}), s8[4194304]{0:T(1024)(128)(4,1)S(1)}, s32[]{:S(2)}) async-start(s8[12582912]{0:T(1024)(128)(4,1)} %bitcast.170), calls=%async_computation.8 | async-start | bytes 8388608
  435.5 11.3 %slice-start.1 = ((s8[12582912]{0:T(1024)(128)(4,1)}), s8[4194304]{0:T(1024)(128)(4,1)S(1)}, s32[]{:S(2)}) async-start(s8[12582912]{0:T(1024)(128)(4,1)} %bitcast.170), calls=%async_computation.9 | async-start | bytes 8388608
  435.5 13.2 %slice-start.2 = ((s8[12582912]{0:T(1024)(128)(4,1)}), s8[4194304]{0:T(1024)(128)(4,1)S(1)}, s32[]{:S(2)}) async-start(s8[12582912]{0:T(1024)(128)(4,1)} %bitcast.170), calls=%async_computation.10 | async-start | bytes 8388608
  435.5 13.2 %copy-start.32 = (f32[12,256]{1,0:T(8,128)S(1)}, f32[12,256]{1,0:T(8,128)}, u32[]{:S(2)}) copy-start(f32[12,256]{1,0:T(8,128)} %log_add_fusion) | copy-start | bytes 36868
  455.1 2.7 copy-start.3
  460.2 117.6 %reduce-scatter.5.cloned.1.call-start = ((), (), s32[]{:S(2)}) async-start(), calls=%async_computation.5 | async-start | bytes 1966080 | tf_op jit(solution)/shard_map/reduce_scatter | solution.py:371
  487.2 13.2 %copy-start.37 = (f32[1536]{0:T(1024)S(1)}, f32[1536]{0:T(1024)}, u32[]{:S(2)}) copy-start(f32[1536]{0:T(1024)} %get-tuple-element.50) | copy-start | bytes 18436
  529.4 6.9 copy-start.15
  544.1 2.2 copy-start.7
  544.1 2.8 copy-start.8
  546.4 1.2 copy-start.22
  547.0 1.0 copy-start.20
  547.6 5.9 copy-start.4
  548.0 5.5 copy-start.6
  577.8 5.0 copy-start.35
  577.8 8.6 %copy-start.21 = (bf16[1,256,12,64]{1,3,2,0:T(8,128)(2,1)S(1)}, bf16[1,256,12,64]{1,3,2,0:T(8,128)(2,1)}, u32[]{:S(2)}) copy-start(bf16[1,256,12,64]{1,3,2,0:T(8,128)(2,1)} %reduce-scatter.3.cloned.1.call-done) | copy-start | bytes 1179652
  811.5 6.5 copy-start.40
  811.6 6.5 copy-start.23
  811.6 6.5 copy-start.39
  819.6 8.5 %copy-start.17 = (f32[2,6,8,2048]{3,2,1,0:T(8,128)S(1)}, f32[2,6,8,2048]{3,2,1,0:T(8,128)}, u32[]{:S(2)}) copy-start(f32[2,6,8,2048]{3,2,1,0:T(8,128)} %get-tuple-element.65) | copy-start | bytes 2359300
  819.6 9.5 %copy-start.16 = (f32[2,6,8,2048]{3,2,1,0:T(8,128)S(1)}, f32[2,6,8,2048]{3,2,1,0:T(8,128)}, u32[]{:S(2)}) copy-start(f32[2,6,8,2048]{3,2,1,0:T(8,128)} %get-tuple-element.64) | copy-start | bytes 2359300
  828.1 3.0 copy-start.1
Sparse Core Ops, SparseCore 0:
  12.5 86.4 all-gather.6
  104.9 35.6 all-gather.10
  142.7 35.9 all-gather.12
  181.3 208.1 all-gather.8
  460.3 33.4 reduce-scatter.2
  544.2 33.4 reduce-scatter.4

commit v3 on v1

--- a/solution.py
+++ b/solution.py
@@ -1,11 +1,16 @@
+import functools
+
 import jax
 import jax.numpy as jnp
 from jax import lax
+from jax.experimental import pallas as pl
+from jax.experimental.pallas import tpu as pltpu
 from jax.sharding import PartitionSpec as P
 
 epsilon = 1e-06
 far_bounds = (12, 16, 23, 32, 46, 64, 91)
 highest = lax.Precision.HIGHEST
+mesh_ids = pl.DeviceIdType.MESH
 
 
 def bucket_table(offset):
@@ -48,7 +53,16 @@
     return lax.psum_scatter(half, "seq", scatter_dimension=1, tiled=True)[0, 0]
 
 
-def local(
+def plain_sums(pairs, extra):
+    found = []
+    for left, rights in pairs:
+        for right in rights:
+            part = jnp.einsum("td,tf->df", left, right, preferred_element_type=jnp.float32)
+            found.append(scatter_sum(part.astype(jnp.bfloat16)).astype(jnp.float32))
+    return found, scatter_sum(extra.astype(jnp.bfloat16)).astype(jnp.float32)
+
+
+def plain_local(
     hidden_in,
     segment_ids,
     gain_attn,
@@ -139,10 +153,6 @@
     block_out = middle + jnp.dot(hidden_mid, down_full, preferred_element_type=jnp.float32)
     gain_second = gain_two.astype(jnp.float32)
     grad_out = cotangent.reshape(token_count, model_width)
-    grad_down_parts = jnp.einsum(
-        "tf,td->df", hidden_mid, grad_out, preferred_element_type=jnp.float32
-    ).astype(jnp.bfloat16)
-    down_sum = scatter_sum(grad_down_parts)
     grad_hidden = (
         jnp.einsum("td,fd->tf", grad_out, down_full, preferred_element_type=jnp.float32)
         .astype(jnp.bfloat16)
@@ -151,11 +161,6 @@
     gelu_value, gelu_pull = jax.vjp(lambda value: jax.nn.gelu(value, approximate=True), gate_pre)
     grad_gate = gelu_pull(grad_hidden * up_pre)[0].astype(jnp.bfloat16)
     grad_up = (grad_hidden * gelu_value).astype(jnp.bfloat16)
-    grad_gate_up = jnp.concatenate([grad_gate, grad_up], axis=1)
-    grad_gate_up_parts = jnp.einsum(
-        "td,tf->df", normed_second, grad_gate_up, preferred_element_type=jnp.float32
-    ).astype(jnp.bfloat16)
-    gate_up_sum = scatter_sum(grad_gate_up_parts)
     grad_normed_second = jnp.einsum(
         "tf,df->td", grad_gate, gate_full, preferred_element_type=jnp.float32
     ) + jnp.einsum("tf,df->td", grad_up, up_full, preferred_element_type=jnp.float32)
@@ -163,13 +168,7 @@
         grad_normed_second, middle, scale_second, gain_second
     )
     grad_middle = grad_out.astype(jnp.float32) + grad_middle_norm
-    grad_gate_shard = gate_up_sum[:, :ff_width].astype(jnp.float32)
-    grad_up_shard = gate_up_sum[:, ff_width:].astype(jnp.float32)
-    grad_down_shard = down_sum.T.astype(jnp.float32)
     grad_attended = grad_middle.astype(jnp.bfloat16)
-    grad_wout_parts = jnp.einsum(
-        "ti,td->di", mixed, grad_attended, preferred_element_type=jnp.float32
-    ).astype(jnp.bfloat16)
     grad_mixed = jnp.einsum(
         "td,id->ti", grad_attended, out_full, preferred_element_type=jnp.float32
     ).astype(jnp.bfloat16)
@@ -205,10 +204,6 @@
     )
     grad_keys = grad_keys_part.astype(jnp.bfloat16).reshape(token_count, inner)
     grad_values = grad_values_part.astype(jnp.bfloat16).reshape(token_count, inner)
-    grad_projected = jnp.concatenate([grad_queries, grad_keys, grad_values], axis=1)
-    grad_projection_parts = jnp.einsum(
-        "td,ti->di", normed_first, grad_projected, preferred_element_type=jnp.float32
-    ).astype(jnp.bfloat16)
     grad_normed_first = jnp.einsum(
         "ti,di->td", grad_queries, query_full, preferred_element_type=jnp.float32
     )
@@ -233,32 +228,564 @@
     gain_block = gain_block.reshape(2, device_count, shard_width).transpose(1, 0, 2)
     extra = jnp.concatenate([table_block, gain_block], axis=1).transpose(0, 2, 1)
     extra = extra.reshape(model_width, table_rows + 2)
-    extra = jnp.pad(extra, ((0, 0), (0, -(table_rows + 2) % 128))).astype(jnp.bfloat16)
-    attn_sum = scatter_sum(
-        jnp.concatenate([grad_projection_parts, grad_wout_parts, extra], axis=1)
-    ).astype(jnp.float32)
-    grad_query_shard = attn_sum[:, :inner]
-    grad_key_shard = attn_sum[:, inner : 2 * inner]
-    grad_value_shard = attn_sum[:, 2 * inner : 3 * inner]
-    grad_out_shard = attn_sum[:, 3 * inner : 4 * inner].T
-    table_total = attn_sum[:, 4 * inner : 4 * inner + table_rows].T.reshape(-1)[:table_size]
+    extra = jnp.pad(extra, ((0, 0), (0, -(table_rows + 2) % 128)))
+    pairs = (
+        (normed_second, (grad_gate, grad_up)),
+        (grad_out, (hidden_mid,)),
+        (grad_attended, (mixed,)),
+        (normed_first, (grad_queries, grad_keys, grad_values)),
+    )
+    (gate_sum, up_sum, down_sum, out_sum, query_sum, key_sum, value_sum), extra_sum = plain_sums(
+        pairs, extra
+    )
+    table_total = extra_sum[:, :table_rows].T.reshape(-1)[:table_size]
     table_total = table_total.reshape(bucket_count, head_count)
-    grad_gain_one_shard = attn_sum[:, 4 * inner + table_rows]
-    grad_gain_two_shard = attn_sum[:, 4 * inner + table_rows + 1]
+    grad_gain_one_shard = extra_sum[:, table_rows]
+    grad_gain_two_shard = extra_sum[:, table_rows + 1]
     return (
         block_out.reshape(row_count, local_len, model_width),
         grad_input.reshape(row_count, local_len, model_width),
         grad_gain_one_shard,
-        grad_query_shard,
-        grad_key_shard,
-        grad_value_shard,
-        grad_out_shard,
+        query_sum,
+        key_sum,
+        value_sum,
+        out_sum.T,
         table_total,
         grad_gain_two_shard,
-        grad_gate_shard,
-        grad_up_shard,
-        grad_down_shard,
-    )
+        gate_sum,
+        up_sum,
+        down_sum.T,
+    )
+
+
+gelu_c=0.7978845608028654
+
+def peers_of():
+    dp=lax.axis_index("dp"); z=lax.axis_index("seq")
+    c=lax.rem(dp,2); x=lax.rem(dp//2,2); y=dp//4
+    return dp,z,c,x,y
+
+def remote(src,dst,ss,rs,dev):
+    return pltpu.make_async_remote_copy(src_ref=src,dst_ref=dst,send_sem=ss,recv_sem=rs,device_id=dev,device_id_type=mesh_ids)
+
+def dot(a,b):
+    return jnp.dot(a,b,preferred_element_type=jnp.float32)
+
+def dot_nt(a,b):
+    return lax.dot_general(a,b,(((1,),(1,)),((),())),preferred_element_type=jnp.float32)
+
+def lanes(shape):
+    return lax.broadcasted_iota(jnp.int32,shape,len(shape)-1)
+
+def greet(devices):
+    bar=pltpu.get_barrier_semaphore()
+    for d in devices: pl.semaphore_signal(bar,inc=1,device_id=d,device_id_type=mesh_ids)
+    pl.semaphore_wait(bar,len(devices))
+
+low=jnp.bfloat16
+f32=jnp.float32
+
+def forward_kernel(ff_steps, wp, hid, cot, segr, segc, base,
+                   w, lt_o, hdg_o, q_o, kk_o, vv_o, mx_o, lse_o, gmid_o, bo_o, ggf_o, segr_o, segc_o,
+                   hrow, cotv, sr, sc, wa, wf, qq, kk, vv, mx, lse, bias, part, mid, n2, hd, yy, lt, gs, r1, r2, r3,
+                   s0s, s0r, l0, s1s, s1r, s2s, s2r, s3s, s3r, hs, hr, xs, xr, ll, lo):
+    width=wp.shape[2]
+    cols=[(0,768),(768,896)]+[(1664+512*i,512) for i in range(3*ff_steps)]
+    n=len(cols)
+    dp,z,c,x,y=peers_of()
+    q=dp//2; qx=2*y+1-x; qy=lax.rem(q+2,4); qd=3-q
+    sib=(dp+1-2*c,z); dx=(2*qx+c,z); dy=(2*qy+c,z); dxy=(dx,dy)
+    zs=[lax.rem(z+k,4) for k in (1,2,3)]; zf=[lax.rem(z+4-k,4) for k in (1,2,3)]
+    dz=[(dp,zz) for zz in zs]
+    greet([sib,dx,dy]+dz)
+    def cs(t): return pl.ds(cols[t][0],cols[t][1])
+    def s0(t,recv=False):
+        return remote(wp.at[1-c,:,cs(t)], w.at[(dp+1-2*c) if recv else dp,z,:,cs(t)], s0s.at[t], s0r.at[t], sib)
+    def keep(t): return pltpu.make_async_copy(wp.at[c,:,cs(t)], w.at[dp,z,:,cs(t)], l0.at[t])
+    def s1(t,k,recv=False):
+        r=w.at[pl.ds(2*q,2), zf[k] if recv else z, :, cs(t)]
+        return remote(r,r,s1s.at[t,k],s1r.at[t,k],dz[k])
+    def s2(t,a,recv=False):
+        r=w.at[pl.ds(2*((qx,qy)[a] if recv else q),2),:,:,cs(t)]
+        return remote(r,r,s2s.at[t,a],s2r.at[t,a],dxy[a])
+    def s3(t,a,recv=False):
+        r=w.at[2*(qd if recv else (qy,qx)[a])+a,:,:,cs(t)]
+        return remote(r,r,s3s.at[t,a],s3r.at[t,a],dxy[a])
+    def hz(k,recv=False): return remote(hid,hrow.at[c,zf[k] if recv else z],hs.at[k],hr.at[k],dz[k])
+    done=set()
+    def once(*k):
+        if k in done: return False
+        done.add(k); return True
+    def start1(t):
+        if t<n and once(1,t):
+            keep(t).wait(); s0(t,True).wait_recv()
+            for k in range(3): s1(t,k).start()
+    def start2(t):
+        if t<n and once(2,t):
+            for k in range(3): s1(t,k,True).wait_recv()
+            for a in range(2): s2(t,a).start()
+    def start3(t):
+        if 0<=t<n and once(3,t):
+            for a in range(2): s2(t,a,True).wait_recv()
+            for a in range(2): s3(t,a).start()
+    def finish(t):
+        if 0<=t<n and once(4,t):
+            for a in range(2): s3(t,a,True).wait_recv()
+    def advance(t):
+        start1(t+2); start2(t); start3(t-1); finish(t-2)
+    keep_h=pltpu.make_async_copy(hid,hrow.at[c,z],ll.at[0]); keep_h.start()
+    keep_c=pltpu.make_async_copy(cot,cotv.at[c],ll.at[1]); keep_c.start()
+    keep_r=pltpu.make_async_copy(segr,sr.at[c],ll.at[2]); keep_r.start()
+    keep_s=pltpu.make_async_copy(segc,sc.at[c],ll.at[3]); keep_s.start()
+    for t in range(2): s0(t).start(); keep(t).start()
+    give_c=remote(cot,cotv.at[c],xs.at[0],xr.at[0],sib); give_c.start()
+    give_r=remote(segr,sr.at[c],xs.at[1],xr.at[1],sib); give_r.start()
+    give_s=remote(segc,sc.at[c],xs.at[2],xr.at[2],sib); give_s.start()
+    for t in range(2,n): s0(t).start(); keep(t).start()
+    start1(0); start1(1)
+    for k in range(3): hz(k).start()
+    advance(0); advance(1)
+    start3(1); finish(0); finish(1)
+    load_a=pltpu.make_async_copy(w.at[:,:,:,pl.ds(0,1664)],wa,ll.at[4]); load_a.start()
+    keep_h.wait(); keep_c.wait(); keep_r.wait(); keep_s.wait()
+    remote(segr,sr.at[1-c],xs.at[1],xr.at[1],sib).wait_recv()
+    remote(segc,sc.at[1-c],xs.at[2],xr.at[2],sib).wait_recv()
+    remote(cot,cotv.at[1-c],xs.at[0],xr.at[0],sib).wait_recv()
+    load_a.wait()
+    def wcol(a,b): return wa[:,:,:,a:b].reshape(1536,b-a)
+    pick=(lanes((8,128))==lax.broadcasted_iota(jnp.int32,(8,128),0)).astype(low)
+    gs[...]=dot_nt(pick,wcol(1536,1664))
+    def transpose_cot(i,_):
+        lt[2,:,pl.ds(pl.multiple_of(i*128,128),128)]=cotv[i//2,pl.ds(pl.multiple_of(lax.rem(i,2)*128,128),128),:].astype(f32).T.astype(low)
+        return 0
+    lax.fori_loop(0,4,transpose_cot,0)
+    for k in range(3): hz(k,True).wait_recv()
+    give_h=remote(hrow.at[c],hrow.at[c],xs.at[3],xr.at[3],sib); give_h.start()
+    def normed(v,row):
+        s=lax.rsqrt(jnp.mean(v*v,axis=-1,keepdims=True)+epsilon)
+        return v*s*gs[row:row+1,:]
+    def keys_of(r):
+        def body(i,_):
+            a=pl.ds(pl.multiple_of(lax.rem(i,2)*128,128),128)
+            v=normed(hrow[r,i//2,a,:].astype(f32),0).astype(low)
+            d=pl.ds(pl.multiple_of(i*128,128),128)
+            kk[r,d,:]=dot(v,wcol(384,768)).astype(low)
+            vv[r,d,:]=dot(v,wcol(768,1152)).astype(low)
+            return 0
+        lax.fori_loop(0,8,body,0)
+    keys_of(c)
+    remote(hrow.at[1-c],hrow.at[1-c],xs.at[3],xr.at[3],sib).wait_recv()
+    advance(2)
+    keys_of(1-c)
+    def queries(i,_):
+        a=pl.ds(pl.multiple_of(lax.rem(i,2)*128,128),128)
+        v=normed(hrow[i//2,z,a,:].astype(f32),0)
+        d=pl.ds(pl.multiple_of(i*128,128),128)
+        qq[d,:]=dot(v.astype(low),wcol(0,384)).astype(low)
+        lt[0,:,d]=v.T.astype(low)
+        return 0
+    lax.fori_loop(0,4,queries,0)
+    advance(3)
+    for h in range(6):
+        pair=pl.ds(128*(h//2),128); odd=h%2
+        bias[...]=pltpu.roll(jnp.broadcast_to(base[h:h+1,:],(256,1280)),1024,1,stride=1,stride_axis=0)
+        def attend(i,_):
+            r=i//2; d=pl.ds(pl.multiple_of(i*128,128),128)
+            a=pl.ds(pl.multiple_of(lax.rem(i,2)*128,128),128)
+            mine=(lanes((128,128))>=64) if odd else (lanes((128,128))<64)
+            qh=jnp.where(mine,qq[d,pair].astype(f32),0.0).astype(low)
+            s=dot_nt(qh,kk[r,:,pair])+bias[a,0:1024]
+            s=jnp.where(sc[r,a,0:1]==sr[r,0:1,:],s,-1000000000.0)
+            m=jnp.max(s,axis=-1,keepdims=True)
+            e=jnp.exp(s-m)
+            l=jnp.sum(e,axis=-1,keepdims=True)
+            p=(e*(1.0/l)).astype(low)
+            o=dot(p,vv[r,:,pair])
+            if odd: o=jnp.where(mine,o,mx[d,pair].astype(f32))
+            mx[d,pair]=o.astype(low)
+            lse[r,a,:]=jnp.where(lanes((128,128))==h,m+jnp.log(l),lse[r,a,:]) if h else jnp.broadcast_to(m+jnp.log(l),(128,128))
+            return 0
+        lax.fori_loop(0,4,attend,0)
+        if h in (1,3): advance(4+h//2)
+    def project(i,_):
+        part[i//2,pl.ds(pl.multiple_of(lax.rem(i,2)*128,128),128),:]=dot_nt(mx[pl.ds(pl.multiple_of(i*128,128),128),:],wcol(1152,1536))
+        return 0
+    lax.fori_loop(0,4,project,0)
+    give_p=remote(part,r1,xs.at[4],xr.at[4],sib); give_p.start()
+    outs=[pltpu.make_async_copy(a,b,lo.at[i]) for i,(a,b) in enumerate(((qq,q_o),(kk,kk_o),(vv,vv_o),(mx,mx_o),(lse,lse_o),(sr,segr_o),(sc,segc_o)))]
+    for o in outs: o.start()
+    give_p.wait_recv()
+    def middle(i,_):
+        a=pl.ds(pl.multiple_of(lax.rem(i,2)*128,128),128); r=i//2
+        d=pl.ds(pl.multiple_of(i*128,128),128)
+        v=hrow[r,z,a,:].astype(f32)+(part[r,a,:]+r1[r,a,:])
+        mid[r,a,:]=v
+        v=normed(v,1)
+        n2[d,:]=v.astype(low)
+        lt[1,:,d]=v.T.astype(low)
+        return 0
+    lax.fori_loop(0,4,middle,0)
+    give_p.wait_send()
+    give_lt=pltpu.make_async_copy(lt,lt_o,ll.at[5]); give_lt.start()
+    advance(6)
+    hout=[]
+    for j in range(ff_steps):
+        if j:
+            for t in range(4+3*j,7+3*j): advance(t)
+        loads=[pltpu.make_async_copy(w.at[:,:,:,cs(2+3*j+i)],wf.at[i],ll.at[6+i]) for i in range(3)]
+        for l in loads: l.start()
+        b=j%2
+        if j>=2: hout[j-2].wait()
+        for l in loads: l.wait()
+        def feed(i,_):
+            d=pl.ds(pl.multiple_of(i*256,256),256)
+            v=n2[d,:]
+            wg=wf[0].reshape(1536,512); wu=wf[1].reshape(1536,512); wd=wf[2].reshape(1536,512)
+            gate=dot(v,wg); up=dot(v,wu)
+            gh=dot(cotv[i],wd).astype(low).astype(f32)
+            u2=gate*gate
+            th=jnp.tanh(gelu_c*(gate+0.044715*(gate*u2)))
+            act=0.5*gate*(1.0+th)
+            slope=0.5*(1.0+th)+0.5*gate*(1.0-th*th)*(gelu_c*(1.0+3*0.044715*u2))
+            hm=(act*up).astype(low); dg=(gh*up*slope).astype(low); du=(gh*act).astype(low)
+            hd[b,0,d,:]=hm; hd[b,1,d,:]=dg; hd[b,2,d,:]=du
+            yp=dot_nt(hm,wd); gp=dot_nt(dg,wg)+dot_nt(du,wu)
+            if j: yp=yp+yy[i]; gp=gp+part[i]
+            yy[i]=yp; part[i]=gp
+            return 0
+        lax.fori_loop(0,2,feed,0)
+        o=pltpu.make_async_copy(hd.at[b],hdg_o.at[:,:,pl.ds(512*j,512)],lo.at[7+b]); o.start(); hout.append(o)
+    give_g=remote(part,r2,xs.at[5],xr.at[5],sib); give_g.start()
+    give_y=remote(yy.at[1-c],r3,xs.at[6],xr.at[6],sib); give_y.start()
+    give_g.wait_recv()
+    give_g.wait_send()
+    def gradient(i,acc):
+        a=pl.ds(pl.multiple_of(lax.rem(i,2)*128,128),128); r=i//2
+        v=mid[r,a,:]; gn=part[r,a,:]+r2[r,a,:]
+        s=lax.rsqrt(jnp.mean(v*v,axis=-1,keepdims=True)+epsilon)
+        wg=gn*gs[1:2,:]
+        part[r,a,:]=cotv[r,a,:].astype(f32)+(s*wg-v*(s*s*s)*jnp.mean(wg*v,axis=-1,keepdims=True))
+        return acc+jnp.where(r==c,1.0,0.0)*jnp.sum(gn*v*s,axis=0,keepdims=True)
+    acc=lax.fori_loop(0,4,gradient,jnp.zeros((1,1536),f32))
+    ggf_o[0:8,:]=jnp.broadcast_to(acc,(8,1536))
+    ggf_o[8:16,:]=gs[...]
+    give_m=pltpu.make_async_copy(part,gmid_o,ll.at[9]); give_m.start()
+    give_y.wait_recv(); give_y.wait_send()
+    def final(i,_):
+        a=pl.ds(pl.multiple_of(i*128,128),128)
+        yy[c,a,:]=mid[c,a,:]+(yy[c,a,:]+r3[a,:])
+        return 0
+    lax.fori_loop(0,2,final,0)
+    give_b=pltpu.make_async_copy(yy.at[c],bo_o,ll.at[10]); give_b.start()
+    for o in outs+hout[-2:]: o.wait()
+    give_lt.wait(); give_m.wait(); give_b.wait()
+    give_c.wait_send(); give_r.wait_send(); give_s.wait_send(); give_h.wait_send()
+    for k in range(3): hz(k).wait_send()
+    for t in range(n):
+        s0(t).wait_send()
+        for k in range(3): s1(t,k).wait_send()
+        for a in range(2): s2(t,a).wait_send(); s3(t,a).wait_send()
+
+def forward_call(wp, hid, cot, segr, segc, base, ff_steps, cid=0):
+    n=2+3*ff_steps
+    S=jax.ShapeDtypeStruct; V=pltpu.VMEM; D=pltpu.SemaphoreType.DMA
+    fw=512*ff_steps
+    hbm=pl.BlockSpec(memory_space=pltpu.HBM); vm=pl.BlockSpec(memory_space=pltpu.VMEM)
+    outs=(S((8,4,48,wp.shape[2]),low),S((3,1536,512),low),S((3,512,fw),low),S((512,384),low),S((2,1024,384),low),S((2,1024,384),low),
+          S((512,384),low),S((2,256,128),f32),S((2,256,1536),f32),S((256,1536),f32),S((16,1536),f32),S((2,8,1024),f32),S((2,256,128),f32))
+    ospec=[hbm]*13; ospec[10]=vm
+    scratch=[V((2,4,256,1536),low),V((2,256,1536),low),V((2,8,1024),f32),V((2,256,128),f32),V((8,4,48,1664),low),V((3,8,4,48,512),low),
+             V((512,384),low),V((2,1024,384),low),V((2,1024,384),low),V((512,384),low),V((2,256,128),f32),V((256,1280),f32),
+             V((2,256,1536),f32),V((2,256,1536),f32),V((512,1536),low),V((2,3,512,512),low),V((2,256,1536),f32),V((3,1536,512),low),V((8,1536),f32),
+             V((2,256,1536),f32),V((2,256,1536),f32),V((256,1536),f32),
+             D((n,)),D((n,)),D((n,)),D((n,3)),D((n,3)),D((n,2)),D((n,2)),D((n,2)),D((n,2)),D((3,)),D((3,)),D((7,)),D((7,)),D((11,)),D((9,))]
+    return pl.pallas_call(functools.partial(forward_kernel,ff_steps),out_shape=outs,
+        in_specs=[hbm]*5+[vm],out_specs=tuple(ospec),scratch_shapes=scratch,
+        compiler_params=pltpu.CompilerParams(collective_id=cid,has_side_effects=True,vmem_limit_bytes=62*2**20))(wp,hid,cot,segr,segc,base)
+
+def dot_tn(a,b):
+    return lax.dot_general(a,b,(((0,),(0,)),((),())),preferred_element_type=jnp.float32)
+
+part_slots=2
+sum_slots=3
+def backward_kernel(chunks, ff_steps, w, lt_h, hdg, q_h, kk_h, vv_h, mx_h, lse_h, gmid, segr_h, segc_h, hid_h, base, rows, spots, tile,
+                    out, gin_o, *rest):
+    n=len(chunks)
+    ra1=rest[0:n]; rb1=rest[n:2*n]; ra2=rest[2*n:3*n]; rb2=rest[3*n:4*n]; rz=rest[4*n:5*n]
+    (fin,p,lt,gat,rbuf,wa,qq,kk,vv,mx,gm,lse,sr,sc,bias,dbias,dq,acc,dkv,rkv,dk,dv,part,r3,gin,hid,dtab,ext,
+     ll,lr,lo,s1,v1,s2,v2,s3,v3,s4,v4,ks,kr,xs,xr)=rest[5*n:]
+    dp,z,c,x,y=peers_of()
+    sib=(dp+1-2*c,z); dx=(dp+2-4*x,z); dy=(lax.rem(dp+4,8),z)
+    zs=[lax.rem(z+k,4) for k in (1,2,3)]; dz=[(dp,zz) for zz in zs]
+    loads=[pltpu.make_async_copy(a,b,ll.at[i]) for i,(a,b) in enumerate((
+        (lt_h.at[pl.ds(1,2)],lt),(gmid,part),(w.at[:,:,:,pl.ds(1152,384)],wa.at[:,:,:,pl.ds(0,384)]),(q_h,qq),(kk_h,kk),(vv_h,vv),(mx_h,mx),(lse_h,lse),(segr_h,sr),(segc_h,sc),(hid_h,hid),(gmid.at[c],gin)))]
+    for l in loads: l.start()
+    slots=rbuf.shape[0]
+    def fetch(t):
+        kind,i,j=chunks[t][3]
+        return pltpu.make_async_copy(hdg.at[i,:,pl.ds(512*j,512)],rbuf.at[t%slots],lr.at[t])
+    feeds=[t for t in range(n) if chunks[t][3][0]=="feed"]
+    for t in feeds[:slots]: fetch(t).start()
+    greet([sib,dx,dy]+dz)
+    load_n=pltpu.make_async_copy(lt_h.at[0],lt.at[1],ll.at[14])
+    c1={}; c2={}; c3={}; c4={}; done=set()
+    def once(*k):
+        if k in done: return False
+        done.add(k); return True
+    def stage1(t):
+        left,off,wd,src=chunks[t]; b=t%part_slots
+        if t>=part_slots:
+            for d in c1[t-part_slots]: d.wait_send()
+        if src[0]=="feed":
+            fetch(t).wait()
+            right=lambda: rbuf[t%slots]
+        else:
+            right=(lambda: mx[...],lambda: dq[...],lambda: dk[...],lambda: dv[...],None)[src[1]]
+        if src==("ref",1,0): load_n.wait()
+        if right is None:
+            p[b,:,:,:,:,:,0:wd]=ext[...].T.astype(low).reshape(2,2,2,4,48,wd)
+        else:
+            def body(i,_):
+                rs=pl.ds(pl.multiple_of(i*192,192),192)
+                lhs=gat[rs,:] if left==3 else lt[left,rs,:]
+                p[b,i//4,lax.rem(i//2,2),lax.rem(i,2),:,:,0:wd]=dot(lhs,right()).astype(low).reshape(4,48,wd)
+                return 0
+            lax.fori_loop(0,8,body,0)
+        if t==feeds[-1]:
+            load_n.start()
+        if src[0]=="feed" and t+slots<n and chunks[t+slots][3][0]=="feed": fetch(t+slots).start()
+        a=remote(p.at[b,:,1-x,0,:,:,pl.ds(0,wd)],ra1[t],s1.at[t,0],v1.at[t,0],dx)
+        e=remote(p.at[b,1-y,:,1,:,:,pl.ds(0,wd)],rb1[t],s1.at[t,1],v1.at[t,1],dy)
+        a.start(); e.start(); c1[t]=(a,e)
+    def stage2(t):
+        wd=chunks[t][2]; b=t%part_slots
+        for d in c1[t]: d.wait_recv()
+        def body(i,_):
+            h=i//4; zz=lax.rem(i,4)
+            ra1[t][h,zz]=ra1[t][h,zz]+p[b,h,x,0,zz,:,0:wd]
+            rb1[t][h,zz]=rb1[t][h,zz]+p[b,y,h,1,zz,:,0:wd]
+            return 0
+        lax.fori_loop(0,8,body,0)
+        a=remote(ra1[t].at[1-y],ra2[t],s2.at[t,0],v2.at[t,0],dy)
+        e=remote(rb1[t].at[1-x],rb2[t],s2.at[t,1],v2.at[t,1],dx)
+        a.start(); e.start(); c2[t]=(a,e)
+    def stage3(t):
+        for d in c2[t]: d.wait_recv()
+        def body(zz,_):
+            ra2[t][zz]=ra2[t][zz]+ra1[t][y,zz]
+            rb2[t][zz]=rb2[t][zz]+rb1[t][x,zz]
+            return 0
+        lax.fori_loop(0,4,body,0)
+        cs=[]
+        for k in range(3):
+            cs.append(remote(ra2[t].at[zs[k]],rz[t].at[k,0],s3.at[t,k,0],v3.at[t,k,0],dz[k]))
+            cs.append(remote(rb2[t].at[zs[k]],rz[t].at[k,1],s3.at[t,k,1],v3.at[t,k,1],dz[k]))
+        for d in cs: d.start()
+        c3[t]=cs
+    def stage4(t):
+        off,wd=chunks[t][1:3]
+        for d in c3[t]: d.wait_recv()
+        f0=ra2[t][z].astype(f32); f1=rb2[t][z].astype(f32)
+        for k in range(3):
+            f0=f0+rz[t][k,0].astype(f32); f1=f1+rz[t][k,1].astype(f32)
+        b=t%sum_slots
+        if t>=sum_slots:
+            c4[t-sum_slots][0].wait_send(); c4[t-sum_slots][1].wait()
+        fin[b,0,:,0:wd]=f0; fin[b,1,:,0:wd]=f1
+        cols=pl.ds(off,wd)
+        a=remote(fin.at[b,1-c,:,pl.ds(0,wd)],out.at[c,:,cols],s4.at[t],v4.at[t],sib)
+        e=pltpu.make_async_copy(fin.at[b,c,:,pl.ds(0,wd)],out.at[c,:,cols],lo.at[t])
+        a.start(); e.start(); c4[t]=(a,e)
+    def step(t):
+        for k,f in ((0,stage1),(1,stage2),(2,stage3),(3,stage4)):
+            if 0<=t-k<n and once(k,t-k): f(t-k)
+    loads[0].wait()
+    step(0)
+    for l in loads[1:]: l.wait()
+    def wcol(a,b): return wa[:,:,:,a:b].reshape(1536,b-a)
+    def mixed_grad(i,_):
+        a=pl.ds(pl.multiple_of(lax.rem(i,2)*128,128),128); d=pl.ds(pl.multiple_of(i*128,128),128)
+        v=part[i//2,a,:]
+        gat[:,d]=v.T.astype(low)
+        gm[d,:]=dot(v.astype(low),wcol(0,384)).astype(low)
+        return 0
+    lax.fori_loop(0,4,mixed_grad,0)
+    load_w=pltpu.make_async_copy(w.at[:,:,:,pl.ds(0,1152)],wa,ll.at[13]); load_w.start()
+    step(1)
+    dbias[...]=jnp.zeros((256,1280),f32)
+    ext[...]=jnp.zeros((128,1536),f32)
+    dtab[...]=jnp.zeros((8,1280),f32)
+    gives=[]
+    at=2
+    for h in range(6):
+        odd=h%2; pair=pl.ds(128*(h//2),128); pp=h//2
+        bias[...]=pltpu.roll(jnp.broadcast_to(base[h:h+1,:],(256,1280)),1024,1,stride=1,stride_axis=0)
+        if not odd: acc[...]=jnp.zeros((2,2,1024,128),f32)
+        def attend(i,_):
+            r=i//2; d=pl.ds(pl.multiple_of(i*128,128),128)
+            a=pl.ds(pl.multiple_of(lax.rem(i,2)*128,128),128)
+            mine=(lanes((128,128))>=64) if odd else (lanes((128,128))<64)
+            qh=jnp.where(mine,qq[d,pair].astype(f32),0.0).astype(low)
+            gh=jnp.where(mine,gm[d,pair].astype(f32),0.0).astype(low)
+            s=dot_nt(qh,kk[r,:,pair])+bias[a,0:1024]
+            s=jnp.where(sc[r,a,0:1]==sr[r,0:1,:],s,-1000000000.0)
+            pr=jnp.exp(s-lse[r,a,h:h+1])
+            gp=dot_nt(gh,vv[r,:,pair])
+            gl=(pr*(gp-jnp.sum(pr*gp,axis=-1,keepdims=True))).astype(low)
+            wide=gl.astype(f32)
+            dbias[a,0:1024]=wide+jnp.where(r==0,0.0,1.0)*dbias[a,0:1024]
+            g=jnp.where(mine,dot(gl,kk[r,:,pair]),0.0)
+            if odd: g=g+dq[d,pair].astype(f32)
+            dq[d,pair]=g.astype(low)
+            acc[0,r]=acc[0,r]+dot_tn(gl,qh)
+            acc[1,r]=acc[1,r]+dot_tn(pr.astype(low),gh)
+            return 0
+        lax.fori_loop(0,4,attend,0)
+        m=128
+        v=dbias[0:128,:]+pltpu.roll(dbias[128:256,:],1280-128,1)
+        while m>1:
+            m//=2
+            v=v[0:m]+pltpu.roll(v[m:2*m],1280-m,1)
+        dtab[h:h+1,:]=pltpu.roll(v,256,1)
+        if odd:
+            for j in range(2):
+                for r in range(2):
+                    for zz in range(4):
+                        dkv[zz,pp,j,r]=acc[j,r,256*zz:256*zz+256,:].astype(low)
+            for k in range(3):
+                g=remote(dkv.at[zs[k],pp],rkv.at[k,pp],ks.at[pp,k],kr.at[pp,k],dz[k]); g.start(); gives.append(g)
+            step(at); at+=1
+    tab=dtab[...]
+    high=tab.astype(low); rest1=tab-high.astype(f32); mid1=rest1.astype(low); last=(rest1-mid1.astype(f32)).astype(low)
+    found=dot(high,spots[...])+dot(mid1,spots[...])+dot(last,spots[...])
+    def spread(v,row):
+        upper=v.astype(low)
+        ext[row:row+8,:]=upper.astype(f32)
+        ext[row+8:row+16,:]=v-upper.astype(f32)
+    upper=found.astype(low)
+    ext[0:8,:]=dot(upper,tile[...])
+    ext[8:16,:]=dot((found-upper.astype(f32)).astype(low),tile[...])
+    spread(rows[0:8,:],32)
+    step(at); at+=1
+    step(at); at+=1
+    step(at); at+=1
+    for g in gives: g.wait_recv()
+    for pp in range(3):
+        for j,o in enumerate((dk,dv)):
+            for r in range(2):
+                v=dkv[z,pp,j,r].astype(f32)
+                for k in range(3): v=v+rkv[k,pp,j,r].astype(f32)
+                o[256*r:256*r+256,128*pp:128*pp+128]=v.astype(low)
+    step(at); at+=1
+    load_w.wait()
+    def input_grad(i,_):
+        d=pl.ds(pl.multiple_of(i*128,128),128); a=pl.ds(pl.multiple_of(lax.rem(i,2)*128,128),128)
+        part[i//2,a,:]=dot_nt(dq[d,:],wcol(0,384))+dot_nt(dk[d,:],wcol(384,768))+dot_nt(dv[d,:],wcol(768,1152))
+        return 0
+    lax.fori_loop(0,4,input_grad,0)
+    give=remote(part.at[1-c],r3,xs.at[0],xr.at[0],sib); give.start()
+    step(at); at+=1
+    give.wait_recv()
+    def last_grad(i,total):
+        a=pl.ds(pl.multiple_of(i*128,128),128)
+        v=hid[a,:].astype(f32); gn=part[c,a,:]+r3[a,:]
+        s=lax.rsqrt(jnp.mean(v*v,axis=-1,keepdims=True)+epsilon)
+        wg=gn*rows[8:9,:]
+        gin[a,:]=gin[a,:]+(s*wg-v*(s*s*s)*jnp.mean(wg*v,axis=-1,keepdims=True))
+        return total+jnp.sum(gn*v*s,axis=0,keepdims=True)
+    total=lax.fori_loop(0,2,last_grad,jnp.zeros((1,1536),f32))
+    spread(jnp.broadcast_to(total,(8,1536)),16)
+    give_i=pltpu.make_async_copy(gin,gin_o,ll.at[12]); give_i.start()
+    while at<n+3:
+        step(at); at+=1
+    for t in range(n):
+        off,wd=chunks[t][1:3]; cols=pl.ds(off,wd)
+        remote(fin.at[t%sum_slots,1-c,:,pl.ds(0,wd)],out.at[1-c,:,cols],s4.at[t],v4.at[t],sib).wait_recv()
+        if t>=n-sum_slots:
+            c4[t][0].wait_send(); c4[t][1].wait()
+        if t>=n-part_slots:
+            for d in c1[t]: d.wait_send()
+        for d in c2[t]: d.wait_send()
+        for d in c3[t]: d.wait_send()
+    for g in gives: g.wait_send()
+    give.wait_send(); give_i.wait()
+
+def backward_chunks(ff_steps):
+    fw=512*ff_steps
+    chunks=[]
+    for j in range(ff_steps):
+        chunks+=[(0,512*j,512,("feed",1,j)),(0,fw+512*j,512,("feed",2,j)),(1,2*fw+512*j,512,("feed",0,j))]
+    o=3*fw
+    chunks+=[(3,o,384,("ref",0,0)),(1,o+384,384,("ref",1,0)),(1,o+768,384,("ref",2,0)),(1,o+1152,384,("ref",3,0)),(1,o+1536,128,("ref",4,0))]
+    return chunks
+
+def backward_call(w,lt,hdg,q,kk,vv,mx,lse,gmid,segr,segc,hid,base,rows,spots,tile,ff_steps,cid=1):
+    chunks=backward_chunks(ff_steps); n=len(chunks)
+    C=3*512*ff_steps+1664
+    S=jax.ShapeDtypeStruct; V=pltpu.VMEM; D=pltpu.SemaphoreType.DMA
+    hbm=pl.BlockSpec(memory_space=pltpu.HBM); vm=pl.BlockSpec(memory_space=pltpu.VMEM)
+    ws=[k[2] for k in chunks]
+    scratch=[V((2,4,48,k),low) for k in ws]*1+[V((2,4,48,k),low) for k in ws]+[V((4,48,k),low) for k in ws]+[V((4,48,k),low) for k in ws]+[V((3,2,48,k),low) for k in ws]
+    scratch+=[V((sum_slots,2,48,512),f32),V((part_slots,2,2,2,4,48,512),low),V((2,1536,512),low),V((1536,512),low),V((2,512,512),low),V((8,4,48,1152),low),
+      V((512,384),low),V((2,1024,384),low),V((2,1024,384),low),V((512,384),low),V((512,384),low),V((2,256,128),f32),V((2,8,1024),f32),V((2,256,128),f32),
+      V((256,1280),f32),V((256,1280),f32),V((512,384),low),V((2,2,1024,128),f32),V((4,3,2,2,256,128),low),V((3,3,2,2,256,128),low),V((512,384),low),V((512,384),low),
+      V((2,256,1536),f32),V((256,1536),f32),V((256,1536),f32),V((256,1536),low),V((8,1280),f32),V((128,1536),f32)]
+    scratch+=[D((15,)),D((n,)),D((n,)),D((n,2)),D((n,2)),D((n,2)),D((n,2)),D((n,3,2)),D((n,3,2)),D((n,)),D((n,)),D((3,3)),D((3,3)),D((1,)),D((1,))]
+    return pl.pallas_call(functools.partial(backward_kernel,chunks,ff_steps),out_shape=(S((2,48,C),f32),S((256,1536),f32)),
+        in_specs=[hbm]*12+[vm]*4,out_specs=(hbm,hbm),scratch_shapes=scratch,
+        compiler_params=pltpu.CompilerParams(collective_id=cid,has_side_effects=True,vmem_limit_bytes=62*2**20))(w,lt,hdg,q,kk,vv,mx,lse,gmid,segr,segc,hid,base,rows,spots,tile)
+
+def cut(v,h,w):
+    n=v.shape[1]
+    a=min(h*w,n); b=min((h+1)*w,n)
+    p=v[:,a:b]
+    return jnp.pad(p,((0,0),(0,w-(b-a)))) if b-a<w else p
+def pack(wq,wk,wv,wo,ga,gf,wg,wu,wd,steps):
+    gains=jnp.pad(jnp.stack([ga,gf],axis=1),((0,0),(0,126)))
+    fw=512*steps
+    rows=[]
+    for h in (0,1):
+        m=[cut(v,h,384) for v in (wq,wk,wv,wo.T)]+[gains]
+        f=[cut(v,h,fw) for v in (wg,wu,wd.T)]
+        for j in range(steps):
+            m+=[v[:,512*j:512*j+512] for v in f]
+        rows.append(jnp.concatenate(m,axis=1))
+    return jnp.stack(rows)
+def seg_ids(seg):
+    n=seg.shape[1]
+    place=jnp.arange(n,dtype=jnp.int32)
+    ids=jnp.where(seg[0]>0,seg[0],-1-place).astype(jnp.float32)
+    r=jnp.broadcast_to(ids[None],(8,n))
+    mine=lax.dynamic_slice_in_dim(ids,lax.axis_index("seq")*256,256,0)
+    return r, jnp.broadcast_to(mine[:,None],(256,128))
+def base_of(table):
+    off=jnp.arange(1280,dtype=jnp.int32)-256-256*lax.axis_index("seq")
+    oh=(bucket_table(off)[:,None]==jnp.arange(32,dtype=jnp.int32)).astype(jnp.float32)
+    c=lax.rem(lax.axis_index("dp"),2)
+    tab=table.astype(jnp.float32)
+    mine=jnp.where(c==0,tab[:,:6],tab[:,6:])
+    b=jnp.einsum("ub,bh->hu",oh,mine,precision=lax.Precision.HIGHEST)
+    return jnp.pad(b,((0,2),(0,0))), oh
+
+def joined(o,start,width,total):
+    return jnp.concatenate([o[0,:,start:start+width],o[1,:,start:start+width]],axis=1)[:,:total]
+def kernel_local(hid,seg,ga,wq,wk,wv,wo,tab,gf,wg,wu,wd,cot):
+    steps=4; fw=512*steps; ff=wg.shape[1]
+    wp=pack(wq,wk,wv,wo,ga,gf,wg,wu,wd,steps)
+    r,s=seg_ids(seg); b,oh=base_of(tab)
+    w,lt,hdg,q,kk,vv,mx,lse,gmid,bo,rows,segr,segc=forward_call(wp,hid[0],cot[0],r,s,b,steps)
+    spots=jnp.pad(oh,((0,0),(0,96))).astype(jnp.bfloat16)
+    tile=(jnp.arange(1536)[None,:]%48==jnp.arange(128)[:,None]).astype(jnp.bfloat16)
+    o,gin=backward_call(w,lt,hdg,q,kk,vv,mx,lse,gmid,segr,segc,hid[0],b,rows,spots,tile,steps)
+    e=3*fw+1536
+    i=3*fw
+    ext=o[:,:,e:]
+    t=ext[:,:32,0:8]+ext[:,:32,8:16]
+    table=jnp.concatenate([t[0,:,:6],t[1,:,:6]],axis=1)
+    g=ext[0]+ext[1]
+    gg=lambda a: g[:,a]+g[:,a+8]
+    return (bo[None],gin[None],gg(16),joined(o,i+384,384,768),joined(o,i+768,384,768),joined(o,i+1152,384,768),joined(o,i,384,768).T,table,gg(32),
+            joined(o,0,fw,ff),joined(o,fw,fw,ff),joined(o,2*fw,fw,ff).T)
 
 
 def solution(mesh):
@@ -291,4 +818,6 @@
         P(("dp", "seq"), None),
         P(None, ("dp", "seq")),
     )
+    small = mesh.shape["dp"] == 8 and mesh.shape["seq"] == 4
+    local = kernel_local if small else plain_local
     return jax.shard_map(local, mesh=mesh, in_specs=in_specs, out_specs=out_specs, check_vma=False)

time: 1030 us -> 587 us (0.57)
  waiting for transfers between devices: 754 us -> 0 us
  Pallas kernels: 0 us -> 562 us
  matrix products: 165 us -> 0.51 us
  local copies, waits for them, and re-layouts: 53.6 us -> 10.6 us
  other arithmetic: 34.6 us -> 12.1 us
  between operations: 14.9 us -> 0.97 us
    pallas_call x0 -> x2, Pallas kernels: none -> 562 us  [the longest x1 294 us: forward_call(): pl.pallas_call(functools.partial(forward_kernel, ff_steps), out_shape=out...]
    reduce_scatter x8 -> x0, waiting for transfers between devices: 441 us -> none  [the longest x3 301 us: scatter_sum(): half = lax.psum_scatter(split, 'dp', scatter_dimension=0, tiled=True)]
    all_gather x4 -> x0, waiting for transfers between devices: 312 us -> none  [the longest x2 275 us: gather_rows(): return lax.all_gather(shard, ('dp', 'seq'), axis=0, tiled=True)]
    dot_general x26 -> x1, matrix products: 165 us -> 0.51 us  [base_of(): b = jnp.einsum('ub,bh->hu', oh, mine, precision=lax.Precision.HIGHEST)]
    dot_general x1 -> x0, local copies, waits for them, and re-layouts: 15.8 us -> none  [local(): jnp.einsum('qkb,bh->hqk', onehot, rel_table.astype(jnp.float32), precisio...]
    convert_element_type x3 -> x0, local copies, waits for them, and re-layouts: 14.1 us -> none  [the longest x1 12 us: local(): grad_logits = (probs_again * (grad_probs - row_dot)).astype(jnp.bfloat16)]
    unnamed x82 -> x42, local copies, waits for them, and re-layouts: 14.8 us -> 4.02 us
    convert_element_type x6 -> x5, other arithmetic: 14.1 us -> 3.7 us  [the longest x2 1.39 us: seg_ids(): ids = jnp.where(seg[0] > 0, seg[0], -1 - place).astype(jnp.float32)]
  transfers between devices with their start and end apart: 12 -> 0, of which waited for: 11 -> 0; matrix products, arithmetic and copies ran while one was open for 14% -> 0% of each run, Pallas kernels for 0% -> 0%
where the time goes in v3:
time: 587 us; the launch traced here: 586 us
  Pallas kernels  562 us (96%)
  other arithmetic  12.1 us (2%)
  local copies, waits for them, and re-layouts  10.6 us (2%)
    pallas_call x1, Pallas kernels, forward_call(): pl.pallas_call(functools.partial(forward_kernel, ff_steps), out_shape=out...  294 us
    pallas_call x1, Pallas kernels, backward_call(): pl.pallas_call(functools.partial(backward_kernel, chunks, ff_steps), out_...  267 us

profile of v3, /device:TPU:0, one launch (start us, length us, event | category | flops | bytes accessed | tf_op | source)
XLA Modules:
  0.0 586.0 jit_solution(15080565036835857042)
XLA Ops:
  0.6 0.0 copy-start.7
  0.7 0.0 copy-start.6
  0.7 0.0 copy-start.5
  0.7 0.0 copy-start.8
  0.7 0.7 pad_maximum_fusion.8
  1.4 0.7 fusion.17
  2.1 0.1 dynamic_slice.3
  2.2 0.7 fusion.18
  2.9 0.7 convert_element_type.77
  3.6 0.1 copy.31
  3.7 0.6 broadcast_in_dim.17.segr
  4.4 0.0 copy-start.3
  4.4 0.5 fusion.19
  4.9 0.0 copy-start.2
  4.9 0.6 pad.29.base
  5.5 0.0 copy-start.4
  5.5 0.8 broadcast_in_dim.32.segc
  6.3 0.2 iota_compare_fusion.1
  6.5 0.8 convert_convert_fusion.spots
  7.3 0.9 slice.303
  8.3 0.0 slice-start.1
  8.3 0.8 fusion.tile
  9.1 0.0 copy-done.5
  9.1 0.0 slice-start
  9.1 0.0 copy-done.6
  9.1 0.0 copy-done.7
  9.2 0.0 copy-done.8
  9.2 0.0 copy-done.3
  9.2 0.0 copy-done.2
  9.3 0.0 copy-done.4
  9.5 0.0 slice-done.1
  9.5 0.5 slice-done
  10.1 1.3 pad_maximum_fusion.wp
  11.3 294.4 %shard_map.220 = (bf16[8,4,48,7808]{3,2,1,0:T(8,128)(2,1)}, bf16[3,1536,512]{2,1,0:T(8,128)(2,1)}, bf16[3,512,2048]{2,1,0:T(8,128)(2,1)}, bf16[512,384]{1,0:T(8,...) custom-call(bf16[2,48,7808]{2,1,0:T(8,128)(2,1)} %pad_maximum_fusion, ...), custom_call_target="tpu_custom_call" | custom-call | tf_op jit(solution)/shard_map/pallas_call | solution.py:502
  305.7 267.4 %shard_map.221 = (f32[2,48,7808]{2,1,0:T(8,128)}, f32[256,1536]{1,0:T(8,128)}) custom-call(bf16[8,4,48,7808]{3,2,1,0:T(8,128)(2,1)} %get-tuple-element.28.w, bf16[3,1536,512]{2,1,0:T(8,128)(2,1)} %get-tuple-element.29.lt_h, bf16[3,512,2048]{2,1,0:T(8,128)(2,1)} %get-tuple-element.30.hdg, bf16[512,384]{1,0:T(8,128)(2,1)} %get-tuple-element.31.q_h, ...), custom_call_target="tpu_custom_call" | custom-call | tf_op jit(solution)/shard_map/pallas_call | solution.py:734
  573.1 0.8 add_bitcast_fusion
  573.9 0.7 fusion.2
  574.6 0.9 slice_add_fusion
  575.5 0.1 pad_maximum_fusion.7
  575.6 0.7 copy.32
  576.3 1.2 slice_bitcast_fusion.7
  577.5 1.7 slice_bitcast_fusion.1
  579.2 1.2 fusion.1
  580.5 0.0 copy-start
  580.5 0.7 pad_maximum_fusion.6
  581.2 0.7 pad_maximum_fusion.4
  581.9 0.9 pad_maximum_fusion.3
  582.8 0.0 copy-done
  582.8 0.0 copy-start.1
  582.8 1.1 copy.67
  584.0 0.8 copy-done.1
  584.8 1.1 copy.68
  (26 shorter events, 0.2 us)
Async XLA Ops:
  0.6 8.5 %copy-start.7 = (bf16[48,768]{1,0:T(8,128)(2,1)S(1)}, bf16[48,768]{1,0:T(8,128)(2,1)}, u32[]{:S(2)}) copy-start(bf16[48,768]{1,0:T(8,128)(2,1)} %param.18) | copy-start | bytes 221188
  0.7 8.5 %copy-start.6 = (bf16[48,768]{1,0:T(8,128)(2,1)S(1)}, bf16[48,768]{1,0:T(8,128)(2,1)}, u32[]{:S(2)}) copy-start(bf16[48,768]{1,0:T(8,128)(2,1)} %param.17) | copy-start | bytes 221188
  0.7 8.4 %copy-start.5 = (bf16[48,768]{1,0:T(8,128)(2,1)S(1)}, bf16[48,768]{1,0:T(8,128)(2,1)}, u32[]{:S(2)}) copy-start(bf16[48,768]{1,0:T(8,128)(2,1)} %param.16) | copy-start | bytes 221188
  0.7 8.5 %copy-start.8 = (bf16[768,48]{0,1:T(8,128)(2,1)S(1)}, bf16[768,48]{0,1:T(8,128)(2,1)}, u32[]{:S(2)}) copy-start(bf16[768,48]{0,1:T(8,128)(2,1)} %param.19) | copy-start | bytes 221188
  4.4 4.9 copy-start.3
  4.9 4.4 copy-start.2
  5.5 3.8 copy-start.4
  8.3 1.2 slice-start.1
  9.1 0.9 slice-start
  580.5 2.4 copy-start
  582.8 2.0 copy-start.1

commit v4 on v3

--- a/solution.py
+++ b/solution.py
@@ -285,33 +285,51 @@
 low=jnp.bfloat16
 f32=jnp.float32
 
+h_parts=4
 def forward_kernel(ff_steps, wp, hid, cot, segr, segc, base,
-                   w, lt_o, hdg_o, q_o, kk_o, vv_o, mx_o, lse_o, gmid_o, bo_o, ggf_o, segr_o, segc_o,
-                   hrow, cotv, sr, sc, wa, wf, qq, kk, vv, mx, lse, bias, part, mid, n2, hd, yy, lt, gs, r1, r2, r3,
+                   w1, w2, w, lt_o, hdg_o, q_o, kk_o, vv_o, mx_o, lse_o, gnf_o, yy_o, gs_o, segr_o, segc_o, mid_o, cot_o,
+                   hrow, cotv, sr, sc, wa, wf, qq, kk, vv, mx, lse, bias, part, mid, n2, hd, yy, lt, gs, r1,
                    s0s, s0r, l0, s1s, s1r, s2s, s2r, s3s, s3r, hs, hr, xs, xr, ll, lo):
-    width=wp.shape[2]
     cols=[(0,768),(768,896)]+[(1664+512*i,512) for i in range(3*ff_steps)]
     n=len(cols)
     dp,z,c,x,y=peers_of()
     q=dp//2; qx=2*y+1-x; qy=lax.rem(q+2,4); qd=3-q
     sib=(dp+1-2*c,z); dx=(2*qx+c,z); dy=(2*qy+c,z); dxy=(dx,dy)
-    zs=[lax.rem(z+k,4) for k in (1,2,3)]; zf=[lax.rem(z+4-k,4) for k in (1,2,3)]
-    dz=[(dp,zz) for zz in zs]
-    greet([sib,dx,dy]+dz)
+    zb=lax.rem(z,2); pe=z+1-2*zb; mo=2-z//2; zo=2-2*(z//2)
+    inner=(z==1)|(z==2); outer=(z==0)|(z==3)
+    dpe=(dp,pe); dmo=(dp,mo)
+    greet([sib,dx,dy]+[(dp,lax.rem(z+k,4)) for k in (1,2,3)])
     def cs(t): return pl.ds(cols[t][0],cols[t][1])
+    def wr(t): return (w1,w2)[t] if t<2 else w.at[t-2]
     def s0(t,recv=False):
-        return remote(wp.at[1-c,:,cs(t)], w.at[(dp+1-2*c) if recv else dp,z,:,cs(t)], s0s.at[t], s0r.at[t], sib)
-    def keep(t): return pltpu.make_async_copy(wp.at[c,:,cs(t)], w.at[dp,z,:,cs(t)], l0.at[t])
-    def s1(t,k,recv=False):
-        r=w.at[pl.ds(2*q,2), zf[k] if recv else z, :, cs(t)]
-        return remote(r,r,s1s.at[t,k],s1r.at[t,k],dz[k])
+        return remote(wp.at[1-c,:,cs(t)], wr(t).at[(dp+1-2*c) if recv else dp,z], s0s.at[t], s0r.at[t], sib)
+    def keep(t): return pltpu.make_async_copy(wp.at[c,:,cs(t)], wr(t).at[dp,z], l0.at[t])
+    def s1a(t,recv=False):
+        r=wr(t).at[pl.ds(2*q,2), pe if recv else z]
+        return remote(r,r,s1s.at[t,0],s1r.at[t,0],dpe)
+    def s1b(t):
+        r=wr(t).at[pl.ds(2*q,2), z]
+        return remote(r,r,s1s.at[t,1],s1r.at[t,1+zb],dmo)
+    def s1bw(t,k):
+        r=wr(t).at[pl.ds(2*q,2), zo+k]
+        return remote(r,r,s1s.at[t,1],s1r.at[t,1+k],dmo)
+    def s1c(t):
+        r=wr(t).at[pl.ds(2*q,2), pl.ds(zo,2)]
+        return remote(r,r,s1s.at[t,2],s1r.at[t,3],dpe)
     def s2(t,a,recv=False):
-        r=w.at[pl.ds(2*((qx,qy)[a] if recv else q),2),:,:,cs(t)]
+        r=wr(t).at[pl.ds(2*((qx,qy)[a] if recv else q),2)]
         return remote(r,r,s2s.at[t,a],s2r.at[t,a],dxy[a])
     def s3(t,a,recv=False):
-        r=w.at[2*(qd if recv else (qy,qx)[a])+a,:,:,cs(t)]
+        r=wr(t).at[2*(qd if recv else (qy,qx)[a])+a]
         return remote(r,r,s3s.at[t,a],s3r.at[t,a],dxy[a])
-    def hz(k,recv=False): return remote(hid,hrow.at[c,zf[k] if recv else z],hs.at[k],hr.at[k],dz[k])
+    hp=hrow.shape[2]//h_parts
+    def ht(p): return pl.ds(p*hp,hp)
+    def ha(p,recv=False): return remote(hid.at[ht(p)],hrow.at[c,pe if recv else z,ht(p)],hs.at[p,0],hr.at[p,0],dpe)
+    def hb(p): return remote(hid.at[ht(p)],hrow.at[c,z,ht(p)],hs.at[p,1],hr.at[p,1+zb],dmo)
+    def hbw(p,k): return remote(hid.at[ht(p)],hrow.at[c,zo+k,ht(p)],hs.at[p,1],hr.at[p,1+k],dmo)
+    def hc(p):
+        r=hrow.at[c,pl.ds(zo,2),ht(p)]
+        return remote(r,r,hs.at[p,2],hr.at[p,3],dpe)
     done=set()
     def once(*k):
         if k in done: return False
@@ -319,10 +337,18 @@
     def start1(t):
         if t<n and once(1,t):
             keep(t).wait(); s0(t,True).wait_recv()
-            for k in range(3): s1(t,k).start()
+            s1a(t).start(); s1b(t).start()
+    def forward(t):
+        if t<n and once(5,t):
+            @pl.when(inner)
+            def _():
+                s1bw(t,0).wait_recv(); s1bw(t,1).wait_recv(); s1c(t).start()
     def start2(t):
+        forward(t)
         if t<n and once(2,t):
-            for k in range(3): s1(t,k,True).wait_recv()
+            s1a(t,True).wait_recv()
+            @pl.when(outer)
+            def _(): s1c(t).wait_recv()
             for a in range(2): s2(t,a).start()
     def start3(t):
         if 0<=t<n and once(3,t):
@@ -332,26 +358,39 @@
         if 0<=t<n and once(4,t):
             for a in range(2): s3(t,a,True).wait_recv()
     def advance(t):
-        start1(t+2); start2(t); start3(t-1); finish(t-2)
+        for u in range(t+4): start1(u)
+        for f,u in ((forward,t+1),(start2,t),(start3,t-1),(finish,t-2)):
+            for v in range(u+1): f(v)
+    def h_go(p): ha(p).start(); hb(p).start()
+    def h_on(p):
+        @pl.when(inner)
+        def _():
+            hbw(p,0).wait_recv(); hbw(p,1).wait_recv(); hc(p).start()
     keep_h=pltpu.make_async_copy(hid,hrow.at[c,z],ll.at[0]); keep_h.start()
     keep_c=pltpu.make_async_copy(cot,cotv.at[c],ll.at[1]); keep_c.start()
     keep_r=pltpu.make_async_copy(segr,sr.at[c],ll.at[2]); keep_r.start()
     keep_s=pltpu.make_async_copy(segc,sc.at[c],ll.at[3]); keep_s.start()
-    for t in range(2): s0(t).start(); keep(t).start()
+    for t in range(3): s0(t).start(); keep(t).start()
+    give_h=[remote(hid,hrow.at[c,z],xs.at[3],xr.at[3],sib)]; give_h[0].start()
     give_c=remote(cot,cotv.at[c],xs.at[0],xr.at[0],sib); give_c.start()
     give_r=remote(segr,sr.at[c],xs.at[1],xr.at[1],sib); give_r.start()
     give_s=remote(segc,sc.at[c],xs.at[2],xr.at[2],sib); give_s.start()
-    for t in range(2,n): s0(t).start(); keep(t).start()
-    start1(0); start1(1)
-    for k in range(3): hz(k).start()
-    advance(0); advance(1)
-    start3(1); finish(0); finish(1)
-    load_a=pltpu.make_async_copy(w.at[:,:,:,pl.ds(0,1664)],wa,ll.at[4]); load_a.start()
+    for t in range(3,n): s0(t).start(); keep(t).start()
+    start1(0); start1(1); start1(2); h_go(0)
+    forward(0); start2(0); forward(1); start2(1); forward(2)
+    h_on(0); start1(3); h_go(1)
+    start3(0); start2(2)
     keep_h.wait(); keep_c.wait(); keep_r.wait(); keep_s.wait()
     remote(segr,sr.at[1-c],xs.at[1],xr.at[1],sib).wait_recv()
     remote(segc,sc.at[1-c],xs.at[2],xr.at[2],sib).wait_recv()
     remote(cot,cotv.at[1-c],xs.at[0],xr.at[0],sib).wait_recv()
-    load_a.wait()
+    remote(hid,hrow.at[1-c,z],xs.at[3],xr.at[3],sib).wait_recv()
+    start3(1); forward(3); h_on(1); start1(4); h_go(2)
+    finish(0); finish(1)
+    load_a=[pltpu.make_async_copy(w1,wa.at[:,:,:,pl.ds(0,768)],ll.at[4]),pltpu.make_async_copy(w2,wa.at[:,:,:,pl.ds(768,896)],ll.at[11])]
+    for l in load_a: l.start()
+    start3(2); start2(3); forward(4); h_on(2); start1(5); h_go(3)
+    for l in load_a: l.wait()
     def wcol(a,b): return wa[:,:,:,a:b].reshape(1536,b-a)
     pick=(lanes((8,128))==lax.broadcasted_iota(jnp.int32,(8,128),0)).astype(low)
     gs[...]=dot_nt(pick,wcol(1536,1664))
@@ -359,11 +398,25 @@
         lt[2,:,pl.ds(pl.multiple_of(i*128,128),128)]=cotv[i//2,pl.ds(pl.multiple_of(lax.rem(i,2)*128,128),128),:].astype(f32).T.astype(low)
         return 0
     lax.fori_loop(0,4,transpose_cot,0)
-    for k in range(3): hz(k,True).wait_recv()
-    give_h=remote(hrow.at[c],hrow.at[c],xs.at[3],xr.at[3],sib); give_h.start()
     def normed(v,row):
         s=lax.rsqrt(jnp.mean(v*v,axis=-1,keepdims=True)+epsilon)
         return v*s*gs[row:row+1,:]
+    def queries(i,_):
+        a=pl.ds(pl.multiple_of(lax.rem(i,2)*128,128),128)
+        v=normed(hrow[i//2,z,a,:].astype(f32),0)
+        d=pl.ds(pl.multiple_of(i*128,128),128)
+        qq[d,:]=dot(v.astype(low),wcol(0,384)).astype(low)
+        lt[0,:,d]=v.T.astype(low)
+        return 0
+    lax.fori_loop(0,4,queries,0)
+    start2(4); start3(3); finish(2); forward(5); h_on(3)
+    for p in range(h_parts):
+        ha(p,True).wait_recv()
+        @pl.when(outer)
+        def _(): hc(p).wait_recv()
+    for k in (1,2,3):
+        r=hrow.at[c,lax.rem(z+k,4)]
+        g=remote(r,r,xs.at[6+k],xr.at[6+k],sib); g.start(); give_h.append(g)
     def keys_of(r):
         def body(i,_):
             a=pl.ds(pl.multiple_of(lax.rem(i,2)*128,128),128)
@@ -374,18 +427,12 @@
             return 0
         lax.fori_loop(0,8,body,0)
     keys_of(c)
-    remote(hrow.at[1-c],hrow.at[1-c],xs.at[3],xr.at[3],sib).wait_recv()
-    advance(2)
+    for k in (1,2,3):
+        r=hrow.at[1-c,lax.rem(z+k,4)]
+        remote(r,r,xs.at[6+k],xr.at[6+k],sib).wait_recv()
+    advance(5)
     keys_of(1-c)
-    def queries(i,_):
-        a=pl.ds(pl.multiple_of(lax.rem(i,2)*128,128),128)
-        v=normed(hrow[i//2,z,a,:].astype(f32),0)
-        d=pl.ds(pl.multiple_of(i*128,128),128)
-        qq[d,:]=dot(v.astype(low),wcol(0,384)).astype(low)
-        lt[0,:,d]=v.T.astype(low)
-        return 0
-    lax.fori_loop(0,4,queries,0)
-    advance(3)
+    advance(6)
     for h in range(6):
         pair=pl.ds(128*(h//2),128); odd=h%2
         bias[...]=pltpu.roll(jnp.broadcast_to(base[h:h+1,:],(256,1280)),1024,1,stride=1,stride_axis=0)
@@ -406,13 +453,13 @@
             lse[r,a,:]=jnp.where(lanes((128,128))==h,m+jnp.log(l),lse[r,a,:]) if h else jnp.broadcast_to(m+jnp.log(l),(128,128))
             return 0
         lax.fori_loop(0,4,attend,0)
-        if h in (1,3): advance(4+h//2)
+        if h in (1,3): advance(7+h//2)
     def project(i,_):
         part[i//2,pl.ds(pl.multiple_of(lax.rem(i,2)*128,128),128),:]=dot_nt(mx[pl.ds(pl.multiple_of(i*128,128),128),:],wcol(1152,1536))
         return 0
     lax.fori_loop(0,4,project,0)
     give_p=remote(part,r1,xs.at[4],xr.at[4],sib); give_p.start()
-    outs=[pltpu.make_async_copy(a,b,lo.at[i]) for i,(a,b) in enumerate(((qq,q_o),(kk,kk_o),(vv,vv_o),(mx,mx_o),(lse,lse_o),(sr,segr_o),(sc,segc_o)))]
+    outs=[pltpu.make_async_copy(a,b,lo.at[i]) for i,(a,b) in enumerate(((qq,q_o),(kk,kk_o),(vv,vv_o),(mx,mx_o),(lse,lse_o),(sr,segr_o),(sc,segc_o),(cotv,cot_o)))]
     for o in outs: o.start()
     give_p.wait_recv()
     def middle(i,_):
@@ -427,12 +474,14 @@
     lax.fori_loop(0,4,middle,0)
     give_p.wait_send()
     give_lt=pltpu.make_async_copy(lt,lt_o,ll.at[5]); give_lt.start()
-    advance(6)
+    give_mid=pltpu.make_async_copy(mid,mid_o,ll.at[12]); give_mid.start()
+    gs_o[...]=gs[...]
+    advance(9)
     hout=[]
     for j in range(ff_steps):
         if j:
             for t in range(4+3*j,7+3*j): advance(t)
-        loads=[pltpu.make_async_copy(w.at[:,:,:,cs(2+3*j+i)],wf.at[i],ll.at[6+i]) for i in range(3)]
+        loads=[pltpu.make_async_copy(w.at[3*j+i],wf.at[i],ll.at[6+i]) for i in range(3)]
         for l in loads: l.start()
         b=j%2
         if j>=2: hout[j-2].wait()
@@ -454,36 +503,23 @@
             yy[i]=yp; part[i]=gp
             return 0
         lax.fori_loop(0,2,feed,0)
-        o=pltpu.make_async_copy(hd.at[b],hdg_o.at[:,:,pl.ds(512*j,512)],lo.at[7+b]); o.start(); hout.append(o)
-    give_g=remote(part,r2,xs.at[5],xr.at[5],sib); give_g.start()
-    give_y=remote(yy.at[1-c],r3,xs.at[6],xr.at[6],sib); give_y.start()
-    give_g.wait_recv()
-    give_g.wait_send()
-    def gradient(i,acc):
-        a=pl.ds(pl.multiple_of(lax.rem(i,2)*128,128),128); r=i//2
-        v=mid[r,a,:]; gn=part[r,a,:]+r2[r,a,:]
-        s=lax.rsqrt(jnp.mean(v*v,axis=-1,keepdims=True)+epsilon)
-        wg=gn*gs[1:2,:]
-        part[r,a,:]=cotv[r,a,:].astype(f32)+(s*wg-v*(s*s*s)*jnp.mean(wg*v,axis=-1,keepdims=True))
-        return acc+jnp.where(r==c,1.0,0.0)*jnp.sum(gn*v*s,axis=0,keepdims=True)
-    acc=lax.fori_loop(0,4,gradient,jnp.zeros((1,1536),f32))
-    ggf_o[0:8,:]=jnp.broadcast_to(acc,(8,1536))
-    ggf_o[8:16,:]=gs[...]
-    give_m=pltpu.make_async_copy(part,gmid_o,ll.at[9]); give_m.start()
-    give_y.wait_recv(); give_y.wait_send()
-    def final(i,_):
-        a=pl.ds(pl.multiple_of(i*128,128),128)
-        yy[c,a,:]=mid[c,a,:]+(yy[c,a,:]+r3[a,:])
-        return 0
-    lax.fori_loop(0,2,final,0)
-    give_b=pltpu.make_async_copy(yy.at[c],bo_o,ll.at[10]); give_b.start()
+        o=pltpu.make_async_copy(hd.at[b],hdg_o.at[:,:,pl.ds(512*j,512)],lo.at[8+b]); o.start(); hout.append(o)
+    give_m=[pltpu.make_async_copy(part,gnf_o,ll.at[9]),pltpu.make_async_copy(yy,yy_o,ll.at[10])]
+    for g in give_m: g.start()
     for o in outs+hout[-2:]: o.wait()
-    give_lt.wait(); give_m.wait(); give_b.wait()
-    give_c.wait_send(); give_r.wait_send(); give_s.wait_send(); give_h.wait_send()
-    for k in range(3): hz(k).wait_send()
+    give_lt.wait(); give_mid.wait()
+    for g in give_m: g.wait()
+    give_c.wait_send(); give_r.wait_send(); give_s.wait_send()
+    for g in give_h: g.wait_send()
+    for p in range(h_parts):
+        ha(p).wait_send(); hb(p).wait_send()
+        @pl.when(inner)
+        def _(): hc(p).wait_send()
     for t in range(n):
         s0(t).wait_send()
-        for k in range(3): s1(t,k).wait_send()
+        s1a(t).wait_send(); s1b(t).wait_send()
+        @pl.when(inner)
+        def _(): s1c(t).wait_send()
         for a in range(2): s2(t,a).wait_send(); s3(t,a).wait_send()
 
 def forward_call(wp, hid, cot, segr, segc, base, ff_steps, cid=0):
@@ -491,16 +527,16 @@
     S=jax.ShapeDtypeStruct; V=pltpu.VMEM; D=pltpu.SemaphoreType.DMA
     fw=512*ff_steps
     hbm=pl.BlockSpec(memory_space=pltpu.HBM); vm=pl.BlockSpec(memory_space=pltpu.VMEM)
-    outs=(S((8,4,48,wp.shape[2]),low),S((3,1536,512),low),S((3,512,fw),low),S((512,384),low),S((2,1024,384),low),S((2,1024,384),low),
-          S((512,384),low),S((2,256,128),f32),S((2,256,1536),f32),S((256,1536),f32),S((16,1536),f32),S((2,8,1024),f32),S((2,256,128),f32))
-    ospec=[hbm]*13; ospec[10]=vm
+    outs=(S((8,4,48,768),low),S((8,4,48,896),low),S((3*ff_steps,8,4,48,512),low),S((3,1536,512),low),S((3,512,fw),low),S((512,384),low),S((2,1024,384),low),S((2,1024,384),low),
+          S((512,384),low),S((2,256,128),f32),S((2,256,1536),f32),S((2,256,1536),f32),S((8,1536),f32),S((2,8,1024),f32),S((2,256,128),f32),S((2,256,1536),f32),S((2,256,1536),low))
+    ospec=[hbm]*17; ospec[12]=vm
     scratch=[V((2,4,256,1536),low),V((2,256,1536),low),V((2,8,1024),f32),V((2,256,128),f32),V((8,4,48,1664),low),V((3,8,4,48,512),low),
              V((512,384),low),V((2,1024,384),low),V((2,1024,384),low),V((512,384),low),V((2,256,128),f32),V((256,1280),f32),
              V((2,256,1536),f32),V((2,256,1536),f32),V((512,1536),low),V((2,3,512,512),low),V((2,256,1536),f32),V((3,1536,512),low),V((8,1536),f32),
-             V((2,256,1536),f32),V((2,256,1536),f32),V((256,1536),f32),
-             D((n,)),D((n,)),D((n,)),D((n,3)),D((n,3)),D((n,2)),D((n,2)),D((n,2)),D((n,2)),D((3,)),D((3,)),D((7,)),D((7,)),D((11,)),D((9,))]
+             V((2,256,1536),f32),
+             D((n,)),D((n,)),D((n,)),D((n,3)),D((n,4)),D((n,2)),D((n,2)),D((n,2)),D((n,2)),D((h_parts,3)),D((h_parts,4)),D((10,)),D((10,)),D((13,)),D((10,))]
     return pl.pallas_call(functools.partial(forward_kernel,ff_steps),out_shape=outs,
-        in_specs=[hbm]*5+[vm],out_specs=tuple(ospec),scratch_shapes=scratch,
+        in_specs=[vm]+[hbm]*4+[vm],out_specs=tuple(ospec),scratch_shapes=scratch,
         compiler_params=pltpu.CompilerParams(collective_id=cid,has_side_effects=True,vmem_limit_bytes=62*2**20))(wp,hid,cot,segr,segc,base)
 
 def dot_tn(a,b):
@@ -508,17 +544,32 @@
 
 part_slots=2
 sum_slots=3
-def backward_kernel(chunks, ff_steps, w, lt_h, hdg, q_h, kk_h, vv_h, mx_h, lse_h, gmid, segr_h, segc_h, hid_h, base, rows, spots, tile,
-                    out, gin_o, *rest):
+lag=6
+def backward_kernel(chunks, ff_steps, w1, w2, lt_h, hdg, q_h, kk_h, vv_h, mx_h, lse_h, gnf_h, yy_h, mid_h, cot_h, segr_h, segc_h, hid_h, base, gains, spots, tile,
+                    out, gin_o, bo_o, xg, xy, *rest):
     n=len(chunks)
     ra1=rest[0:n]; rb1=rest[n:2*n]; ra2=rest[2*n:3*n]; rb2=rest[3*n:4*n]; rz=rest[4*n:5*n]
-    (fin,p,lt,gat,rbuf,wa,qq,kk,vv,mx,gm,lse,sr,sc,bias,dbias,dq,acc,dkv,rkv,dk,dv,part,r3,gin,hid,dtab,ext,
-     ll,lr,lo,s1,v1,s2,v2,s3,v3,s4,v4,ks,kr,xs,xr)=rest[5*n:]
+    (fin,p,lt,gat,rbuf,wa,qq,kk,vv,mx,gm,lse,sr,sc,bias,dbias,dq,acc,dkv,rka,rkb,rkc,dk,dv,part,r3,hid,dtab,ext,cb,
+     ll,lr,lo,s1,v1,s2,v2,s3,v3,s4,v4,ks,kr,xs,xr,lb)=rest[5*n:]
     dp,z,c,x,y=peers_of()
     sib=(dp+1-2*c,z); dx=(dp+2-4*x,z); dy=(lax.rem(dp+4,8),z)
     zs=[lax.rem(z+k,4) for k in (1,2,3)]; dz=[(dp,zz) for zz in zs]
+    zb=lax.rem(z,2); pe=z+1-2*zb; mo=2-z//2; zo=2-2*(z//2)
+    inner=(z==1)|(z==2); outer=(z==0)|(z==3)
+    def ka(pp,recv=False): return remote(dkv.at[pp,pe],rka.at[pp],ks.at[pp,0],kr.at[pp,0],(dp,pe))
+    def kc(pp): return remote(dkv.at[pp,pl.ds(zo,2)],rkc.at[pp],ks.at[pp,1],kr.at[pp,1],(dp,pe))
+    def kb(pp,k): return remote(dkv.at[pp,zo+k],rkb.at[pp],ks.at[pp,2+k],kr.at[pp,2],(dp,zo+k))
+    def relay(pp):
+        @pl.when(inner)
+        def _():
+            kc(pp).wait_recv()
+            for k in range(2):
+                for j in range(2):
+                    for r in range(2):
+                        dkv[pp,zo+k,j,r]=(dkv[pp,zo+k,j,r].astype(f32)+rkc[pp,k,j,r].astype(f32)).astype(low)
+                kb(pp,k).start()
     loads=[pltpu.make_async_copy(a,b,ll.at[i]) for i,(a,b) in enumerate((
-        (lt_h.at[pl.ds(1,2)],lt),(gmid,part),(w.at[:,:,:,pl.ds(1152,384)],wa.at[:,:,:,pl.ds(0,384)]),(q_h,qq),(kk_h,kk),(vv_h,vv),(mx_h,mx),(lse_h,lse),(segr_h,sr),(segc_h,sc),(hid_h,hid),(gmid.at[c],gin)))]
+        (lt_h.at[pl.ds(1,2)],lt),(w2.at[:,:,:,pl.ds(384,384)],wa.at[:,:,:,pl.ds(0,384)]),(q_h,qq),(kk_h,kk),(vv_h,vv),(mx_h,mx),(lse_h,lse),(segr_h,sr),(segc_h,sc),(hid_h,hid)))]
     for l in loads: l.start()
     slots=rbuf.shape[0]
     def fetch(t):
@@ -596,27 +647,46 @@
         a=remote(fin.at[b,1-c,:,pl.ds(0,wd)],out.at[c,:,cols],s4.at[t],v4.at[t],sib)
         e=pltpu.make_async_copy(fin.at[b,c,:,pl.ds(0,wd)],out.at[c,:,cols],lo.at[t])
         a.start(); e.start(); c4[t]=(a,e)
-    def step(t):
-        for k,f in ((0,stage1),(1,stage2),(2,stage3),(3,stage4)):
-            if 0<=t-k<n and once(k,t-k): f(t-k)
+    def step(s):
+        for f,t in ((stage2,s),(stage1,s+2),(stage3,s-1),(stage4,s-lag)):
+            if 0<=t<n and once(f.__name__,t): f(t)
+    give_g=remote(gnf_h,xg,xs.at[1],xr.at[1],sib); give_g.start()
+    give_y=remote(yy_h.at[1-c],xy,xs.at[2],xr.at[2],sib); give_y.start()
     loads[0].wait()
-    step(0)
+    stage1(0); stage1(1); once("stage1",0); once("stage1",1)
     for l in loads[1:]: l.wait()
     def wcol(a,b): return wa[:,:,:,a:b].reshape(1536,b-a)
-    def mixed_grad(i,_):
-        a=pl.ds(pl.multiple_of(lax.rem(i,2)*128,128),128); d=pl.ds(pl.multiple_of(i*128,128),128)
-        v=part[i//2,a,:]
-        gat[:,d]=v.T.astype(low)
-        gm[d,:]=dot(v.astype(low),wcol(0,384)).astype(low)
-        return 0
-    lax.fori_loop(0,4,mixed_grad,0)
-    load_w=pltpu.make_async_copy(w.at[:,:,:,pl.ds(0,1152)],wa,ll.at[13]); load_w.start()
-    step(1)
+    give_g.wait_recv()
+    total=jnp.zeros((1,1536),f32)
+    for i in range(4):
+        r=i//2; a=pl.ds(128*(i%2),128); d=pl.ds(128*i,128)
+        first=part.at[0,pl.ds(0,128)]; second=part.at[0,pl.ds(128,128)]; third=part.at[1,pl.ds(0,128)]
+        moves=[pltpu.make_async_copy(f,g,lb.at[k]) for k,(f,g) in enumerate(((mid_h.at[r,a],first),(gnf_h.at[r,a],second),(xg.at[r,a],third),(cot_h.at[r,a],cb)))]
+        for m in moves: m.start()
+        for m in moves: m.wait()
+        v=part[0,0:128,:]; gn=part[0,128:256,:]+part[1,0:128,:]
+        s=lax.rsqrt(jnp.mean(v*v,axis=-1,keepdims=True)+epsilon)
+        wg=gn*gains[1:2,:]
+        g=cb[...].astype(f32)+(s*wg-v*(s*s*s)*jnp.mean(wg*v,axis=-1,keepdims=True))
+        total=total+jnp.where(c==r,1.0,0.0)*jnp.sum(gn*v*s,axis=0,keepdims=True)
+        part[1,128:256,:]=g
+        @pl.when(c==r)
+        def _():
+            back=pltpu.make_async_copy(part.at[1,pl.ds(128,128)],gin_o.at[a],lb.at[4]); back.start(); back.wait()
+        gat[:,d]=g.T.astype(low)
+        gm[d,:]=dot(g.astype(low),wcol(0,384)).astype(low)
+    ext[...]=jnp.zeros((128,1536),f32)
+    def spread(v,row):
+        upper=v.astype(low)
+        ext[row:row+8,:]=upper.astype(f32)
+        ext[row+8:row+16,:]=v-upper.astype(f32)
+    spread(jnp.broadcast_to(total,(8,1536)),32)
+    load_w=[pltpu.make_async_copy(w1,wa.at[:,:,:,pl.ds(0,768)],ll.at[13]),pltpu.make_async_copy(w2.at[:,:,:,pl.ds(0,384)],wa.at[:,:,:,pl.ds(768,384)],ll.at[15])]
+    for l in load_w: l.start()
+    step(0)
     dbias[...]=jnp.zeros((256,1280),f32)
-    ext[...]=jnp.zeros((128,1536),f32)
     dtab[...]=jnp.zeros((8,1280),f32)
-    gives=[]
-    at=2
+    at=1
     for h in range(6):
         odd=h%2; pair=pl.ds(128*(h//2),128); pp=h//2
         bias[...]=pltpu.roll(jnp.broadcast_to(base[h:h+1,:],(256,1280)),1024,1,stride=1,stride_axis=0)
@@ -651,33 +721,39 @@
             for j in range(2):
                 for r in range(2):
                     for zz in range(4):
-                        dkv[zz,pp,j,r]=acc[j,r,256*zz:256*zz+256,:].astype(low)
-            for k in range(3):
-                g=remote(dkv.at[zs[k],pp],rkv.at[k,pp],ks.at[pp,k],kr.at[pp,k],dz[k]); g.start(); gives.append(g)
+                        dkv[pp,zz,j,r]=acc[j,r,256*zz:256*zz+256,:].astype(low)
+            ka(pp).start()
+            @pl.when(outer)
+            def _(): kc(pp).start()
             step(at); at+=1
+            if pp: relay(pp-1)
     tab=dtab[...]
     high=tab.astype(low); rest1=tab-high.astype(f32); mid1=rest1.astype(low); last=(rest1-mid1.astype(f32)).astype(low)
     found=dot(high,spots[...])+dot(mid1,spots[...])+dot(last,spots[...])
-    def spread(v,row):
-        upper=v.astype(low)
-        ext[row:row+8,:]=upper.astype(f32)
-        ext[row+8:row+16,:]=v-upper.astype(f32)
     upper=found.astype(low)
     ext[0:8,:]=dot(upper,tile[...])
     ext[8:16,:]=dot((found-upper.astype(f32)).astype(low),tile[...])
-    spread(rows[0:8,:],32)
+    give_y.wait_recv()
+    for i in range(2):
+        a=pl.ds(128*i,128)
+        first=part.at[0,pl.ds(0,128)]; second=part.at[0,pl.ds(128,128)]; third=part.at[1,pl.ds(0,128)]
+        moves=[pltpu.make_async_copy(f,g,lb.at[k]) for k,(f,g) in enumerate(((mid_h.at[c,a],first),(yy_h.at[c,a],second),(xy.at[a],third)))]
+        for m in moves: m.start()
+        for m in moves: m.wait()
+        part[1,128:256,:]=part[0,0:128,:]+(part[0,128:256,:]+part[1,0:128,:])
+        back=pltpu.make_async_copy(part.at[1,pl.ds(128,128)],bo_o.at[a],lb.at[4]); back.start(); back.wait()
     step(at); at+=1
-    step(at); at+=1
-    step(at); at+=1
-    for g in gives: g.wait_recv()
+    relay(2)
+    while at<9:
+        step(at); at+=1
     for pp in range(3):
+        ka(pp).wait_recv(); kb(pp,0).wait_recv()
         for j,o in enumerate((dk,dv)):
             for r in range(2):
-                v=dkv[z,pp,j,r].astype(f32)
-                for k in range(3): v=v+rkv[k,pp,j,r].astype(f32)
+                v=dkv[pp,z,j,r].astype(f32)+rka[pp,j,r].astype(f32)+rkb[pp,j,r].astype(f32)
                 o[256*r:256*r+256,128*pp:128*pp+128]=v.astype(low)
     step(at); at+=1
-    load_w.wait()
+    for l in load_w: l.wait()
     def input_grad(i,_):
         d=pl.ds(pl.multiple_of(i*128,128),128); a=pl.ds(pl.multiple_of(lax.rem(i,2)*128,128),128)
         part[i//2,a,:]=dot_nt(dq[d,:],wcol(0,384))+dot_nt(dk[d,:],wcol(384,768))+dot_nt(dv[d,:],wcol(768,1152))
@@ -685,18 +761,20 @@
     lax.fori_loop(0,4,input_grad,0)
     give=remote(part.at[1-c],r3,xs.at[0],xr.at[0],sib); give.start()
     step(at); at+=1
-    give.wait_recv()
+    give.wait_send()
+    load_i=pltpu.make_async_copy(gin_o,part.at[1-c],lb.at[0]); load_i.start()
+    give.wait_recv(); load_i.wait()
     def last_grad(i,total):
         a=pl.ds(pl.multiple_of(i*128,128),128)
         v=hid[a,:].astype(f32); gn=part[c,a,:]+r3[a,:]
         s=lax.rsqrt(jnp.mean(v*v,axis=-1,keepdims=True)+epsilon)
-        wg=gn*rows[8:9,:]
-        gin[a,:]=gin[a,:]+(s*wg-v*(s*s*s)*jnp.mean(wg*v,axis=-1,keepdims=True))
+        wg=gn*gains[0:1,:]
+        part[1-c,a,:]=part[1-c,a,:]+(s*wg-v*(s*s*s)*jnp.mean(wg*v,axis=-1,keepdims=True))
         return total+jnp.sum(gn*v*s,axis=0,keepdims=True)
     total=lax.fori_loop(0,2,last_grad,jnp.zeros((1,1536),f32))
     spread(jnp.broadcast_to(total,(8,1536)),16)
-    give_i=pltpu.make_async_copy(gin,gin_o,ll.at[12]); give_i.start()
-    while at<n+3:
+    give_i=pltpu.make_async_copy(part.at[1-c],gin_o,ll.at[12]); give_i.start()
+    while at<n+lag:
         step(at); at+=1
     for t in range(n):
         off,wd=chunks[t][1:3]; cols=pl.ds(off,wd)
@@ -707,8 +785,13 @@
             for d in c1[t]: d.wait_send()
         for d in c2[t]: d.wait_send()
         for d in c3[t]: d.wait_send()
-    for g in gives: g.wait_send()
-    give.wait_send(); give_i.wait()
+    for pp in range(3):
+        ka(pp).wait_send()
+        @pl.when(outer)
+        def _(): kc(pp).wait_send()
+        @pl.when(inner)
+        def _(): kb(pp,0).wait_send(); kb(pp,1).wait_send()
+    give_i.wait(); give_g.wait_send(); give_y.wait_send()
 
 def backward_chunks(ff_steps):
     fw=512*ff_steps
@@ -719,7 +802,7 @@
     chunks+=[(3,o,384,("ref",0,0)),(1,o+384,384,("ref",1,0)),(1,o+768,384,("ref",2,0)),(1,o+1152,384,("ref",3,0)),(1,o+1536,128,("ref",4,0))]
     return chunks
 
-def backward_call(w,lt,hdg,q,kk,vv,mx,lse,gmid,segr,segc,hid,base,rows,spots,tile,ff_steps,cid=1):
+def backward_call(w1,w2,lt,hdg,q,kk,vv,mx,lse,gnf,yy,mid,cot,segr,segc,hid,base,gains,spots,tile,ff_steps,cid=1):
     chunks=backward_chunks(ff_steps); n=len(chunks)
     C=3*512*ff_steps+1664
     S=jax.ShapeDtypeStruct; V=pltpu.VMEM; D=pltpu.SemaphoreType.DMA
@@ -728,12 +811,12 @@
     scratch=[V((2,4,48,k),low) for k in ws]*1+[V((2,4,48,k),low) for k in ws]+[V((4,48,k),low) for k in ws]+[V((4,48,k),low) for k in ws]+[V((3,2,48,k),low) for k in ws]
     scratch+=[V((sum_slots,2,48,512),f32),V((part_slots,2,2,2,4,48,512),low),V((2,1536,512),low),V((1536,512),low),V((2,512,512),low),V((8,4,48,1152),low),
       V((512,384),low),V((2,1024,384),low),V((2,1024,384),low),V((512,384),low),V((512,384),low),V((2,256,128),f32),V((2,8,1024),f32),V((2,256,128),f32),
-      V((256,1280),f32),V((256,1280),f32),V((512,384),low),V((2,2,1024,128),f32),V((4,3,2,2,256,128),low),V((3,3,2,2,256,128),low),V((512,384),low),V((512,384),low),
-      V((2,256,1536),f32),V((256,1536),f32),V((256,1536),f32),V((256,1536),low),V((8,1280),f32),V((128,1536),f32)]
-    scratch+=[D((15,)),D((n,)),D((n,)),D((n,2)),D((n,2)),D((n,2)),D((n,2)),D((n,3,2)),D((n,3,2)),D((n,)),D((n,)),D((3,3)),D((3,3)),D((1,)),D((1,))]
-    return pl.pallas_call(functools.partial(backward_kernel,chunks,ff_steps),out_shape=(S((2,48,C),f32),S((256,1536),f32)),
-        in_specs=[hbm]*12+[vm]*4,out_specs=(hbm,hbm),scratch_shapes=scratch,
-        compiler_params=pltpu.CompilerParams(collective_id=cid,has_side_effects=True,vmem_limit_bytes=62*2**20))(w,lt,hdg,q,kk,vv,mx,lse,gmid,segr,segc,hid,base,rows,spots,tile)
+      V((256,1280),f32),V((256,1280),f32),V((512,384),low),V((2,2,1024,128),f32),V((3,4,2,2,256,128),low),V((3,2,2,256,128),low),V((3,2,2,256,128),low),V((3,2,2,2,256,128),low),V((512,384),low),V((512,384),low),
+      V((2,256,1536),f32),V((256,1536),f32),V((256,1536),low),V((8,1280),f32),V((128,1536),f32),V((128,1536),low)]
+    scratch+=[D((16,)),D((n,)),D((n,)),D((n,2)),D((n,2)),D((n,2)),D((n,2)),D((n,3,2)),D((n,3,2)),D((n,)),D((n,)),D((3,4)),D((3,3)),D((3,)),D((3,)),D((5,))]
+    return pl.pallas_call(functools.partial(backward_kernel,chunks,ff_steps),out_shape=(S((2,48,C),f32),S((256,1536),f32),S((256,1536),f32),S((2,256,1536),f32),S((256,1536),f32)),
+        in_specs=[hbm]*16+[vm]*4,out_specs=(hbm,)*5,scratch_shapes=scratch,
+        compiler_params=pltpu.CompilerParams(collective_id=cid,has_side_effects=True,vmem_limit_bytes=62*2**20))(w1,w2,lt,hdg,q,kk,vv,mx,lse,gnf,yy,mid,cot,segr,segc,hid,base,gains,spots,tile)
 
 def cut(v,h,w):
     n=v.shape[1]
@@ -773,10 +856,10 @@
     steps=4; fw=512*steps; ff=wg.shape[1]
     wp=pack(wq,wk,wv,wo,ga,gf,wg,wu,wd,steps)
     r,s=seg_ids(seg); b,oh=base_of(tab)
-    w,lt,hdg,q,kk,vv,mx,lse,gmid,bo,rows,segr,segc=forward_call(wp,hid[0],cot[0],r,s,b,steps)
+    w1,w2,w,lt,hdg,q,kk,vv,mx,lse,gnf,yy,gains,segr,segc,mid,cot2=forward_call(wp,hid[0],cot[0],r,s,b,steps)
     spots=jnp.pad(oh,((0,0),(0,96))).astype(jnp.bfloat16)
     tile=(jnp.arange(1536)[None,:]%48==jnp.arange(128)[:,None]).astype(jnp.bfloat16)
-    o,gin=backward_call(w,lt,hdg,q,kk,vv,mx,lse,gmid,segr,segc,hid[0],b,rows,spots,tile,steps)
+    o,gin,bo,_,_=backward_call(w1,w2,lt,hdg,q,kk,vv,mx,lse,gnf,yy,mid,cot2,segr,segc,hid[0],b,gains,spots,tile,steps)
     e=3*fw+1536
     i=3*fw
     ext=o[:,:,e:]

time: 587 us -> 529 us (0.901); the launches traced: 586 us -> 519 us
  Pallas kernels: 562 us -> 482 us
  local copies, waits for them, and re-layouts: 10.6 us -> 24.7 us
    pallas_call x1, Pallas kernels: 267 us -> 225 us  [backward_call(): pl.pallas_call(functools.partial(backward_kernel, chunks, ff_steps), out_...]
    pallas_call x1, Pallas kernels: 294 us -> 258 us  [forward_call(): pl.pallas_call(functools.partial(forward_kernel, ff_steps), out_shape=out...]
    unnamed x42 -> x32, local copies, waits for them, and re-layouts: 4.02 us -> 17.7 us
where the time goes in v4:
time: 529 us; the launch traced here: 519 us
  Pallas kernels  482 us (91%)
  local copies, waits for them, and re-layouts  24.7 us (5%)
  other arithmetic  9.93 us (2%)
    pallas_call x1, Pallas kernels, forward_call(): pl.pallas_call(functools.partial(forward_kernel, ff_steps), out_shape=out...  258 us
    pallas_call x1, Pallas kernels, backward_call(): pl.pallas_call(functools.partial(backward_kernel, chunks, ff_steps), out_...  225 us
    unnamed x32, local copies, waits for them, and re-layouts  17.7 us

profile of v4, /device:TPU:0, one launch (start us, length us, event | category | flops | bytes accessed | tf_op | source)
XLA Modules:
  0.0 518.6 jit_solution(282511161971364083)
XLA Ops:
  0.6 0.0 slice-start
  0.7 0.0 slice-start.1
  0.7 0.8 constant_dynamic-update-slice_fusion.16
  1.5 0.8 constant_dynamic-update-slice_fusion.15
  2.3 0.8 constant_dynamic-update-slice_fusion.14
  3.1 0.8 constant_dynamic-update-slice_fusion.13
  3.9 0.7 pad_maximum_fusion.8
  4.6 0.1 copy.31
  4.7 0.8 constant_dynamic-update-slice_fusion.11
  5.5 0.8 constant_dynamic-update-slice_fusion.10
  6.3 0.8 constant_dynamic-update-slice_fusion.9
  7.1 0.8 constant_dynamic-update-slice_fusion.8
  8.0 0.8 constant_dynamic-update-slice_fusion.7
  8.8 0.8 constant_dynamic-update-slice_fusion.6
  9.6 0.8 constant_dynamic-update-slice_fusion.5
  10.4 0.8 constant_dynamic-update-slice_fusion.4
  11.2 0.8 constant_dynamic-update-slice_fusion.3
  12.0 0.8 constant_dynamic-update-slice_fusion.2
  12.9 0.0 copy-start.3
  12.9 0.8 constant_dynamic-update-slice_fusion.1
  13.7 0.8 constant_dynamic-update-slice_fusion.23
  14.5 0.0 copy-start.2
  14.5 0.8 constant_dynamic-update-slice_fusion.22
  15.3 0.8 constant_dynamic-update-slice_fusion.21
  16.1 0.8 constant_dynamic-update-slice_fusion
  17.0 0.0 slice-done
  17.0 0.0 slice-done.1
  17.0 0.9 slice.303
  18.0 1.3 pad_maximum_fusion.wp
  19.3 0.0 copy-done.3
  19.3 0.5 fusion.19
  19.8 0.6 pad.29.base
  20.4 0.0 copy-done.2
  20.5 0.1 dynamic_slice.3
  20.5 0.8 broadcast_in_dim.32.segc
  21.3 0.6 broadcast_in_dim.17.segr
  21.9 257.6 %shard_map.220 = (bf16[8,4,48,768]{3,2,1,0:T(8,128)(2,1)}, bf16[8,4,48,896]{3,2,1,0:T(8,128)(2,1)}, bf16[12,8,4,48,512]{4,3,2,1,0:T(8,128)(2,1)}, bf16[3,1536,51...) custom-call(bf16[2,48,7808]{2,1,0:T(8,128)(2,1)} %pad_maximum_fusion, ...), custom_call_target="tpu_custom_call" | custom-call | tf_op jit(solution)/shard_map/pallas_call | solution.py:538
  279.5 0.2 iota_compare_fusion.1
  279.8 0.8 convert_convert_fusion.spots
  280.6 0.8 fusion.tile
  281.4 224.6 %shard_map.221 = (f32[2,48,7808]{2,1,0:T(8,128)}, f32[256,1536]{1,0:T(8,128)}, f32[256,1536]{1,0:T(8,128)}, f32[2,256,1536]{2,1,0:T(8,128)}, f32[256,1536]{1,0:T(8,128)}) custom-call(bf16[8,4,48,768]{3,2,1,0:T(8,128)(2,1)} %get-tuple-element.31.w1, bf16[8,4,48,896]{3,2,1,0:T(8,128)(2,1)} %get-tuple-element.32.w2, ...), custom_call_target="tpu_custom_call" | custom-call | tf_op jit(solution)/shard_map/pallas_call | solution.py:817
  506.1 1.7 slice_bitcast_fusion.1
  507.8 1.2 fusion.1
  509.0 0.0 copy-start.1
  509.0 0.9 pad_maximum_fusion.3
  510.0 0.9 slice_add_fusion
  510.9 0.1 pad_maximum_fusion.7
  510.9 0.7 copy.32
  511.6 0.0 copy-start
  511.6 1.3 slice_bitcast_fusion.7
  512.9 0.7 pad_maximum_fusion.6
  513.7 0.7 pad_maximum_fusion.4
  514.4 0.8 add_bitcast_fusion
  515.2 0.7 fusion.2
  515.9 0.0 copy-done.1
  515.9 1.1 copy.67
  517.0 0.0 copy-done
  517.0 1.1 copy.68
  (10 shorter events, 0.1 us)
Async XLA Ops:
  0.6 16.3 %slice-start = ((bf16[48,3968]{1,0:T(8,128)(2,1)}), bf16[48,1920]{1,0:T(8,128)(2,1)S(1)}, s32[]{:S(2)}) async-start(bf16[48,3968]{1,0:T(8,128)(2,1)} %param.22), calls=%async_computation | async-start | bytes 368640 | tf_op jit(solution)/shard_map/slice | solution.py:824
  0.7 16.3 %slice-start.1 = ((bf16[48,3968]{1,0:T(8,128)(2,1)}), bf16[48,1920]{1,0:T(8,128)(2,1)S(1)}, s32[]{:S(2)}) async-start(bf16[48,3968]{1,0:T(8,128)(2,1)} %param.23), calls=%async_computation.1 | async-start | bytes 368640 | tf_op jit(solution)/shard_map/slice | solution.py:824
  12.9 6.4 %copy-start.3 = (bf16[32,12]{0,1:T(8,128)(2,1)S(1)}, bf16[32,12]{0,1:T(8,128)(2,1)}, u32[]{:S(2)}) copy-start(bf16[32,12]{0,1:T(8,128)(2,1)} %param.20) | copy-start | bytes 2308
  14.5 5.9 %copy-start.2 = (s32[1,1024]{1,0:T(1,128)S(1)}, s32[1,1024]{1,0:T(1,128)}, u32[]{:S(2)}) copy-start(s32[1,1024]{1,0:T(1,128)} %param.14) | copy-start | bytes 12292
  509.0 6.8 %copy-start.1 = (f32[256,1536]{1,0:T(8,128)S(1)}, f32[256,1536]{1,0:T(8,128)}, u32[]{:S(2)}) copy-start(f32[256,1536]{1,0:T(8,128)} %get-tuple-element.47) | copy-start | bytes 4718596
  511.6 5.4 %copy-start = (f32[256,1536]{1,0:T(8,128)S(1)}, f32[256,1536]{1,0:T(8,128)}, u32[]{:S(2)}) copy-start(f32[256,1536]{1,0:T(8,128)} %get-tuple-element.48) | copy-start | bytes 4718596

commit v5 on v4

--- a/solution.py
+++ b/solution.py
@@ -286,9 +286,10 @@
 f32=jnp.float32
 
 h_parts=4
-def forward_kernel(ff_steps, wp, hid, cot, segr, segc, base,
+across_first=2
+def forward_kernel(ff_steps, w_q, w_k, w_v, w_o, w_g, w_u, w_d, gains, hid, cot, segr, segc, base,
                    w1, w2, w, lt_o, hdg_o, q_o, kk_o, vv_o, mx_o, lse_o, gnf_o, yy_o, gs_o, segr_o, segc_o, mid_o, cot_o,
-                   hrow, cotv, sr, sc, wa, wf, qq, kk, vv, mx, lse, bias, part, mid, n2, hd, yy, lt, gs, r1,
+                   hrow, cotv, sr, sc, wa, wf, qq, kk, vv, mx, lse, bias, part, mid, n2, hd, yy, lt, gs, r1, wp,
                    s0s, s0r, l0, s1s, s1r, s2s, s2r, s3s, s3r, hs, hr, xs, xr, ll, lo):
     cols=[(0,768),(768,896)]+[(1664+512*i,512) for i in range(3*ff_steps)]
     n=len(cols)
@@ -304,23 +305,26 @@
     def s0(t,recv=False):
         return remote(wp.at[1-c,:,cs(t)], wr(t).at[(dp+1-2*c) if recv else dp,z], s0s.at[t], s0r.at[t], sib)
     def keep(t): return pltpu.make_async_copy(wp.at[c,:,cs(t)], wr(t).at[dp,z], l0.at[t])
+    across=set(range(n-across_first,n))
+    def group(t): return pl.ds(0,8) if t in across else pl.ds(2*q,2)
+    def span(t): return z if t in across else pl.ds(0,4)
     def s1a(t,recv=False):
-        r=wr(t).at[pl.ds(2*q,2), pe if recv else z]
+        r=wr(t).at[group(t), pe if recv else z]
         return remote(r,r,s1s.at[t,0],s1r.at[t,0],dpe)
     def s1b(t):
-        r=wr(t).at[pl.ds(2*q,2), z]
+        r=wr(t).at[group(t), z]
         return remote(r,r,s1s.at[t,1],s1r.at[t,1+zb],dmo)
     def s1bw(t,k):
-        r=wr(t).at[pl.ds(2*q,2), zo+k]
+        r=wr(t).at[group(t), zo+k]
         return remote(r,r,s1s.at[t,1],s1r.at[t,1+k],dmo)
     def s1c(t):
-        r=wr(t).at[pl.ds(2*q,2), pl.ds(zo,2)]
+        r=wr(t).at[group(t), pl.ds(zo,2)]
         return remote(r,r,s1s.at[t,2],s1r.at[t,3],dpe)
     def s2(t,a,recv=False):
-        r=wr(t).at[pl.ds(2*((qx,qy)[a] if recv else q),2)]
+        r=wr(t).at[pl.ds(2*((qx,qy)[a] if recv else q),2), span(t)]
         return remote(r,r,s2s.at[t,a],s2r.at[t,a],dxy[a])
     def s3(t,a,recv=False):
-        r=wr(t).at[2*(qd if recv else (qy,qx)[a])+a]
+        r=wr(t).at[2*(qd if recv else (qy,qx)[a])+a, span(t)]
         return remote(r,r,s3s.at[t,a],s3r.at[t,a],dxy[a])
     hp=hrow.shape[2]//h_parts
     def ht(p): return pl.ds(p*hp,hp)
@@ -335,27 +339,44 @@
         if k in done: return False
         done.add(k); return True
     def start1(t):
-        if t<n and once(1,t):
+        if t<n and t not in across and once(1,t):
             keep(t).wait(); s0(t,True).wait_recv()
             s1a(t).start(); s1b(t).start()
+    def across1(t):
+        keep(t).wait(); s0(t,True).wait_recv()
+        for a in range(2): s2(t,a).start()
+    def across2(t):
+        for a in range(2): s2(t,a,True).wait_recv()
+        for a in range(2): s3(t,a).start()
+    def across3(t):
+        for a in range(2): s3(t,a,True).wait_recv()
+        s1a(t).start(); s1b(t).start()
+    def across4(t):
+        @pl.when(inner)
+        def _():
+            s1bw(t,0).wait_recv(); s1bw(t,1).wait_recv(); s1c(t).start()
+    def across5(t):
+        s1a(t,True).wait_recv()
+        @pl.when(outer)
+        def _(): s1c(t).wait_recv()
     def forward(t):
-        if t<n and once(5,t):
+        if t<n and t not in across and once(5,t):
             @pl.when(inner)
             def _():
                 s1bw(t,0).wait_recv(); s1bw(t,1).wait_recv(); s1c(t).start()
     def start2(t):
         forward(t)
-        if t<n and once(2,t):
+        if t<n and t not in across and once(2,t):
             s1a(t,True).wait_recv()
             @pl.when(outer)
             def _(): s1c(t).wait_recv()
             for a in range(2): s2(t,a).start()
     def start3(t):
-        if 0<=t<n and once(3,t):
+        if 0<=t<n and t not in across and once(3,t):
             for a in range(2): s2(t,a,True).wait_recv()
             for a in range(2): s3(t,a).start()
     def finish(t):
-        if 0<=t<n and once(4,t):
+        if 0<=t<n and t not in across and once(4,t):
             for a in range(2): s3(t,a,True).wait_recv()
     def advance(t):
         for u in range(t+4): start1(u)
@@ -366,19 +387,29 @@
         @pl.when(inner)
         def _():
             hbw(p,0).wait_recv(); hbw(p,1).wait_recv(); hc(p).start()
+    for h in range(2):
+        for i,v in enumerate((w_q,w_k,w_v,w_o)): wp[h,:,384*i:384*i+384]=v[:,384*h:384*h+384]
+        wp[h,:,1536:1664]=gains[...]
+        for j in range(ff_steps):
+            for i,v in enumerate((w_g,w_u,w_d)):
+                a=1664+1536*j+512*i; f=512*(ff_steps*h+j); g=min(512,v.shape[1]-f)
+                if g>0: wp[h,:,a:a+g]=v[:,f:f+g]
+                if g<512: wp[h,:,a+max(g,0):a+512]=jnp.zeros((48,512-max(g,0)),low)
     keep_h=pltpu.make_async_copy(hid,hrow.at[c,z],ll.at[0]); keep_h.start()
     keep_c=pltpu.make_async_copy(cot,cotv.at[c],ll.at[1]); keep_c.start()
     keep_r=pltpu.make_async_copy(segr,sr.at[c],ll.at[2]); keep_r.start()
     keep_s=pltpu.make_async_copy(segc,sc.at[c],ll.at[3]); keep_s.start()
-    for t in range(3): s0(t).start(); keep(t).start()
+    for t in [*range(3),*sorted(across)]: s0(t).start(); keep(t).start()
     give_h=[remote(hid,hrow.at[c,z],xs.at[3],xr.at[3],sib)]; give_h[0].start()
     give_c=remote(cot,cotv.at[c],xs.at[0],xr.at[0],sib); give_c.start()
     give_r=remote(segr,sr.at[c],xs.at[1],xr.at[1],sib); give_r.start()
     give_s=remote(segc,sc.at[c],xs.at[2],xr.at[2],sib); give_s.start()
-    for t in range(3,n): s0(t).start(); keep(t).start()
+    for t in range(3,n-across_first): s0(t).start(); keep(t).start()
     start1(0); start1(1); start1(2); h_go(0)
+    for t in sorted(across): across1(t)
     forward(0); start2(0); forward(1); start2(1); forward(2)
     h_on(0); start1(3); h_go(1)
+    for t in sorted(across): across2(t)
     start3(0); start2(2)
     keep_h.wait(); keep_c.wait(); keep_r.wait(); keep_s.wait()
     remote(segr,sr.at[1-c],xs.at[1],xr.at[1],sib).wait_recv()
@@ -409,7 +440,7 @@
         lt[0,:,d]=v.T.astype(low)
         return 0
     lax.fori_loop(0,4,queries,0)
-    start2(4); start3(3); finish(2); forward(5); h_on(3)
+    start2(4); start3(3); finish(2); forward(5); h_on(3); start2(5); start3(4)
     for p in range(h_parts):
         ha(p,True).wait_recv()
         @pl.when(outer)
@@ -433,6 +464,7 @@
     advance(5)
     keys_of(1-c)
     advance(6)
+    for t in sorted(across)[:1]: across3(t)
     for h in range(6):
         pair=pl.ds(128*(h//2),128); odd=h%2
         bias[...]=pltpu.roll(jnp.broadcast_to(base[h:h+1,:],(256,1280)),1024,1,stride=1,stride_axis=0)
@@ -454,11 +486,15 @@
             return 0
         lax.fori_loop(0,4,attend,0)
         if h in (1,3): advance(7+h//2)
+        if h==3:
+            for t in sorted(across)[:1]: across4(t)
+            for t in sorted(across)[1:]: across3(t)
     def project(i,_):
         part[i//2,pl.ds(pl.multiple_of(lax.rem(i,2)*128,128),128),:]=dot_nt(mx[pl.ds(pl.multiple_of(i*128,128),128),:],wcol(1152,1536))
         return 0
     lax.fori_loop(0,4,project,0)
     give_p=remote(part,r1,xs.at[4],xr.at[4],sib); give_p.start()
+    advance(9)
     outs=[pltpu.make_async_copy(a,b,lo.at[i]) for i,(a,b) in enumerate(((qq,q_o),(kk,kk_o),(vv,vv_o),(mx,mx_o),(lse,lse_o),(sr,segr_o),(sc,segc_o),(cotv,cot_o)))]
     for o in outs: o.start()
     give_p.wait_recv()
@@ -476,11 +512,14 @@
     give_lt=pltpu.make_async_copy(lt,lt_o,ll.at[5]); give_lt.start()
     give_mid=pltpu.make_async_copy(mid,mid_o,ll.at[12]); give_mid.start()
     gs_o[...]=gs[...]
-    advance(9)
+    advance(10)
+    for t in sorted(across)[1:]: across4(t)
     hout=[]
     for j in range(ff_steps):
         if j:
-            for t in range(4+3*j,7+3*j): advance(t)
+            for t in range(4+3*j,7+3*j) if j==ff_steps-1 else [10+j]: advance(t)
+            if j==ff_steps-1:
+                for t in sorted(across): across5(t)
         loads=[pltpu.make_async_copy(w.at[3*j+i],wf.at[i],ll.at[6+i]) for i in range(3)]
         for l in loads: l.start()
         b=j%2
@@ -522,7 +561,7 @@
         def _(): s1c(t).wait_send()
         for a in range(2): s2(t,a).wait_send(); s3(t,a).wait_send()
 
-def forward_call(wp, hid, cot, segr, segc, base, ff_steps, cid=0):
+def forward_call(weights, gains, hid, cot, segr, segc, base, ff_steps, cid=0):
     n=2+3*ff_steps
     S=jax.ShapeDtypeStruct; V=pltpu.VMEM; D=pltpu.SemaphoreType.DMA
     fw=512*ff_steps
@@ -533,11 +572,11 @@
     scratch=[V((2,4,256,1536),low),V((2,256,1536),low),V((2,8,1024),f32),V((2,256,128),f32),V((8,4,48,1664),low),V((3,8,4,48,512),low),
              V((512,384),low),V((2,1024,384),low),V((2,1024,384),low),V((512,384),low),V((2,256,128),f32),V((256,1280),f32),
              V((2,256,1536),f32),V((2,256,1536),f32),V((512,1536),low),V((2,3,512,512),low),V((2,256,1536),f32),V((3,1536,512),low),V((8,1536),f32),
-             V((2,256,1536),f32),
+             V((2,256,1536),f32),V((2,48,1664+1536*ff_steps),low),
              D((n,)),D((n,)),D((n,)),D((n,3)),D((n,4)),D((n,2)),D((n,2)),D((n,2)),D((n,2)),D((h_parts,3)),D((h_parts,4)),D((10,)),D((10,)),D((13,)),D((10,))]
     return pl.pallas_call(functools.partial(forward_kernel,ff_steps),out_shape=outs,
-        in_specs=[vm]+[hbm]*4+[vm],out_specs=tuple(ospec),scratch_shapes=scratch,
-        compiler_params=pltpu.CompilerParams(collective_id=cid,has_side_effects=True,vmem_limit_bytes=62*2**20))(wp,hid,cot,segr,segc,base)
+        in_specs=[vm]*8+[hbm]*4+[vm],out_specs=tuple(ospec),scratch_shapes=scratch,
+        compiler_params=pltpu.CompilerParams(collective_id=cid,has_side_effects=True,vmem_limit_bytes=62*2**20))(*weights,gains,hid,cot,segr,segc,base)
 
 def dot_tn(a,b):
     return lax.dot_general(a,b,(((0,),(0,)),((),())),preferred_element_type=jnp.float32)
@@ -545,8 +584,8 @@
 part_slots=2
 sum_slots=3
 lag=6
-def backward_kernel(chunks, ff_steps, w1, w2, lt_h, hdg, q_h, kk_h, vv_h, mx_h, lse_h, gnf_h, yy_h, mid_h, cot_h, segr_h, segc_h, hid_h, base, gains, spots, tile,
-                    out, gin_o, bo_o, xg, xy, *rest):
+def backward_kernel(chunks, ff_steps, w1, w2, lt_h, hdg, q_h, kk_h, vv_h, mx_h, lse_h, gnf_h, yy_h, mid_h, cot_h, segr_h, segc_h, hid_h, base, gains,
+                    og, ou, od, oo, oq, ok, ov, oe, gin_o, bo_o, xg, xy, *rest):
     n=len(chunks)
     ra1=rest[0:n]; rb1=rest[n:2*n]; ra2=rest[2*n:3*n]; rb2=rest[3*n:4*n]; rz=rest[4*n:5*n]
     (fin,p,lt,gat,rbuf,wa,qq,kk,vv,mx,gm,lse,sr,sc,bias,dbias,dq,acc,dkv,rka,rkb,rkc,dk,dv,part,r3,hid,dtab,ext,cb,
@@ -584,7 +623,7 @@
         if k in done: return False
         done.add(k); return True
     def stage1(t):
-        left,off,wd,src=chunks[t]; b=t%part_slots
+        left,off,wd,src=chunks[t][:4]; b=t%part_slots
         if t>=part_slots:
             for d in c1[t-part_slots]: d.wait_send()
         if src[0]=="feed":
@@ -633,20 +672,40 @@
             cs.append(remote(rb2[t].at[zs[k]],rz[t].at[k,1],s3.at[t,k,1],v3.at[t,k,1],dz[k]))
         for d in cs: d.start()
         c3[t]=cs
+    def place(t,pair,acts,half):
+        o,offset,width,total=chunks[t][4]
+        o=(og,ou,od,oo,oq,ok,ov,oe)[o]
+        last=total-(width[1]+offset)
+        def act(size):
+            cols=pl.ds(pl.multiple_of(half*width[1]+offset,128),size)
+            for m,how in zip(pair(None,size,cols,o),acts):
+                if how: getattr(m,how)()
+        if last>=width[0]: act(width[0])
+        else:
+            @pl.when(half==0)
+            def _(): act(width[0])
+            if last>0:
+                @pl.when(half==1)
+                def _(): act(last)
+    def drain(t):
+        place(t,lambda _,width,cols,o: (
+            remote(fin.at[0,0,:,pl.ds(0,width)],o.at[:,cols],s4.at[t],v4.at[t],sib),
+            pltpu.make_async_copy(fin.at[0,0,:,pl.ds(0,width)],o.at[:,cols],lo.at[t])),("wait_send","wait"),c)
+    def arrive(t):
+        place(t,lambda _,width,cols,o: (remote(fin.at[0,0,:,pl.ds(0,width)],o.at[:,cols],s4.at[t],v4.at[t],sib),),("wait_recv",),1-c)
     def stage4(t):
-        off,wd=chunks[t][1:3]
+        wd=chunks[t][2]
         for d in c3[t]: d.wait_recv()
         f0=ra2[t][z].astype(f32); f1=rb2[t][z].astype(f32)
         for k in range(3):
             f0=f0+rz[t][k,0].astype(f32); f1=f1+rz[t][k,1].astype(f32)
         b=t%sum_slots
         if t>=sum_slots:
-            c4[t-sum_slots][0].wait_send(); c4[t-sum_slots][1].wait()
+            drain(t-sum_slots)
         fin[b,0,:,0:wd]=f0; fin[b,1,:,0:wd]=f1
-        cols=pl.ds(off,wd)
-        a=remote(fin.at[b,1-c,:,pl.ds(0,wd)],out.at[c,:,cols],s4.at[t],v4.at[t],sib)
-        e=pltpu.make_async_copy(fin.at[b,c,:,pl.ds(0,wd)],out.at[c,:,cols],lo.at[t])
-        a.start(); e.start(); c4[t]=(a,e)
+        place(t,lambda _,width,cols,o: (
+            remote(fin.at[b,1-c,:,pl.ds(0,width)],o.at[:,cols],s4.at[t],v4.at[t],sib),
+            pltpu.make_async_copy(fin.at[b,c,:,pl.ds(0,width)],o.at[:,cols],lo.at[t])),("start","start"),c)
     def step(s):
         for f,t in ((stage2,s),(stage1,s+2),(stage3,s-1),(stage4,s-lag)):
             if 0<=t<n and once(f.__name__,t): f(t)
@@ -729,10 +788,13 @@
             if pp: relay(pp-1)
     tab=dtab[...]
     high=tab.astype(low); rest1=tab-high.astype(f32); mid1=rest1.astype(low); last=(rest1-mid1.astype(f32)).astype(low)
-    found=dot(high,spots[...])+dot(mid1,spots[...])+dot(last,spots[...])
+    shift=lax.broadcasted_iota(jnp.int32,(1280,128),0)-256-256*z
+    spots=jnp.where(bucket_table(shift)==lanes((1280,128)),1.0,0.0).astype(low)
+    tile=jnp.where(lax.rem(lanes((128,1536)),48)==lax.broadcasted_iota(jnp.int32,(128,1536),0),1.0,0.0).astype(low)
+    found=dot(high,spots)+dot(mid1,spots)+dot(last,spots)
     upper=found.astype(low)
-    ext[0:8,:]=dot(upper,tile[...])
-    ext[8:16,:]=dot((found-upper.astype(f32)).astype(low),tile[...])
+    ext[0:8,:]=dot(upper,tile)
+    ext[8:16,:]=dot((found-upper.astype(f32)).astype(low),tile)
     give_y.wait_recv()
     for i in range(2):
         a=pl.ds(128*i,128)
@@ -777,10 +839,8 @@
     while at<n+lag:
         step(at); at+=1
     for t in range(n):
-        off,wd=chunks[t][1:3]; cols=pl.ds(off,wd)
-        remote(fin.at[t%sum_slots,1-c,:,pl.ds(0,wd)],out.at[1-c,:,cols],s4.at[t],v4.at[t],sib).wait_recv()
-        if t>=n-sum_slots:
-            c4[t][0].wait_send(); c4[t][1].wait()
+        arrive(t)
+        if t>=n-sum_slots: drain(t)
         if t>=n-part_slots:
             for d in c1[t]: d.wait_send()
         for d in c2[t]: d.wait_send()
@@ -793,18 +853,18 @@
         def _(): kb(pp,0).wait_send(); kb(pp,1).wait_send()
     give_i.wait(); give_g.wait_send(); give_y.wait_send()
 
-def backward_chunks(ff_steps):
+def backward_chunks(ff_steps,ff):
     fw=512*ff_steps
     chunks=[]
     for j in range(ff_steps):
-        chunks+=[(0,512*j,512,("feed",1,j)),(0,fw+512*j,512,("feed",2,j)),(1,2*fw+512*j,512,("feed",0,j))]
-    o=3*fw
-    chunks+=[(3,o,384,("ref",0,0)),(1,o+384,384,("ref",1,0)),(1,o+768,384,("ref",2,0)),(1,o+1152,384,("ref",3,0)),(1,o+1536,128,("ref",4,0))]
+        for left,i,o in ((0,1,0),(0,2,1),(1,0,2)):
+            chunks.append((left,0,512,("feed",i,j),(o,512*j,(512,fw),ff)))
+    for k in range(4): chunks.append((3 if k==0 else 1,0,384,("ref",k,0),(3+k,0,(384,384),768)))
+    chunks.append((1,0,128,("ref",4,0),(7,0,(128,128),256)))
     return chunks
 
-def backward_call(w1,w2,lt,hdg,q,kk,vv,mx,lse,gnf,yy,mid,cot,segr,segc,hid,base,gains,spots,tile,ff_steps,cid=1):
-    chunks=backward_chunks(ff_steps); n=len(chunks)
-    C=3*512*ff_steps+1664
+def backward_call(w1,w2,lt,hdg,q,kk,vv,mx,lse,gnf,yy,mid,cot,segr,segc,hid,base,gains,ff_steps,ff,cid=1):
+    chunks=backward_chunks(ff_steps,ff); n=len(chunks)
     S=jax.ShapeDtypeStruct; V=pltpu.VMEM; D=pltpu.SemaphoreType.DMA
     hbm=pl.BlockSpec(memory_space=pltpu.HBM); vm=pl.BlockSpec(memory_space=pltpu.VMEM)
     ws=[k[2] for k in chunks]
@@ -814,9 +874,9 @@
       V((256,1280),f32),V((256,1280),f32),V((512,384),low),V((2,2,1024,128),f32),V((3,4,2,2,256,128),low),V((3,2,2,256,128),low),V((3,2,2,256,128),low),V((3,2,2,2,256,128),low),V((512,384),low),V((512,384),low),
       V((2,256,1536),f32),V((256,1536),f32),V((256,1536),low),V((8,1280),f32),V((128,1536),f32),V((128,1536),low)]
     scratch+=[D((16,)),D((n,)),D((n,)),D((n,2)),D((n,2)),D((n,2)),D((n,2)),D((n,3,2)),D((n,3,2)),D((n,)),D((n,)),D((3,4)),D((3,3)),D((3,)),D((3,)),D((5,))]
-    return pl.pallas_call(functools.partial(backward_kernel,chunks,ff_steps),out_shape=(S((2,48,C),f32),S((256,1536),f32),S((256,1536),f32),S((2,256,1536),f32),S((256,1536),f32)),
-        in_specs=[hbm]*16+[vm]*4,out_specs=(hbm,)*5,scratch_shapes=scratch,
-        compiler_params=pltpu.CompilerParams(collective_id=cid,has_side_effects=True,vmem_limit_bytes=62*2**20))(w1,w2,lt,hdg,q,kk,vv,mx,lse,gnf,yy,mid,cot,segr,segc,hid,base,gains,spots,tile)
+    return pl.pallas_call(functools.partial(backward_kernel,chunks,ff_steps),out_shape=(S((48,ff),f32),)*3+(S((48,768),f32),)*4+(S((48,256),f32),S((256,1536),f32),S((256,1536),f32),S((2,256,1536),f32),S((256,1536),f32)),
+        in_specs=[hbm]*16+[vm]*2,out_specs=(hbm,)*12,scratch_shapes=scratch,
+        compiler_params=pltpu.CompilerParams(collective_id=cid,has_side_effects=True,vmem_limit_bytes=62*2**20))(w1,w2,lt,hdg,q,kk,vv,mx,lse,gnf,yy,mid,cot,segr,segc,hid,base,gains)
 
 def cut(v,h,w):
     n=v.shape[1]
@@ -850,25 +910,18 @@
     b=jnp.einsum("ub,bh->hu",oh,mine,precision=lax.Precision.HIGHEST)
     return jnp.pad(b,((0,2),(0,0))), oh
 
-def joined(o,start,width,total):
-    return jnp.concatenate([o[0,:,start:start+width],o[1,:,start:start+width]],axis=1)[:,:total]
 def kernel_local(hid,seg,ga,wq,wk,wv,wo,tab,gf,wg,wu,wd,cot):
-    steps=4; fw=512*steps; ff=wg.shape[1]
-    wp=pack(wq,wk,wv,wo,ga,gf,wg,wu,wd,steps)
-    r,s=seg_ids(seg); b,oh=base_of(tab)
-    w1,w2,w,lt,hdg,q,kk,vv,mx,lse,gnf,yy,gains,segr,segc,mid,cot2=forward_call(wp,hid[0],cot[0],r,s,b,steps)
-    spots=jnp.pad(oh,((0,0),(0,96))).astype(jnp.bfloat16)
-    tile=(jnp.arange(1536)[None,:]%48==jnp.arange(128)[:,None]).astype(jnp.bfloat16)
-    o,gin,bo,_,_=backward_call(w1,w2,lt,hdg,q,kk,vv,mx,lse,gnf,yy,mid,cot2,segr,segc,hid[0],b,gains,spots,tile,steps)
-    e=3*fw+1536
-    i=3*fw
-    ext=o[:,:,e:]
-    t=ext[:,:32,0:8]+ext[:,:32,8:16]
-    table=jnp.concatenate([t[0,:,:6],t[1,:,:6]],axis=1)
-    g=ext[0]+ext[1]
+    ff=wg.shape[1]; steps=-(-ff//1024)
+    gain_cols=jnp.pad(jnp.stack([ga,gf],axis=1),((0,0),(0,126)))
+    r,s=seg_ids(seg); b=base_of(tab)[0]
+    w1,w2,w,lt,hdg,q,kk,vv,mx,lse,gnf,yy,gains,segr,segc,mid,cot2=forward_call((wq,wk,wv,wo.T,wg,wu,wd.T),gain_cols,hid[0],cot[0],r,s,b,steps)
+    og,ou,od,oo,oq,ok,ov,oe,gin,bo,_,_=backward_call(w1,w2,lt,hdg,q,kk,vv,mx,lse,gnf,yy,mid,cot2,segr,segc,hid[0],b,gains,steps,ff)
+    e=oe.reshape(48,2,128)
+    t=e[:32,:,0:8]+e[:32,:,8:16]
+    table=t[:,:,:6].reshape(32,12)
+    g=e[:,0]+e[:,1]
     gg=lambda a: g[:,a]+g[:,a+8]
-    return (bo[None],gin[None],gg(16),joined(o,i+384,384,768),joined(o,i+768,384,768),joined(o,i+1152,384,768),joined(o,i,384,768).T,table,gg(32),
-            joined(o,0,fw,ff),joined(o,fw,fw,ff),joined(o,2*fw,fw,ff).T)
+    return (bo[None],gin[None],gg(16),oq,ok,ov,oo.T,table,gg(32),og,ou,od.T)
 
 
 def solution(mesh):

time: 529 us -> 481 us (0.909)
  Pallas kernels: 482 us -> 453 us
  local copies, waits for them, and re-layouts: 24.7 us -> 13.5 us
  other arithmetic: 9.93 us -> 3.31 us
    pallas_call x1, Pallas kernels: 258 us -> 234 us  [forward_call(): pl.pallas_call(functools.partial(forward_kernel, ff_steps), out_shape=out...]
    unnamed x32 -> x25, local copies, waits for them, and re-layouts: 17.7 us -> 9.09 us
    pallas_call x1, Pallas kernels: 225 us -> 219 us  [backward_call(): pl.pallas_call(functools.partial(backward_kernel, chunks, ff_steps), out_...]
where the time goes in v5:
time: 481 us; the launch traced here: 471 us
  Pallas kernels  453 us (94%)
  local copies, waits for them, and re-layouts  13.5 us (3%)
    pallas_call x1, Pallas kernels, forward_call(): pl.pallas_call(functools.partial(forward_kernel, ff_steps), out_shape=out...  234 us
    pallas_call x1, Pallas kernels, backward_call(): pl.pallas_call(functools.partial(backward_kernel, chunks, ff_steps), out_...  219 us

profile of v5, /device:TPU:0, one launch (start us, length us, event | category | flops | bytes accessed | tf_op | source)
XLA Modules:
  0.0 471.3 jit_solution(13815355399300377656)
XLA Ops:
  0.7 0.7 pad_maximum_fusion
  1.3 0.7 fusion.13
  2.0 0.1 dynamic_slice.3
  2.1 0.7 fusion.14
  2.8 0.7 convert_element_type.65
  3.5 0.1 copy.36
  3.6 0.6 pad.8.gains
  4.2 0.5 fusion
  4.7 0.6 pad.9.base
  5.4 0.6 broadcast_in_dim.29.segr
  6.0 0.8 broadcast_in_dim.30.segc
  6.8 234.3 %shard_map.220 = (bf16[8,4,48,768]{3,2,1,0:T(8,128)(2,1)}, bf16[8,4,48,896]{3,2,1,0:T(8,128)(2,1)}, bf16[12,8,4,48,512]{4,3,2,1,0:T(8,128)(2,1)}, bf16[3,1536,51...) custom-call(bf16[48,768]{1,0:T(8,128)(2,1)} %w_q.1, ...), custom_call_target="tpu_custom_call" | custom-call | tf_op jit(solution)/shard_map/pallas_call | solution.py:577
  241.1 218.5 %shard_map.221 = (f32[48,3968]{1,0:T(8,128)}, f32[48,3968]{1,0:T(8,128)}, f32[48,3968]{1,0:T(8,128)}, f32[48,768]{1,0:T(8,128)}, f32[48,768]{1,0:T(8,128)}, /*in...) custom-call(bf16[8,4,48,768]{3,2,1,0:T(8,128)(2,1)} %get-tuple-eleme, ...), custom_call_target="tpu_custom_call" | custom-call | tf_op jit(solution)/shard_map/pallas_call | solution.py:877
  459.6 0.0 copy-start
  459.6 1.0 copy.41
  460.6 0.5 fusion.17
  461.2 0.6 reshape.74
  461.8 2.7 copy.51
  464.4 0.0 copy-done
  464.4 0.0 copy-start.7
  464.4 0.0 copy-start.6
  464.4 0.0 copy-start.5
  464.4 0.0 copy-start.4
  464.4 0.0 copy-start.3
  464.5 0.0 copy-start.2
  464.5 1.1 copy.52
  465.6 0.0 copy-done.7
  465.6 0.0 copy-start.1
  465.6 0.7 copy.53
  466.3 0.0 copy-done.6
  466.3 0.7 copy.54
  466.9 0.0 copy-done.5
  466.9 0.7 copy.55
  467.6 0.0 copy-done.4
  467.6 0.7 copy.56
  468.3 0.0 copy-done.3
  468.3 0.9 copy.57
  469.1 0.0 copy-done.2
  469.1 0.9 copy.58
  470.0 0.0 copy-done.1
  470.0 0.9 copy.59
  (4 shorter events, 0.0 us)
Async XLA Ops:
  459.6 4.8 %copy-start = (f32[256,1536]{1,0:T(8,128)S(1)}, f32[256,1536]{1,0:T(8,128)}, u32[]{:S(2)}) copy-start(f32[256,1536]{1,0:T(8,128)} %get-tuple-element.55) | copy-start | bytes 4718596
  464.4 1.2 copy-start.7
  464.4 1.9 copy-start.6
  464.4 2.5 copy-start.5
  464.4 3.2 copy-start.4
  464.4 3.8 copy-start.3
  464.5 4.7 copy-start.2
  465.6 4.4 copy-start.1
